TPU v7x, 32 devices: a whole 2x2x4 slice. The times are simulated.
32 devices in a mesh: dp: 4 (over x, core), seq: 8 (over z, y).
Axes of the slice: x: 2, y: 2, z: 4, core: 2. Of those that a mesh axis runs over, the one named last changes fastest.
Arguments:
- tokens: bfloat16 [32768, 1152], P(('dp', 'seq')), may hold values from -6 to 6
- condition: bfloat16 [128, 1152], P('dp'), may hold values from -6 to 6
- lengths: int32 [128], P(('dp', 'seq')), may hold values from 1 to 256, 22937 in all
- kept_index: int32 [128, 256], P(('dp', 'seq')), may hold values from 0 to 255, each once within a row
- heads_weight: bfloat16 [1152, 3456], P('seq'), may hold values from -0.1875 to 0.1875
- heads_bias: bfloat16 [2304], replicated, may hold values from -1.5 to 1.5
- merge_weight: bfloat16 [1152, 1152], P('seq'), may hold values from -1.5 to 1.5
- merge_bias: bfloat16 [1152], replicated, may hold values from -4 to 4
- up_weight: bfloat16 [1152, 4608], P('seq'), may hold values from -0.1875 to 0.1875
- up_bias: bfloat16 [4608], replicated, may hold values from -4 to 4
- down_weight: bfloat16 [1152, 4608], P('seq'), may hold values from -0.1875 to 0.1875
- down_bias: bfloat16 [1152], replicated, may hold values from -4 to 4
- modulate_weight: bfloat16 [1152, 6912], P('seq'), may hold values from -0.1875 to 0.1875
- modulate_bias: bfloat16 [6912], replicated, may hold values from -4 to 4
- relative_table: bfloat16 [16, 961], replicated, may hold values from -6 to 6
- cotangent: bfloat16 [32768, 1152], P(('dp', 'seq')), may hold values from -6 to 6
Outputs:
- output: bfloat16 [32768, 1152], P(('dp', 'seq'))
- tokens_grad: float32 [32768, 1152], P(('dp', 'seq'))
- heads_weight_grad: float32 [1152, 3456], P('seq')
- merge_weight_grad: float32 [1152, 1152], P('seq')
- up_weight_grad: float32 [1152, 4608], P('seq')
- down_weight_grad: float32 [1152, 4608], P('seq')
- modulate_weight_grad: float32 [1152, 6912], P('seq')
- heads_bias_grad: float32 [2304], replicated
- merge_bias_grad: float32 [1152], replicated
- up_bias_grad: float32 [4608], replicated
- down_bias_grad: float32 [1152], replicated
- modulate_bias_grad: float32 [6912], replicated
- relative_table_grad: float32 [16, 961], replicated
Inputs may be any that keep to these rules, and one draw needn't show every extreme that they name: The first lengths[s] slots of sample s hold its kept tokens, the rest are empty. Each sample's row is a permutation of the 256 patch positions; slot r's patch lies at row kept_index // 16, column kept_index % 16.
All inputs are finite; a program needn't handle non-finite values. No bound on the sum of `lengths` on one device may be relied on, other than what follows from the above.
Results may differ from a plain program's by a relative error of at most 0.019.
Values may be sent and summed in bfloat16 or wider, within the bound.
No kernel may reach another device: no remote copies, remote signals or barrier semaphores. Data moves between devices by JAX's collectives and lax.ppermute only.
A program may use at most 320 MiB of HBM per device.

v0:
```python
from functools import partial
import math

import jax
import jax.numpy as jnp
from jax import lax
from jax.sharding import PartitionSpec as P

D = 1152
HEADS = 16
HEAD = 72
FF = 4608
SIDE = 16
MICRO = 2
SAMP_DEV = 4
GRID = 256


epsilon = 1e-06


def layer_norm(values):
    center = values - jnp.mean(values, axis=-1, keepdims=True)
    spread = jnp.mean(center * center, axis=-1, keepdims=True)
    return center * lax.rsqrt(spread + epsilon)


def modulated(values, scales, shifts):
    return layer_norm(values) * (1.0 + scales) + shifts


def gelu_tanh(values):
    return jax.nn.gelu(values, approximate=True)


def fold_rows(left, portion):
    return jnp.dot(left, portion, preferred_element_type=jnp.float32)


def right_transposed(left, portion):
    return lax.dot_general(
        left, portion, (((1,), (1,)), ((), ())), preferred_element_type=jnp.float32
    )


def column_outer(left, right):
    return lax.dot_general(
        left, right, (((0,), (0,)), ((), ())), preferred_element_type=jnp.float32
    )


def relative_index(positions):
    row_place = positions // SIDE
    col_place = positions % SIDE
    row_gap = row_place[..., :, None] - row_place[..., None, :] + (SIDE - 1)
    col_gap = col_place[..., :, None] - col_place[..., None, :] + (SIDE - 1)
    return row_gap * (2 * SIDE - 1) + col_gap


def slot_onehot(index_pair):
    return (index_pair[..., :, None] == jnp.arange(GRID)[None, None, :]).astype(jnp.bfloat16)


def pair_scores(packed, lens_pair, index_pair, position_bias):
    parts = packed.reshape(2, GRID, 3, HEADS, HEAD)
    queries = parts[:, :, 0]
    key_part = parts[:, :, 1]
    value_part = parts[:, :, 2]
    scaling = 1.0 / math.sqrt(HEAD)
    onehot = slot_onehot(index_pair)
    rows_placed = jnp.einsum(
        "srp,hpq->hsrq", onehot, position_bias, preferred_element_type=jnp.float32
    ).astype(jnp.bfloat16)
    bias_pair = jnp.einsum(
        "hsrq,skq->hsrk", rows_placed, onehot, preferred_element_type=jnp.float32
    )
    scores = (
        jnp.einsum("sqhe,skhe->hsqk", queries, key_part, preferred_element_type=jnp.float32)
        * scaling
    )
    scores = scores + bias_pair
    living = jnp.arange(GRID)[None, :] < lens_pair[:, None]
    scores = jnp.where(living[None, :, None, :], scores, -1e30)
    return (scores, queries, key_part, value_part, onehot)


def attend_pair(arguments, position_bias):
    packed, lens_pair, index_pair = arguments
    scores, queries, key_part, value_part, onehot = pair_scores(
        packed, lens_pair, index_pair, position_bias
    )
    peak = jnp.max(scores, axis=-1, keepdims=True)
    expo = jnp.exp(scores - peak)
    mass = jnp.sum(expo, axis=-1, keepdims=True)
    probs_low = (expo / mass).astype(jnp.bfloat16)
    mixed = jnp.einsum("hsqk,skhe->sqhe", probs_low, value_part, preferred_element_type=jnp.float32)
    return (mixed.astype(jnp.bfloat16).reshape(2 * GRID, D), (peak + jnp.log(mass))[..., 0])


def attend_pair_back(arguments, position_bias):
    packed, lens_pair, index_pair, logsum, grad_mixed = arguments
    scores, queries, key_part, value_part, onehot = pair_scores(
        packed, lens_pair, index_pair, position_bias
    )
    probs = jnp.exp(scores - logsum[..., None])
    grad_mixed = grad_mixed.reshape(2, GRID, HEADS, HEAD)
    grad_probs = jnp.einsum(
        "sqhe,skhe->hsqk", grad_mixed, value_part, preferred_element_type=jnp.float32
    )
    inner = jnp.sum(probs * grad_probs, axis=-1, keepdims=True)
    grad_scores = (probs * (grad_probs - inner)).astype(jnp.bfloat16)
    scaling = 1.0 / math.sqrt(HEAD)
    grad_query = (
        jnp.einsum("hsqk,skhe->sqhe", grad_scores, key_part, preferred_element_type=jnp.float32)
        * scaling
    )
    grad_key = (
        jnp.einsum("hsqk,sqhe->skhe", grad_scores, queries, preferred_element_type=jnp.float32)
        * scaling
    )
    grad_value = jnp.einsum(
        "hsqk,sqhe->skhe",
        probs.astype(jnp.bfloat16),
        grad_mixed,
        preferred_element_type=jnp.float32,
    )
    stacked = (
        jnp.stack([grad_query, grad_key, grad_value], axis=2)
        .astype(jnp.bfloat16)
        .reshape(2 * GRID, 3 * D)
    )
    rows_back = jnp.einsum(
        "hsrk,srp->hspk", grad_scores, onehot, preferred_element_type=jnp.float32
    ).astype(jnp.bfloat16)
    placed_grad = jnp.einsum("hspk,skq->hpq", rows_back, onehot, preferred_element_type=jnp.float32)
    return (stacked, placed_grad)


def offsets_table(placed_grad):
    spots = jnp.arange(SIDE)
    reach = jnp.arange(2 * SIDE - 1)
    gaps = (
        spots[:, None, None] - spots[None, :, None] + (SIDE - 1) == reach[None, None, :]
    ).astype(jnp.float32)
    grid_grad = placed_grad.reshape(HEADS, SIDE, SIDE, SIDE, SIDE)
    by_rows = jnp.einsum("hwxyz,wya->haxz", grid_grad, gaps, precision=lax.Precision.HIGHEST)
    return jnp.einsum("haxz,xzb->hab", by_rows, gaps, precision=lax.Precision.HIGHEST).reshape(
        HEADS, (2 * SIDE - 1) ** 2
    )


def local(
    tokens,
    condition,
    lengths,
    kept_index,
    heads_weight,
    heads_bias,
    merge_weight,
    merge_bias,
    up_weight,
    up_bias,
    down_weight,
    down_bias,
    modulate_weight,
    modulate_bias,
    relative_table,
    cotangent,
):
    position = lax.axis_index("seq")
    position_bias = jnp.take(relative_table, relative_index(jnp.arange(GRID)), axis=1)
    own_cond = lax.dynamic_slice_in_dim(condition, position * SAMP_DEV, SAMP_DEV, 0)
    own_silu = jax.nn.silu(own_cond.astype(jnp.float32)).astype(jnp.bfloat16)
    modulation = fold_rows(own_silu, lax.all_gather(modulate_weight, "seq", axis=0, tiled=True))
    modulation = (modulation + modulate_bias.astype(jnp.float32)).reshape(SAMP_DEV, 1, 6, D)
    full_bias = jnp.concatenate(
        [heads_bias[:D], jnp.zeros((D,), jnp.bfloat16), heads_bias[D:]]
    ).astype(jnp.float32)
    parts_count = MICRO
    samples = SAMP_DEV // parts_count
    rows = samples * GRID
    pairs = samples // 2
    kept = {
        "out": [],
        "tgrad": [],
        "mgrad": [],
        "hone": [],
        "gpack": [],
        "attn": [],
        "gbranch": [],
        "htwo": [],
        "gup": [],
        "gmlp": [],
        "act": [],
    }
    placed_total = jnp.zeros((HEADS, GRID, GRID), jnp.float32)
    for part in range(parts_count):
        slab = tokens[part * rows : (part + 1) * rows].astype(jnp.float32).reshape(samples, GRID, D)
        mods = modulation[part * samples : (part + 1) * samples]
        shift_one, scale_one, gate_one, shift_two, scale_two, gate_two = [
            mods[:, :, index] for index in range(6)
        ]
        lens_part = lengths[part * samples : (part + 1) * samples]
        index_part = kept_index[part * samples : (part + 1) * samples]
        living = (jnp.arange(GRID)[None, :] < lens_part[:, None])[:, :, None]
        hidden_one = modulated(slab, scale_one, shift_one).astype(jnp.bfloat16).reshape(rows, D)
        packed = (
            fold_rows(hidden_one, lax.all_gather(heads_weight, "seq", axis=0, tiled=True))
            + full_bias
        ).astype(jnp.bfloat16)
        packed_pairs = packed.reshape(pairs, 2 * GRID, 3 * D)
        lens_pairs = lens_part.reshape(pairs, 2)
        index_pairs = index_part.reshape(pairs, 2, GRID)
        attended, logsum = lax.map(
            partial(attend_pair, position_bias=position_bias),
            (packed_pairs, lens_pairs, index_pairs),
        )
        attended = attended.reshape(rows, D)
        branch = fold_rows(
            attended, lax.all_gather(merge_weight, "seq", axis=0, tiled=True)
        ) + merge_bias.astype(jnp.float32)
        branch = branch.reshape(samples, GRID, D)
        middle = slab + gate_one * branch
        hidden_two = modulated(middle, scale_two, shift_two).astype(jnp.bfloat16).reshape(rows, D)
        up_value = fold_rows(
            hidden_two, lax.all_gather(up_weight, "seq", axis=0, tiled=True)
        ) + up_bias.astype(jnp.float32)
        activated = gelu_tanh(up_value).astype(jnp.bfloat16)
        mlp_out = right_transposed(
            activated, lax.all_gather(down_weight, "seq", axis=0, tiled=True)
        )
        mlp_out = (mlp_out + down_bias.astype(jnp.float32)).reshape(samples, GRID, D)
        final = jnp.where(living, middle + gate_two * mlp_out, 0.0)
        kept["out"].append(final.astype(jnp.bfloat16).reshape(rows, D))
        grad_final = jnp.where(
            living,
            cotangent[part * rows : (part + 1) * rows]
            .astype(jnp.float32)
            .reshape(samples, GRID, D),
            0.0,
        )
        gate_two_grad = jnp.sum(grad_final * mlp_out, axis=1, keepdims=True)
        grad_mlp = (gate_two * grad_final).astype(jnp.bfloat16).reshape(rows, D)
        grad_act = fold_rows(grad_mlp, lax.all_gather(down_weight, "seq", axis=0, tiled=True))
        grad_up = jax.vjp(gelu_tanh, up_value)[1](grad_act)[0].astype(jnp.bfloat16)
        grad_hidden_two = right_transposed(
            grad_up, lax.all_gather(up_weight, "seq", axis=0, tiled=True)
        )
        middle_ln, scale_two_grad, shift_two_grad = jax.vjp(
            modulated, middle, scale_two, shift_two
        )[1](grad_hidden_two.reshape(samples, GRID, D))
        grad_middle = grad_final + middle_ln
        gate_one_grad = jnp.sum(grad_middle * branch, axis=1, keepdims=True)
        grad_branch = (gate_one * grad_middle).astype(jnp.bfloat16).reshape(rows, D)
        grad_attended = right_transposed(
            grad_branch, lax.all_gather(merge_weight, "seq", axis=0, tiled=True)
        ).astype(jnp.bfloat16)
        grad_packed, placed_parts = lax.map(
            partial(attend_pair_back, position_bias=position_bias),
            (
                packed_pairs,
                lens_pairs,
                index_pairs,
                logsum,
                grad_attended.reshape(pairs, 2 * GRID, D),
            ),
        )
        grad_packed = grad_packed.reshape(rows, 3 * D)
        placed_total = placed_total + jnp.sum(placed_parts, axis=0)
        grad_hidden_one = right_transposed(
            grad_packed, lax.all_gather(heads_weight, "seq", axis=0, tiled=True)
        )
        slab_ln, scale_one_grad, shift_one_grad = jax.vjp(modulated, slab, scale_one, shift_one)[1](
            grad_hidden_one.reshape(samples, GRID, D)
        )
        kept["tgrad"].append((grad_middle + slab_ln).reshape(rows, D))
        kept["mgrad"].append(
            jnp.concatenate(
                [
                    shift_one_grad,
                    scale_one_grad,
                    gate_one_grad,
                    shift_two_grad,
                    scale_two_grad,
                    gate_two_grad,
                ],
                axis=-1,
            ).reshape(samples, 6 * D)
        )
        kept["hone"].append(hidden_one)
        kept["gpack"].append(grad_packed)
        kept["attn"].append(attended)
        kept["gbranch"].append(grad_branch)
        kept["htwo"].append(hidden_two)
        kept["gup"].append(grad_up)
        kept["gmlp"].append(grad_mlp)
        kept["act"].append(activated)
    table_grad = offsets_table(placed_total)
    joined = {name: jnp.concatenate(items, axis=0) for name, items in kept.items()}
    mod_grad = joined["mgrad"].astype(jnp.bfloat16)
    pieces = [
        column_outer(joined["hone"], joined["gpack"]),
        column_outer(joined["attn"], joined["gbranch"]),
        column_outer(joined["htwo"], joined["gup"]),
        column_outer(joined["gmlp"], joined["act"]),
        column_outer(own_silu, mod_grad),
    ]
    summed = lax.psum_scatter(
        jnp.concatenate(pieces, axis=1).astype(jnp.bfloat16), "seq", scatter_dimension=0, tiled=True
    )
    share = lax.psum_scatter(summed, "dp", scatter_dimension=0, tiled=True).astype(jnp.float32)
    replicated = lax.all_gather(share.astype(jnp.bfloat16), "dp", axis=0, tiled=True).astype(
        share.dtype
    )
    packed_sums = jnp.sum(joined["gpack"], axis=0, dtype=jnp.float32)
    heads_part = jnp.concatenate([packed_sums[:D], packed_sums[2 * D :]])
    merge_part = jnp.sum(joined["gbranch"], axis=0, dtype=jnp.float32)
    up_part = jnp.sum(joined["gup"], axis=0, dtype=jnp.float32)
    down_part = jnp.sum(joined["gmlp"], axis=0, dtype=jnp.float32)
    modulate_part = jnp.sum(mod_grad, axis=0, dtype=jnp.float32)
    heads_total, merge_total, up_total, down_total, modulate_total, table_total = lax.psum(
        (heads_part, merge_part, up_part, down_part, modulate_part, table_grad), ("dp", "seq")
    )
    edges = [0, 3 * D, 4 * D, 4 * D + FF, 4 * D + 2 * FF, 10 * D + 2 * FF]
    return (
        joined["out"],
        joined["tgrad"],
        replicated[:, edges[0] : edges[1]],
        replicated[:, edges[1] : edges[2]],
        replicated[:, edges[2] : edges[3]],
        replicated[:, edges[3] : edges[4]],
        replicated[:, edges[4] : edges[5]],
        heads_total,
        merge_total,
        up_total,
        down_total,
        modulate_total,
        table_total,
    )


def solution(mesh):
    in_specs = (
        P(("dp", "seq"), None),
        P("dp", None),
        P(("dp", "seq")),
        P(("dp", "seq"), None),
        P("seq", None),
        P(),
        P("seq", None),
        P(),
        P("seq", None),
        P(),
        P("seq", None),
        P(),
        P("seq", None),
        P(),
        P(),
        P(("dp", "seq"), None),
    )
    out_specs = (
        P(("dp", "seq"), None),
        P(("dp", "seq"), None),
        P("seq", None),
        P("seq", None),
        P("seq", None),
        P("seq", None),
        P("seq", None),
        P(),
        P(),
        P(),
        P(),
        P(),
        P(),
    )
    return jax.shard_map(local, mesh=mesh, in_specs=in_specs, out_specs=out_specs, check_vma=False)
```

profile of v0, /device:TPU:0, one launch (start us, length us, event | category | flops | bytes accessed | tf_op | source)
XLA Modules:
  0.0 2065.9 jit_solution(3447131822799105786)
XLA Ops:
  21.8 4.4 slice_convert_fusion.1
  26.2 227.8 %gather_fusion = bf16[65536,16]{1,0:T(8,128)(2,1)} fusion(bf16[16,961]{0,1:T(8,128)(2,1)S(1)} %copy.147, s32[65536]{0:T(1024)S(1)} %broadcast_clamp_fusion), kind=kCustom, calls=%fused_computation | custom fusion | bytes 4456448 | tf_op jit(solution)/shard_map/jit(_take)/gather | solution.py:171
  254.1 16.7 copy.148
  270.8 5.1 convert_bitcast_fusion
  275.8 3.4 convert_bitcast_fusion.1
  279.9 8.4 convolution_add_fusion
  292.9 57.3 %all-gather.10.cloned.1.call-done = bf16[1152,3456]{1,0:T(8,128)(2,1)} async-done(((bf16[144,3456]{1,0:T(8,128)(2,1)}), bf16[1152,3456]{1,0:T(8,128)(2,1)}) %all-gather.10.cloned.1.call-update) | async-done | bytes 7962640 | tf_op jit(solution)/shard_map/all_gather | solution.py:208
  350.2 9.5 add_convert_fusion.1
  359.8 5.8 copy.143
  365.5 8.3 reshape.859
  373.9 4.0 fusion.217
  391.1 14.6 all-gather.12.cloned.1.call-done
  405.7 6.8 fusion.212
  413.0 11.3 add_convert_fusion
  424.3 5.8 copy.152
  430.1 8.3 reshape.861
  438.4 3.9 fusion.218
  455.3 4.2 fusion.214
  469.5 89.3 %all-gather.14.cloned.1.call-done = bf16[1152,4608]{1,0:T(8,128)(2,1)} async-done(((bf16[144,4608]{1,0:T(8,128)(2,1)}), bf16[1152,4608]{1,0:T(8,128)(2,1)}) %all-gather.14.cloned.1.call-update) | async-done | bytes 10616848 | tf_op jit(solution)/shard_map/all_gather | solution.py:226
  558.8 11.6 fusion.231
  570.4 8.9 fusion.230
  579.3 132.2 %all-gather.16.cloned.1.call-done = bf16[1152,4608]{1,0:T(8,128)(2,1)} async-done(((bf16[144,4608]{1,0:T(8,128)(2,1)}), bf16[1152,4608]{1,0:T(8,128)(2,1)}) %all-gather.16.cloned.1.call-update) | async-done | bytes 10616848 | tf_op jit(solution)/shard_map/all_gather | solution.py:230
  711.5 11.6 fusion.232
  723.1 24.2 %fusion.11 = (bf16[512,4608]{1,0:T(8,128)(2,1)}, bf16[512,4608]{1,0:T(8,128)(2,1)}, bf16[512,4608]{1,0:T(8,128)(2,1)}, bf16[512,4608]{1,0:T(8,128)(2,1)}) fusion(f32[512,4608]{1,0:T(8,128)} %fusion.230, f32[4608]{0:T(1024)S(1)} %copy-done.104, f32[512,4608]{1,0:T(8,128)} %fusion.231, f32[512,4608]{1,0:T(8,128)} %fusion.232, ...), kind=kOutput, calls=%fused_computation.21 | convolution fusion | flops 5544345600 | bytes 59000832 | tf_op jit(solution)/shard_map/dot_general | solution.py:37
  747.3 12.7 multiply_reduce_fusion.11
  760.7 13.2 multiply_reduce_fusion.9
  774.6 14.4 fusion.210
  789.0 13.1 fusion.211
  803.3 3.8 fusion.71
  811.4 2.9 reshape.867
  814.4 5.3 multiply_reduce_fusion.1
  822.6 3.6 multiply_bitcast_fusion.2
  829.1 3.6 copy.181
  836.4 4.8 convolution_convert_fusion.4
  846.4 3.7 reshape.873
  850.9 6.1 multiply_reduce_fusion
  857.5 4.0 multiply_convert_fusion.2
  861.5 3.7 multiply_bitcast_fusion
  868.4 5.5 copy.182
  877.8 5.2 copy.183
  887.1 8.8 multiply_reduce_fusion.10
  903.3 10.3 multiply_reduce_fusion.8
  913.7 4.8 multiply_reduce_fusion.4
  920.1 10.9 fusion.4
  931.0 3.5 constant_dynamic-update-slice_fusion.14
  934.6 17.3 fusion.3
  951.9 16.6 fusion.2
  968.6 4.2 multiply_reduce_fusion.6
  974.6 3.7 multiply_reduce_fusion.5
  979.0 8.7 fusion.1
  987.7 748.8 %reduce-scatter.4.cloned.1.call-done = bf16[144,20736]{1,0:T(8,128)(2,1)} async-done(((bf16[1152,20736]{1,0:T(8,128)(2,1)}), bf16[144,20736]{1,0:T(8,128)(2,1)}) %reduce-scatter.4.cloned.1.call-update) | async-done | bytes 5971984 | tf_op jit(solution)/shard_map/reduce_scatter | solution.py:308
  1736.5 61.7 %fusion = bf16[40,20736]{1,0:T(8,128)(2,1)} fusion(bf16[144,20736]{1,0:T(8,128)(2,1)} %reduce-scatter.4.cloned.1.call-done), kind=kCustom, calls=%all-reduce-scatter | all-reduce-scatter fusion | flops 3317761 | bytes 7631360
  1803.7 17.0 concatenate.72
  1820.7 3.1 dynamic-slice_bitcast_fusion
  1823.9 6.8 fusion.32
  1830.7 8.1 bitcast_add_fusion.2
  1838.8 19.8 add.547
  1858.5 33.3 %fusion.185 = f32[31,16,16,16,1]{0,3,2,4,1:T(8,128)} fusion(f32[16,16,16,16,16]{4,3,2,1,0:T(8,128)} %add.547, s32[16,16]{1,0:T(8,128)S(1)} %subtract_add_fusion), kind=kOutput, calls=%fused_computation.258 | convolution fusion | flops 390078208 | bytes 4703232 | tf_op jit(solution)/shard_map/hwxyz,wya->haxz/dot_general | solution.py:146
  1891.9 4.1 fusion.151
  1899.3 4.2 convert_reduce_fusion.1
  1915.2 4.3 convert_reduce_fusion
  1919.5 10.3 reshape.899
  1929.9 5.7 fusion.216
  1942.0 108.8 %all-reduce.5.cloned.1.call-done = (f32[2304]{0:T(1024)}, f32[1152]{0:T(1024)}, f32[4608]{0:T(1024)}, f32[1152]{0:T(1024)}, f32[6912]{0:T(1024)}, /*index=5*/f32[16,961]{1,0:T(8,128)}) async-done(((f32[2304]{0:T(1024)}, f32[1152]{0:T(1024)}, f32[4608]{0:T(1024)}, f32[1152]{0:T(1024)}, f32[6912]{0:T(1024)}, /*index=5*/f32[16,961]{1,0:T(8,128)}), (f32[2304]{0:T(1024)}, f32[1152]{0:T(1024)}, f32[4608]{0:T(1024)}, ...) | async-done | bytes 126032 | tf_op jit(solution)/shard_map/psum | solution.py:321
  (480 shorter events, 135.2 us)
Async XLA Ops:
  7.2 272.7 %all-gather.8.cloned.1.call-start = ((), (), s32[]{:S(2)}) async-start(), calls=%async_computation.1 | async-start | bytes 17915904 | tf_op jit(solution)/shard_map/all_gather | solution.py:174
  7.9 342.3 %all-gather.10.cloned.1.call-start = ((), (), s32[]{:S(2)}) async-start(), calls=%async_computation.2 | async-start | bytes 8957952 | tf_op jit(solution)/shard_map/all_gather | solution.py:208
  8.7 397.0 %all-gather.12.cloned.1.call-start = ((), (), s32[]{:S(2)}) async-start(), calls=%async_computation.3 | async-start | bytes 2985984 | tf_op jit(solution)/shard_map/all_gather | solution.py:220
  9.4 549.4 %all-gather.14.cloned.1.call-start = ((), (), s32[]{:S(2)}) async-start(), calls=%async_computation.4 | async-start | bytes 11943936 | tf_op jit(solution)/shard_map/all_gather | solution.py:226
  10.0 701.5 %all-gather.16.cloned.1.call-start = ((), (), s32[]{:S(2)}) async-start(), calls=%async_computation.5 | async-start | bytes 11943936 | tf_op jit(solution)/shard_map/all_gather | solution.py:230
  10.6 1725.9 %reduce-scatter.4.cloned.1.call-start = ((), (), s32[]{:S(2)}) async-start(), calls=%async_computation.6 | async-start | bytes 53747712 | tf_op jit(solution)/shard_map/reduce_scatter | solution.py:308
  13.3 6.3 copy-start.150
  13.4 6.8 copy-start.151
  13.4 7.4 copy-start.128
  13.4 7.4 copy-start.129
  13.4 8.1 copy-start.127
  13.4 8.1 copy-start.100
  17.2 253.6 %copy-start.135 = (s32[2,256]{1,0:T(2,128)}, s32[2,256]{1,0:T(2,128)S(1)}, u32[]{:S(2)}) copy-start(s32[2,256]{1,0:T(2,128)S(1)} %get-tuple-element.193) | copy-start | bytes 6148
  17.2 362.1 %copy-start.98 = (s32[2,256]{1,0:T(2,128)}, s32[2,256]{1,0:T(2,128)S(1)}, u32[]{:S(2)}) copy-start(s32[2,256]{1,0:T(2,128)S(1)} %get-tuple-element.192) | copy-start | bytes 6148
  292.9 66.9 %copy-start.63 = (bf16[512,1152]{1,0:T(8,128)(2,1)}, bf16[512,1152]{1,0:T(8,128)(2,1)S(1)}, u32[]{:S(2)}) copy-start(bf16[512,1152]{1,0:T(8,128)(2,1)S(1)} %fusion.98) | copy-start | bytes 3538948
  378.0 7.5 copy-start.35
  388.9 16.7 copy-start.103
  390.4 22.0 %copy-start.54 = (bf16[144,8,2,256]{3,1,2,0:T(8,128)(2,1)}, bf16[144,8,2,256]{3,1,2,0:T(8,128)(2,1)S(1)}, u32[]{:S(2)}) copy-start(bf16[144,8,2,256]{3,1,2,0:T(8,128)(2,1)S(1)} %copy.251) | copy-start | bytes 3538948
  391.1 21.3 %copy-start.70 = (f32[2,1152]{1,0:T(2,128)}, f32[2,1152]{1,0:T(2,128)S(1)}, u32[]{:S(2)}) copy-start(f32[2,1152]{1,0:T(2,128)S(1)} %get-tuple-element.247) | copy-start | bytes 27652
  442.3 7.8 copy-start.37
  463.0 311.6 %copy-start.74 = (f32[2,1152]{1,0:T(2,128)}, f32[2,1152]{1,0:T(2,128)S(1)}, u32[]{:S(2)}) copy-start(f32[2,1152]{1,0:T(2,128)S(1)} %get-tuple-element.239) | copy-start | bytes 27652
  465.7 323.3 %copy-start.81 = (f32[2,1152]{1,0:T(2,128)}, f32[2,1152]{1,0:T(2,128)S(1)}, u32[]{:S(2)}) copy-start(f32[2,1152]{1,0:T(2,128)S(1)} %get-tuple-element.235) | copy-start | bytes 27652
  558.8 11.7 copy-start.66
  558.8 11.7 copy-start.155
  711.5 11.6 copy-start.5
  711.5 11.6 copy-start.104
  760.7 13.2 copy-start.110
  760.7 13.8 copy-start.88
  760.7 13.8 copy-start.108
  760.7 13.8 copy-start.149
  774.5 14.5 copy-start.10
  774.5 14.5 copy-start.11
  774.5 14.5 copy-start.106
  774.5 14.5 copy-start.147
  789.0 14.2 copy-start.71
  850.9 6.1 slice-start.2
  850.9 6.6 slice-start.3
  887.0 8.9 copy-start.139
  887.0 8.9 copy-start.1
  887.0 8.9 copy-start.13
  887.1 8.9 copy-start.15
  887.1 8.9 copy-start.114
  903.3 10.3 copy-start.138
  903.3 10.4 copy-start.12
  903.3 10.4 copy-start.14
  903.3 10.4 copy-start.73
  903.3 10.4 copy-start.115
  920.1 10.9 copy-start.17
  934.6 17.3 copy-start.52
  951.8 16.7 copy-start.75
  951.8 16.7 copy-start.126
  951.9 16.7 copy-start.134
  968.6 6.0 copy-start.28
  968.6 6.0 copy-start.82
  987.7 814.8 %copy-start.154 = (u32[32]{0:T(128)S(1)}, u32[32]{0:T(128)}, u32[]{:S(2)}) copy-start(u32[32]{0:T(128)} %constant.195) | copy-start | bytes 388
  987.7 931.9 %all-gather.18.cloned.1.call-start = ((), (), s32[]{:S(2)}) async-start(), calls=%async_computation.7 | async-start | bytes 8294400 | tf_op jit(solution)/shard_map/all_gather | solution.py:312
  1800.3 3.4 collective-permute-start
  1823.8 226.9 %all-reduce.5.cloned.1.call-start = ((), (), s32[]{:S(2)}) async-start(), calls=%async_computation.8 | async-start | bytes 286720 | tf_op jit(solution)/shard_map/psum | solution.py:321
  1823.9 6.8 copy-start.99
  1899.2 6.8 copy-start.43
  1899.2 6.9 copy-start.44
  1899.2 8.5 copy-start.77
  1899.3 8.5 copy-start.80
  1929.9 8.5 copy-start.4
  (107 other events, 345.6 us)
Sparse Core Ops, SparseCore 0:
  10.2 219.8 all-gather.7
  232.3 117.8 all-gather.9
  352.4 53.1 all-gather.11
  407.7 151.0 all-gather.13
  560.8 150.6 all-gather.15
  987.8 748.6 reduce-scatter.3
  1824.0 55.2 all-gather.17
  1919.6 131.0 all-reduce.4
where the time goes:
time: 2070 us
  waiting for transfers between devices  1150 us (56%)
  local copies, waits for them, and re-layouts  431 us (21%)
  matrix products  327 us (16%)
  other arithmetic  73 us (4%)
  blocking collectives  61.7 us (3%)
    reduce_scatter x1, waiting for transfers between devices, local(): lax.psum_scatter(jnp.concatenate(pieces, axis=1).astype(jnp.bfloat16), 's...  749 us
    gather x2, local copies, waits for them, and re-layouts, local(): jnp.take(relative_table, relative_index(jnp.arange(GRID)), axis=1)  245 us
    all_gather x1, waiting for transfers between devices, local(): lax.all_gather(down_weight, 'seq', axis=0, tiled=True)  132 us
    psum x1, waiting for transfers between devices, local(): lax.psum((heads_part, merge_part, up_part, down_part, modulate_part, tabl...  109 us
    dot_general x9, matrix products, fold_rows(): return jnp.dot(left, portion, preferred_element_type=jnp.float32)  96.5 us
    all_gather x1, waiting for transfers between devices, local(): lax.all_gather(up_weight, 'seq', axis=0, tiled=True)  89.3 us
    dot_general x8, matrix products, right_transposed(): lax.dot_general(left, portion, (((1,), (1,)), ((), ())), preferred_elemen...  77.3 us
    unnamed x359, local copies, waits for them, and re-layouts  65.2 us
  transfers between devices with their start and end apart: 9, of which 6 were waited for; matrix products, arithmetic and copies ran while one was open for 25% of the time, Pallas kernels for 0%

commit v1 on v0

v1 whole, which is shorter than its diff:
```python
import functools
import math

import jax
import jax.numpy as jnp
import numpy as np
from jax import lax
from jax.experimental import pallas as pl
from jax.experimental.pallas import tpu as pltpu
from jax.sharding import PartitionSpec as P

D = 1152
HEADS = 16
HEAD = 72
FF = 4608
SIDE = 16
GRID = 256
SPAN = 2 * SIDE - 1
WIDE = 4608
TILE = 768
ROWS8 = 144
QUARTERS = 4
LIFT = math.log2(math.e)
SCALE = 1.0 / math.sqrt(HEAD)
EPS = 1e-06
ORDER = (0, 4, 2, 6, 1, 5, 3, 7)
BF = jnp.bfloat16
F32 = jnp.float32
VMEM_LIMIT = 60 * 1024 * 1024


def dot(a, b):
    return jnp.dot(a, b, preferred_element_type=F32)


def dot_rt(a, b):
    return lax.dot_general(a, b, (((1,), (1,)), ((), ())), preferred_element_type=F32)


def dot_lt(a, b):
    return lax.dot_general(a, b, (((0,), (0,)), ((), ())), preferred_element_type=F32)


def params():
    return pltpu.CompilerParams(
        vmem_limit_bytes=VMEM_LIMIT, dimension_semantics=("arbitrary",)
    )


def cost(flops, bytes_accessed, transcendentals=0):
    return pl.CostEstimate(
        flops=int(flops), bytes_accessed=int(bytes_accessed), transcendentals=int(transcendentals)
    )


def rows_spec(width):
    return lambda first: pl.BlockSpec((GRID, width), lambda s, *_: (s + first, 0))


def own_rows(width):
    return lambda first: pl.BlockSpec((GRID, width), lambda s, *_: (s, 0))


def per_sample(*tail):
    return lambda first: pl.BlockSpec((1,) + tail, lambda s, *_: (s + first,) + (0,) * len(tail))


def fixed(*shape, at=None):
    where = (0,) * len(shape) if at is None else at
    return lambda first: pl.BlockSpec(shape, lambda s, *_: where)


def anywhere(first):
    return pl.BlockSpec(memory_space=pl.ANY)


def call(kernel, scal, inputs, in_specs, outs, scratch, span, name, price, prior=None, steps=None):
    first, samples = span
    kept = [] if prior is None else [(i, v) for i, v in enumerate(prior) if v is not None]
    count = len(inputs)

    def body(scal_ref, *refs):
        kernel(span, scal_ref, *refs[:count], *refs[count + len(kept) :])

    return pl.pallas_call(
        body,
        grid_spec=pltpu.PrefetchScalarGridSpec(
            num_scalar_prefetch=1,
            grid=(samples if steps is None else steps,),
            in_specs=[spec(first) for spec in in_specs] + [anywhere(first)] * len(kept),
            out_specs=[spec(first) for _, _, spec in outs],
            scratch_shapes=scratch,
        ),
        out_shape=[jax.ShapeDtypeStruct(shape, kind) for shape, kind, _ in outs],
        input_output_aliases={1 + count + n: i for n, (i, _) in enumerate(kept)},
        compiler_params=params(),
        cost_estimate=price,
        name=name,
    )(scal, *inputs, *[v for _, v in kept])


def normal(values):
    center = values - jnp.mean(values, axis=-1, keepdims=True)
    inverse = lax.rsqrt(jnp.mean(center * center, axis=-1, keepdims=True) + EPS)
    return center * inverse, inverse


def norm_back(unit, inverse, grad):
    return (
        grad
        - jnp.mean(grad, axis=-1, keepdims=True)
        - unit * jnp.mean(grad * unit, axis=-1, keepdims=True)
    ) * inverse


def accumulate(ref, value, step):
    @pl.when(step == 0)
    def _():
        ref[...] = value

    @pl.when(step > 0)
    def _():
        ref[...] = ref[...] + value


def column_sum(values):
    return jnp.sum(values.astype(F32), axis=0, keepdims=True)


def place_kernel(span, scal, tokens, cotangent, index, xg, cg, mask):
    length = scal[2 + span[0] + pl.program_id(0)]
    spots = lax.broadcasted_iota(jnp.int32, (GRID, GRID), 0)
    slots = lax.broadcasted_iota(jnp.int32, (GRID, GRID), 1)
    hit = spots == index[0]
    xg[...] = dot(hit.astype(F32).astype(BF), tokens[...]).astype(BF)
    alive = jnp.logical_and(hit, slots < length).astype(F32).astype(BF)
    cg[...] = dot(alive, cotangent[...]).astype(BF)
    row = dot_rt(jnp.ones((8, GRID), BF), alive)[0:1]
    mask[0] = jnp.where(row > 0.5, 0.0, -1e30)


def bias_kernel(span, scal, strips, out):
    strip = strips[0]
    for row in range(SIDE):
        start = (SIDE - 1 - row) * SIDE
        out[0, row * SIDE : (row + 1) * SIDE, :] = strip[:, start : start + GRID] * LIFT


def strips_kernel(span, scal, first, second, out):
    out[...] = jnp.zeros_like(out)
    for row in range(SIDE):
        start = (SIDE - 1 - row) * SIDE
        rows = slice(row * SIDE, (row + 1) * SIDE)
        out[0, :, start : start + GRID] = out[0, :, start : start + GRID] + (first[0, rows, :] + second[0, rows, :])


def window(h):
    start = jnp.minimum((h * HEAD) // 128 * 128, D - 256)
    lanes = lax.broadcasted_iota(jnp.int32, (1, 256), 1) + start
    inside = jnp.logical_and(lanes >= h * HEAD, lanes < (h + 1) * HEAD)
    return pl.multiple_of(start, 128), inside.astype(F32).astype(BF)


def piece_copies(pieces, gap_dp, scal, target, sems):
    copies = []
    for i, gap in enumerate(ORDER):
        rows = pl.ds(pl.multiple_of((scal[0] ^ gap) * ROWS8, ROWS8), ROWS8)
        source = pieces[2 * (gap_dp // 2) + i // 4].at[i % 4]
        copies.append(pltpu.make_async_copy(source, target.at[rows, :], sems.at[i]))
    return copies


def qkv_kernel(span, scal, xg, mods, full_bias, weight, h1, packed):
    unit, _ = normal(xg[...].astype(F32))
    hidden = (unit * (1.0 + mods[0, 1:2]) + mods[0, 0:1]).astype(BF)
    h1[...] = hidden
    for j in range(3):
        cols = slice(j * D, (j + 1) * D)
        packed[:, cols] = (dot(hidden, weight[j]) + full_bias[:, cols]).astype(BF)


def attend_kernel(span, scal, packed, mask, table, attended, lse, mixed):
    mixed[...] = jnp.zeros_like(mixed)
    lse[...] = jnp.zeros_like(lse)
    lane = lax.broadcasted_iota(jnp.int32, (GRID, 128), 1)

    def head(h, _):
        start, inside = window(h)
        query = packed[:, pl.ds(start, 256)] * inside
        key = packed[:, pl.ds(pl.multiple_of(D + start, 128), 256)]
        value = packed[:, pl.ds(pl.multiple_of(2 * D + start, 128), 256)] * inside
        scores = dot_rt(query, key) * (SCALE * LIFT) + table[h] + mask[0]
        peak = jnp.max(scores, axis=1, keepdims=True)
        expo = jnp.exp2(scores - peak)
        mass = jnp.sum(expo, axis=1, keepdims=True)
        probs = (expo * (1.0 / mass)).astype(BF)
        cols = pl.ds(start, 256)
        mixed[:, cols] = mixed[:, cols] + dot(probs, value)
        lse[...] = jnp.where(lane == h, peak + jnp.log2(mass), lse[...])
        return 0

    lax.fori_loop(0, HEADS, head, 0, unroll=HEADS)
    attended[...] = mixed[...].astype(BF)


def merge_kernel(span, scal, attended, xg, cg, mods, merge_bias, weight, branch, middle, h2, gm, gm_sum):
    low = (mods[0, 5:6] * cg[...].astype(F32)).astype(BF)
    gm[...] = low
    accumulate(gm_sum, column_sum(low), pl.program_id(0))
    merged = dot(attended[...], weight[0]) + merge_bias[...]
    branch[...] = merged.astype(BF)
    mid = xg[...].astype(F32) + mods[0, 2:3] * merged
    middle[...] = mid
    unit, _ = normal(mid)
    h2[...] = (unit * (1.0 + mods[0, 4:5]) + mods[0, 3:4]).astype(BF)


def up_kernel(samples, gaps, scal, quarters, h2, bias, *refs):
    step = pl.program_id(0)
    if gaps is None:
        weight, act, slope = refs
        matrix = lambda: weight[0]
    else:
        pieces = refs[:4]
        act, slope, spread, target, sems, out_sems = refs[4:]
        steps = len(gaps)
        matrix = lambda: target[step]
        fetch = [piece_copies(pieces, gap, scal, target.at[n], sems.at[n]) for n, gap in enumerate(gaps)]
        store = [pltpu.make_async_copy(target.at[n], spread.at[n], out_sems.at[n]) for n in range(steps)]
        for n in range(steps):
            @pl.when(step == 0)
            def _():
                for copy in fetch[n]:
                    copy.start()
        for n in range(steps):
            @pl.when(step == n)
            def _():
                for copy in fetch[n]:
                    copy.wait()
                store[n].start()

    root = math.sqrt(2.0 / math.pi)
    for s in range(samples):
        rows = slice(s * GRID, (s + 1) * GRID)
        u = dot(h2[rows, :], matrix()) + bias[...]
        square = u * u
        t = jnp.tanh(u * ((root * 0.044715) * square + root))
        half = 0.5 * t + 0.5
        act[rows, :] = (u * half).astype(BF)
        bell = half * (1.0 - half)
        slope[rows, :] = (half + bell * (u * ((6 * root * 0.044715) * square + 2 * root))).astype(BF)
    if gaps is not None:
        for n in range(steps):
            @pl.when(step == steps - 1)
            def _():
                store[n].wait()


def up_quarters(h2, bias, weight, scal, quarters, gaps):
    count, steps = h2.shape[0], quarters.shape[0]
    column = pl.BlockSpec((None, count, D), lambda k, *_: (k, 0, 0))
    out = [jax.ShapeDtypeStruct((steps, count, D), BF)] * 2
    if gaps is None:
        weight = [weight]
        weight_specs, out_specs, scratch = [pl.BlockSpec((1, D, D), lambda k, scal, q: (q[k], 0, 0))], [column] * 2, []
    else:
        weight_specs, out_specs = [anywhere(0)] * 4, [column] * 2 + [anywhere(0)]
        out = out + [jax.ShapeDtypeStruct((steps, D, D), BF)]
        scratch = [pltpu.VMEM((steps, D, D), BF), pltpu.SemaphoreType.DMA((steps, 8)), pltpu.SemaphoreType.DMA((steps,))]
    return pl.pallas_call(
        functools.partial(up_kernel, count // GRID, gaps),
        grid_spec=pltpu.PrefetchScalarGridSpec(
            num_scalar_prefetch=2,
            grid=(steps,),
            in_specs=[pl.BlockSpec((count, D), lambda k, *_: (0, 0)), pl.BlockSpec((1, D), lambda k, scal, q: (0, q[k]))]
            + weight_specs,
            out_specs=out_specs,
            scratch_shapes=scratch,
        ),
        out_shape=out,
        compiler_params=params(),
        cost_estimate=cost(2 * count * D * D * steps, 2 * D * steps * (3 * count + 2 * D), count * D * steps),
        name="up",
    )(scal, quarters, h2, bias, *weight)


def act_back_kernel(samples, scal, quarters, gm, slope, weight, *refs):
    gu, gu_sum = refs[-2:]
    total = jnp.zeros((1, D), F32)
    for s in range(samples):
        rows = slice(s * GRID, (s + 1) * GRID)
        low = (dot(gm[rows, :], weight[0]) * slope[rows, :].astype(F32)).astype(BF)
        gu[0, rows, :] = low
        total = total + column_sum(low)
    gu_sum[...] = total


def act_back(gm, slope, weight, scal, quarters, prior):
    count, steps = gm.shape[0], quarters.shape[0]
    whole = pl.BlockSpec((count, D), lambda k, *_: (0, 0))
    return pl.pallas_call(
        functools.partial(act_back_kernel, count // GRID),
        grid_spec=pltpu.PrefetchScalarGridSpec(
            num_scalar_prefetch=2,
            grid=(steps,),
            in_specs=[
                whole,
                pl.BlockSpec((None, count, D), lambda k, *_: (k, 0, 0)),
                pl.BlockSpec((1, D, D), lambda k, scal, q: (q[k], 0, 0)),
            ]
            + [anywhere(0)] * (prior is not None),
            out_specs=[
                pl.BlockSpec((1, count, D), lambda k, *_: (k, 0, 0)),
                pl.BlockSpec((1, D), lambda k, scal, q: (0, q[k])),
            ],
        ),
        out_shape=[jax.ShapeDtypeStruct((steps, count, D), BF), jax.ShapeDtypeStruct((1, FF), F32)],
        input_output_aliases={} if prior is None else {5: 1},
        compiler_params=params(),
        cost_estimate=cost(2 * count * D * D * steps, 2 * D * steps * (2 * count + D)),
        name="act_back",
    )(scal, quarters, gm, slope, weight, *([] if prior is None else [prior]))


def turned_product(parts, scal, quarters, weights, late, late_specs, outs, finish, span, name, prior=None):
    first, samples = span
    count, tiles = samples * GRID, quarters.shape[0]
    kept = [] if prior is None else [(i, v) for i, v in enumerate(prior) if v is not None]
    starts = np.minimum(np.cumsum([0] + [p.shape[0] if p.ndim == 3 else p.shape[1] // D for p in parts]), tiles)
    used = len(parts) + len(weights)

    def body(scal_ref, quarters_ref, *refs):
        total = refs[-1]
        ins, ws = refs[: len(parts)], refs[len(parts) : used]
        late_refs = refs[used : used + len(late)]
        out_refs = refs[used + len(late) + len(kept) : -1]
        step = pl.program_id(0)
        for n, ref in enumerate(ins):
            w = ws[n % len(ws)]

            @pl.when(jnp.logical_and(step >= starts[n], step < starts[n + 1]))
            def _():
                for s in range(samples):
                    part = dot_rt(ref[s * GRID : (s + 1) * GRID, :], w[0])

                    @pl.when(step == 0)
                    def _():
                        total[s] = part

                    @pl.when(step > 0)
                    def _():
                        total[s] = total[s] + part

        @pl.when(step >= tiles)
        def _():
            finish(span, scal_ref, step - tiles, total[step - tiles], late_refs, out_refs)

    def shift(spec):
        block = spec(first)
        return pl.BlockSpec(block.block_shape, lambda k, *a: block.index_map(jnp.maximum(k - tiles, 0), *a))

    def part_spec(n):
        low, high = int(starts[n]), int(starts[n + 1]) - 1
        offset = 0 if parts[n].shape[-2] == count else first // samples
        return column_block(parts[n], count, D, lambda k, *_: jnp.clip(k, low, high) - low, offset)

    def weight_spec(n):
        if len(weights) == 1:
            return pl.BlockSpec((1, D, D), lambda k, scal, q: (q[jnp.minimum(k, tiles - 1)], 0, 0))
        low, high = int(starts[n]), int(starts[n + 1]) - 1
        return pl.BlockSpec((1, D, D), lambda k, *_: (jnp.clip(k, low, high) - low, 0, 0))

    return pl.pallas_call(
        body,
        grid_spec=pltpu.PrefetchScalarGridSpec(
            num_scalar_prefetch=2,
            grid=(tiles + samples,),
            in_specs=[part_spec(n) for n in range(len(parts))]
            + [weight_spec(n) for n in range(len(weights))]
            + [shift(spec) for spec in late_specs]
            + [anywhere(0)] * len(kept),
            out_specs=[shift(spec) for _, _, spec in outs],
            scratch_shapes=[pltpu.VMEM((samples, GRID, D), F32)],
        ),
        out_shape=[jax.ShapeDtypeStruct(shape, kind) for shape, kind, _ in outs],
        input_output_aliases={2 + used + len(late) + n: i for n, (i, _) in enumerate(kept)},
        compiler_params=params(),
        cost_estimate=cost(2 * count * D * D * tiles, 2 * D * tiles * (count + D) + 10 * count * D),
        name=name,
    )(scal, quarters, *parts, *weights, *late, *[v for _, v in kept])


def mid_back_finish(span, scal, sample, grad, late, outs):
    middle, branch, cg, mods = late
    gmid, gbr, gbr_sum, grads = outs
    unit, inverse = normal(middle[...])
    whole = cg[...].astype(F32) + norm_back(unit, inverse, grad * (1.0 + mods[0, 4:5]))
    gmid[...] = whole
    low = (mods[0, 2:3] * whole).astype(BF)
    gbr[...] = low
    accumulate(gbr_sum, column_sum(low), sample)
    grads[0, 0:1] = column_sum(whole * branch[...].astype(F32))
    grads[0, 1:2] = column_sum(grad)
    grads[0, 2:3] = column_sum(grad * unit)


def front_back_finish(span, scal, sample, grad, late, outs):
    xg, gmid, mods, column = late
    tgrad, grads = outs
    unit, inverse = normal(xg[...].astype(F32))
    grads[0, 0:1] = column_sum(grad)
    grads[0, 1:2] = column_sum(grad * unit)
    whole = gmid[...] + norm_back(unit, inverse, grad * (1.0 + mods[0, 1:2]))
    pick = (lax.broadcasted_iota(jnp.int32, (GRID, GRID), 1) == column[...]).astype(F32).astype(BF)
    high = whole.astype(BF)
    rest = (whole - high.astype(F32)).astype(BF)
    tgrad[...] = dot(pick, high) + dot(pick, rest)


def down_finish(span, scal, sample, product, late, outs):
    middle, cg, mods, bias, column = late
    out, grads = outs
    mlp = product + bias[...]
    grads[0] = column_sum(cg[...].astype(F32) * mlp)
    final = (middle[...] + mods[0, 5:6] * mlp).astype(BF)
    length = scal[2 + span[0] + sample]
    spots = lax.broadcasted_iota(jnp.int32, (GRID, GRID), 1)
    slots = lax.broadcasted_iota(jnp.int32, (GRID, GRID), 0)
    pick = jnp.logical_and(spots == column[...], slots < length).astype(F32).astype(BF)
    out[...] = dot(pick, final).astype(BF)


def attend_back_kernel(span, scal, gbr, packed, lse, mask, table, weight, joined, joined_sum, placed, gatt, gq, gk, gv):
    gatt[...] = dot_rt(gbr[...], weight[0]).astype(BF)
    for ref in (gq, gk, gv):
        ref[...] = jnp.zeros_like(ref)

    @pl.when(pl.program_id(0) == 0)
    def _():
        placed[...] = jnp.zeros_like(placed)
        joined_sum[...] = jnp.zeros_like(joined_sum)

    lane = lax.broadcasted_iota(jnp.int32, (GRID, 128), 1)

    def head(h, _):
        start, inside = window(h)
        cols = pl.ds(start, 256)
        query = packed[:, cols] * inside
        key = packed[:, pl.ds(pl.multiple_of(D + start, 128), 256)] * inside
        value = packed[:, pl.ds(pl.multiple_of(2 * D + start, 128), 256)]
        grad = gatt[:, cols] * inside
        scores = dot_rt(query, key) * (SCALE * LIFT) + table[h] + mask[0]
        own = jnp.sum(jnp.where(lane == h, lse[...], 0.0), axis=1, keepdims=True)
        probs = jnp.exp2(scores - own)
        gprobs = dot_rt(grad, value)
        weighted = probs * gprobs
        inner = jnp.sum(weighted, axis=1, keepdims=True)
        gscores = (weighted - probs * inner).astype(BF)
        placed[h] = placed[h] + gscores.astype(F32)
        gq[:, cols] = gq[:, cols] + dot(gscores, key)
        gk[:, cols] = gk[:, cols] + dot_lt(gscores, query)
        gv[:, cols] = gv[:, cols] + dot_lt(probs.astype(BF), grad)
        return 0

    lax.fori_loop(0, HEADS, head, 0, unroll=HEADS)
    for j, (ref, factor) in enumerate(((gq, SCALE), (gk, SCALE), (gv, 1.0))):
        cols = slice(j * D, (j + 1) * D)
        low = (ref[...] * factor).astype(BF)
        joined[:, cols] = low
        joined_sum[:, cols] = joined_sum[:, cols] + column_sum(low)
    joined[:, 3 * D :] = gbr[...]


def column_block(array, rows, width, at, row=0):
    if array.ndim == 2:
        return pl.BlockSpec((rows, width), lambda *a: (row, at(*a)))
    return pl.BlockSpec((None, rows, width), lambda *a: (at(*a), row, 0))


def plain_outer_kernel(kinds, scal, *refs):
    lefts, (right, out) = refs[:kinds], refs[kinds:]
    for kind, left in enumerate(lefts):
        def product():
            out[0] = dot_lt(left[...], right[...]).astype(BF)

        if kinds == 1:
            product()
        else:
            pl.when((pl.program_id(0) == QUARTERS - 1) == (kind == 1))(product)


def plain_outer(lefts, right, scal, name):
    count = right.shape[-2]
    return pl.pallas_call(
        functools.partial(plain_outer_kernel, len(lefts)),
        grid_spec=pltpu.PrefetchScalarGridSpec(
            num_scalar_prefetch=1,
            grid=(QUARTERS,),
            in_specs=[pl.BlockSpec((count, D), lambda q, *_: (0, 0))] * len(lefts)
            + [column_block(right, count, D, lambda q, *_: q)],
            out_specs=pl.BlockSpec((1, D, D), lambda q, *_: (q, 0, 0)),
        ),
        out_shape=jax.ShapeDtypeStruct((QUARTERS, D, D), BF),
        compiler_params=params(),
        cost_estimate=cost(2 * count * D * WIDE, 2 * count * (D + WIDE) + 2 * D * WIDE),
        name=name,
    )(scal, *lefts, right)


def outer_kernel(kinds, sources, tile_width, roles, parts, order, scal, blocks, *refs):
    lefts, rights = refs[: sources * kinds], refs[sources * kinds : sources * (kinds + 1)]
    outs, tile = refs[sources * (kinds + 1) : -1], refs[-1]
    step = pl.program_id(0)

    def product(kind, cols):
        total = dot_lt(lefts[sources * kind][...], rights[0][:, cols])
        for n in range(1, sources):
            total = total + dot_lt(lefts[sources * kind + n][...], rights[n][:, cols])
        tile[:, cols] = total.astype(BF)

    if kinds == 1:
        product(0, slice(0, tile_width))
    else:
        half = tile_width // 2
        for part in range(2):
            from_first = blocks[step] * 2 + part < 3 * D // half
            cols = slice(part * half, (part + 1) * half)
            pl.when(from_first)(functools.partial(product, 0, cols))
            pl.when(jnp.logical_not(from_first))(functools.partial(product, 1, cols))
    for r in range(roles):
        @pl.when(step == r)
        def _():
            for i in range(8):
                start = i * ROWS8 if order is None else pl.multiple_of((scal[0] ^ order[i]) * ROWS8, ROWS8)
                rows = pl.ds(start, ROWS8)
                outs[parts * r + i * parts // 8][i % (8 // parts)] = tile[rows, :]


def outer_tiles(lefts, rights, scal, blocks, width, parts, order, name):
    count, kinds, roles, sources = rights[0].shape[-2], len(lefts), blocks.shape[0], len(rights)
    some = pl.BlockSpec((8 // parts, ROWS8, width), lambda r, *_: (0, 0, 0))
    each = sources // len(lefts[0])
    left_specs = [pl.BlockSpec((count, D), lambda r, *_, n=n: (n, 0)) for n in range(each)] * (len(lefts[0]) * kinds)
    return pl.pallas_call(
        functools.partial(outer_kernel, kinds, sources, width, roles, parts, order),
        grid_spec=pltpu.PrefetchScalarGridSpec(
            num_scalar_prefetch=2,
            grid=(roles,),
            in_specs=left_specs + [column_block(rights[0], count, width, lambda r, scal, blocks: blocks[r])] * sources,
            out_specs=[some] * (parts * roles),
            scratch_shapes=[pltpu.VMEM((D, width), BF)],
        ),
        out_shape=[jax.ShapeDtypeStruct((8 // parts, ROWS8, width), BF)] * (parts * roles),
        compiler_params=params(),
        cost_estimate=cost(
            2 * sources * count * D * width * roles, 2 * sources * count * (D * kinds + width * roles)
        ),
        name=name,
    )(scal, blocks, *[v for left in lefts for v in left for _ in range(each)], *rights)


ON_THE_WAY = []


def flip(value, axis, size, bit):
    ON_THE_WAY.append(lax.ppermute(value, axis, [(i, i ^ bit) for i in range(size)]))
    return ON_THE_WAY[-1]


def bits_of(size):
    return [1 << k for k in range(size.bit_length() - 1)]


def gather_steps(value, axes):
    for axis, size in axes:
        own = lax.axis_index(axis)
        for bit in bits_of(size):
            (value,) = yield [value]
            other = flip(value, axis, size, bit)
            low = (own & bit) == 0
            value = jnp.concatenate([jnp.where(low, value, other), jnp.where(low, other, value)], axis=0)
    return value


def scatter_steps(value, axis, size):
    own = lax.axis_index(axis)
    for bit in bits_of(size):
        value = value.reshape((value.shape[0] // 2, 2) + value.shape[1:])
        low = (own & bit) == 0
        keep = jnp.where(low, value[:, 0], value[:, 1])
        send = jnp.where(low, value[:, 1], value[:, 0]).astype(BF)
        (send,) = yield [send]
        value = keep + flip(send, axis, size, bit).astype(F32)
    return value


class Chain:
    def __init__(self, steps):
        self.steps, self.result = steps, None
        self.ready = next(steps)

    def advance(self, operands):
        if self.result is None:
            try:
                self.ready = self.steps.send(operands)
            except StopIteration as end:
                self.ready, self.result = [], end.value

    def finish(self):
        while self.result is None:
            self.advance(self.ready)
        return self.result


def slot(inputs, chains=(), after=(), slow=()):
    chains, slow = list(chains), list(slow)
    inputs, operands, _ = lax.optimization_barrier(
        (tuple(inputs), [c.ready for c in chains + slow], (*after, *ON_THE_WAY))
    )
    ON_THE_WAY.clear()
    for chain, ready in zip(slow, operands[len(chains) :]):
        chain.advance(ready)
    ON_THE_WAY.clear()
    for chain, ready in zip(chains, operands):
        chain.advance(ready)
    return inputs


class Wires:
    def __init__(self, mesh):
        self.dp, self.seq = mesh.shape["dp"], mesh.shape["seq"]
        self.cube = self.dp == 4 and self.seq == 8
        self.place, self.me = lax.axis_index("dp"), lax.axis_index("seq")

    def far(self, value, bit):
        return flip(value, "seq", self.seq, bit)

    def across(self, value):
        return flip(value, "dp", self.dp, 2)

    def sibling(self, value):
        return flip(value, "dp", self.dp, 1)

    def quarter(self, shards):
        if len(shards) == 1:
            return lax.dynamic_slice_in_dim(shards[0], self.place * D, D, 1)[None]
        heads = lax.dynamic_slice_in_dim(shards[0], jnp.minimum(self.place, 2) * D, D, 1)
        return jnp.where(self.place == 3, shards[1], heads)[None]

    def gather(self, quarter):
        return lax.all_gather(quarter, ("dp", "seq"), axis=0, tiled=True).reshape(QUARTERS, D, D)

    def gather_steps(self, quarter):
        (one,) = yield [quarter]
        two = jnp.concatenate([one, self.far(one, 4)], axis=0)
        (two,) = yield [two]
        four = jnp.concatenate([two, self.far(two, 2)], axis=0)
        (four,) = yield [four]
        rest, cross = self.far(four, 1), self.across(four)
        rest, cross, four = yield [rest, cross, four]
        cross_rest, near = self.across(rest), [self.sibling(four), self.sibling(rest), self.sibling(cross)]
        cross_rest, *near = yield [cross_rest, *near]
        return [four, rest, cross, cross_rest], [*near, self.sibling(cross_rest)]

    def scatter(self, whole):
        rows = D // self.seq
        parts = whole.reshape(QUARTERS * self.seq, rows, D)
        return lax.psum_scatter(parts, ("dp", "seq"), scatter_dimension=0, tiled=True)

    def spread(self, part):
        parts = yield from gather_steps(part, (("dp", self.dp),))
        return jnp.concatenate([parts[q] for q in range(QUARTERS)], axis=1)

    def reduce_quarter(self, cross, quarter, groups):
        got = {}
        for group in groups:
            sent = yield [cross[part] for part in group]
            for part, value in zip(group, sent):
                got[part] = self.across(value)
        upper = [(quarter[part].astype(F32) + got[part].astype(F32)).astype(BF) for part in (2, 3)]
        left = [part for part in (0, 1) if part not in got]
        send, *sent = yield [jnp.concatenate(upper, axis=0)] + [cross[part] for part in left]
        near = self.far(send, 1)
        for part, value in zip(left, sent):
            got[part] = self.across(value)
        (send,) = yield [(total_of([quarter[1], got[1]], 0, 2) + near[2:4].astype(F32)).astype(BF)]
        parts = [quarter[0], got[0], near, self.far(send, 2)]
        (send,) = yield [total_of(parts, 1, 2).astype(BF)]
        parts.append(self.far(send, 4))
        return (yield from self.spread(total_of(parts, 0, 1).astype(BF)))

    def reduce(self, give):
        core, x = self.place % 2, self.place // 2
        give = yield [give[1], give[0], give[2]]
        got = [self.sibling(value) for value in give]
        keep = yield []
        cross, quarter, common = [keep[1], got[0]], [keep[0], got[1]], [keep[2], got[2]]
        (high,) = yield [total_of(cross, 4, 8).astype(BF)]
        high = self.across(high)
        low, send = yield [total_of(cross, 0, 4).astype(BF), total_of(common, 4, 8).astype(BF)]
        low = self.across(low)
        common.append(self.far(send, 1))
        send, other = yield [
            (total_of(quarter, 4, 8) + high.astype(F32)).astype(BF), total_of(common, 2, 4).astype(BF)
        ]
        quarter += [low, self.far(send, 1)]
        common.append(self.far(other, 2))
        send, other = yield [total_of(quarter, 2, 4).astype(BF), total_of(common, 1, 2).astype(BF)]
        quarter.append(self.far(send, 2))
        common.append(self.far(other, 4))
        send, end = yield [total_of(quarter, 1, 2).astype(BF), total_of(common, 0, 1).astype(BF)]
        quarter.append(self.far(send, 4))
        (ends,) = yield [jnp.concatenate([total_of(quarter, 0, 1).astype(BF), end], axis=0)]
        other = self.across(ends)
        shared = (ends[1].astype(F32) + other[1].astype(F32)).astype(BF)
        (mine,) = yield [jnp.stack([ends[0], other[0], shared])]
        theirs = self.sibling(mine)
        columns = []
        first, left = core == 0, x == 0
        for quarter_index in range(4):
            of_core, of_x = divmod(quarter_index, 2)
            near, far = (mine, theirs) if of_core == 0 else (theirs, mine)
            same = jnp.where(first, near[:2], far[:2])
            columns.append(jnp.where(left == (of_x == 0), same[0], same[1]))
        columns.append(jnp.where(first, mine[2], theirs[2]))
        columns.append(jnp.where(first, theirs[2], mine[2]))
        return jnp.concatenate(columns, axis=1)

    def roles(self):
        core, x = self.place % 2, self.place // 2
        return jnp.stack([2 * core + x, 2 * core + 1 - x, 4 + core]).astype(jnp.int32)


def total_of(parts, start, stop):
    summed = 0.0
    for part in parts:
        summed = summed + part[start:stop].astype(F32)
    return summed


def unit_gaps():
    spots = np.arange(SIDE)
    reach = np.arange(SPAN)
    return (spots[None, :, None] - spots[None, None, :] + (SIDE - 1) == reach[:, None, None]).astype(np.float32)


def local(
    mesh,
    tokens,
    condition,
    lengths,
    kept_index,
    heads_weight,
    heads_bias,
    merge_weight,
    merge_bias,
    up_weight,
    up_bias,
    down_weight,
    down_bias,
    modulate_weight,
    modulate_bias,
    relative_table,
    cotangent,
):
    ON_THE_WAY.clear()
    wires = Wires(mesh)
    dp, seq = wires.dp, wires.seq
    samples, count = kept_index.shape[0], tokens.shape[0]
    shard_rows = heads_weight.shape[0]
    everything, half_a, half_b = (0, samples), (0, samples // 2), (samples // 2, samples - samples // 2)
    everyone = (("seq", seq), ("dp", dp))
    line = lambda v: v.astype(F32).reshape(1, -1)
    scal = jnp.concatenate([jnp.stack([wires.me, wires.place]).astype(jnp.int32), lengths])
    in_order = jnp.arange(QUARTERS, dtype=jnp.int32)

    own_cols = lax.dynamic_slice_in_dim(condition, wires.me * shard_rows, shard_rows, 1)
    own_silu = jax.nn.silu(own_cols.astype(F32)).astype(BF)
    partial = dot(own_silu, modulate_weight).reshape(seq, samples, 6 * D)
    mod_chain = Chain(scatter_steps(partial, "seq", seq))
    cond_chain = Chain(gather_steps(own_cols, (("dp", dp),)))
    joint = wires.gather(wires.quarter([heads_weight, merge_weight]))
    up_chain = [Chain(wires.gather_steps(wires.quarter([up_weight])))] if wires.cube else []
    upw = None if wires.cube else wires.gather(wires.quarter([up_weight]))

    index_row = kept_index.reshape(samples, 1, GRID)
    index_col = kept_index.reshape(count, 1)
    inputs = slot((tokens, cotangent, index_row), [cond_chain], slow=up_chain)
    xg, cg, mask = call(
        place_kernel, scal, inputs, [rows_spec(D), rows_spec(D), per_sample(1, GRID)],
        [((count, D), BF, rows_spec(D)), ((count, D), BF, rows_spec(D)), ((samples, 1, GRID), F32, per_sample(1, GRID))],
        [], everything, "place", cost(4 * count * GRID * D, 8 * count * D),
    )
    (later, _) = lax.optimization_barrier((down_weight, mask))
    downw = wires.gather(wires.quarter([later]))

    gaps = unit_gaps()
    turned = relative_table.reshape(HEADS, SPAN, SPAN)[:, ::-1]
    strips = jnp.einsum("hkj,jpq->hpkq", turned, jnp.asarray(gaps, BF), preferred_element_type=F32)
    strips = jnp.pad(strips.reshape(HEADS, SIDE, SPAN * SIDE), ((0, 0), (0, 0), (0, SIDE)))
    inputs = slot((strips,), up_chain + [mod_chain, cond_chain], (mask,))
    (table,) = call(
        bias_kernel, scal, inputs, [per_sample(SIDE, 2 * GRID)], [((HEADS, GRID, GRID), F32, per_sample(GRID, GRID))],
        [], (0, HEADS), "bias", cost(0, 5 << 20),
    )
    (table,) = slot((table,), [mod_chain], slow=up_chain)
    (table,) = slot((table,), [mod_chain])
    modulation = mod_chain.finish().reshape(samples, 6 * D) + modulate_bias.astype(F32)
    mods = modulation.reshape(samples, 6, D)

    full_bias = jnp.concatenate([heads_bias[:D], jnp.zeros((D,), BF), heads_bias[D:]])
    inputs = slot((xg, mods, line(full_bias), joint), slow=up_chain, after=(table,))
    h1, packed = call(
        qkv_kernel, scal, inputs,
        [rows_spec(D), per_sample(6, D), fixed(1, 3 * D), fixed(3, D, D)],
        [((count, D), BF, rows_spec(D)), ((count, 3 * D), BF, rows_spec(3 * D))],
        [], everything, "qkv", cost(2 * count * D * 3 * D, 22 << 20),
    )
    inputs = slot((packed, mask, table))
    attended, lse = call(
        attend_kernel, scal, inputs, [rows_spec(3 * D), per_sample(1, GRID), fixed(HEADS, GRID, GRID)],
        [((count, D), BF, rows_spec(D)), ((count, 128), F32, rows_spec(128))],
        [pltpu.VMEM((GRID, D), F32)], everything, "attend", cost(4 * count * GRID * 256 * HEADS, 15 << 20, count * GRID * HEADS),
    )
    inputs = slot((attended, xg, cg, mods, line(merge_bias), joint), slow=up_chain)
    branch, middle, h2, gm, gm_sum = call(
        merge_kernel, scal, inputs,
        [rows_spec(D), rows_spec(D), rows_spec(D), per_sample(6, D), fixed(1, D), fixed(1, D, D, at=(3, 0, 0))],
        [((count, D), BF, rows_spec(D)), ((count, D), F32, rows_spec(D)), ((count, D), BF, rows_spec(D)),
         ((count, D), BF, rows_spec(D)), ((1, D), F32, fixed(1, D))],
        [], everything, "merge", cost(2 * count * D * D, 20 << 20),
    )

    def pair(values):
        return [[v, wires.sibling(v)] for v in values]

    up_line, sums = line(up_bias), []
    if wires.cube:
        place = wires.place.astype(jnp.int32)
        own_quarters, their_quarters = jnp.stack([place, place ^ 2]), jnp.stack([place ^ 1, place ^ 3])
        order, cross_first = jnp.concatenate([own_quarters, their_quarters]), jnp.array([1, 0], jnp.int32)
        own_pieces, their_pieces = up_chain[0].finish()
        h2, *their_pieces = slot((h2, *their_pieces))
        act_theirs, slope_theirs, up_theirs = up_quarters(h2, up_line, their_pieces, scal, their_quarters, (1, 3))
        h2, *own_pieces = slot((h2, *own_pieces), after=(act_theirs,))
        arrived = wires.sibling(act_theirs)
        gm_pair, h2_pair = pair([gm, h2])
        act_own, slope_own, up_own = up_quarters(h2, up_line, own_pieces, scal, own_quarters, (0, 2))
        acts, upws = [act_own, act_theirs], [up_own, up_theirs]
        act_own, arrived = slot((act_own, arrived))
        tiles = outer_tiles([gm_pair], [act_own, arrived], scal, cross_first, D, 4, ORDER, "down_outer")
        down_sum = Chain(wires.reduce_quarter(tiles[:4], tiles[4:], ((2,), (3,))))
        gm, slope_theirs, downw = slot((gm, slope_theirs, downw), after=(tiles[0],))
        gu_theirs, gu_sum = act_back(gm, slope_theirs, downw, scal, their_quarters, None)
        gm, slope_own, downw, gu_sum = slot((gm, slope_own, downw, gu_sum), [down_sum], (gu_theirs,))
        arrived = wires.sibling(gu_theirs)
        gu_own, gu_sum = act_back(gm, slope_own, downw, scal, own_quarters, gu_sum)
        gu_parts = [gu_own, gu_theirs]
        gu_own, arrived = slot((gu_own, arrived), [down_sum])
        tiles = outer_tiles([h2_pair], [gu_own, arrived], scal, cross_first, D, 4, ORDER, "up_outer")
        up_sum = Chain(wires.reduce_quarter(tiles[:4], tiles[4:], ((2, 3),)))
        sums = [down_sum, up_sum]
        gu_parts = slot(gu_parts, [down_sum], (tiles[0],))
    else:
        order, upws = in_order, [upw]
        act, slope = up_quarters(h2, up_line, upw, scal, in_order, None)
        down_part = wires.scatter(plain_outer([gm], act, scal, "down_outer"))
        gu, gu_sum = act_back(gm, slope, downw, scal, in_order, None)
        up_part = wires.scatter(plain_outer([h2], gu, scal, "up_outer"))
        acts, gu_parts = [act], [gu]

    gmid, gbr, gbr_sum, mid_grads = turned_product(
        gu_parts, scal, order, upws, (middle, branch, cg, mods), [rows_spec(D), rows_spec(D), rows_spec(D), per_sample(6, D)],
        [((count, D), F32, rows_spec(D)), ((count, D), BF, rows_spec(D)), ((1, D), F32, fixed(1, D)), ((samples, 3, D), F32, per_sample(3, D))],
        mid_back_finish, everything, "mid_back",
    )
    mid_all = lax.all_gather(mid_grads.reshape(1, samples * 3, D), ("dp", "seq"), axis=0, tiled=True)
    mid_all = mid_all.astype(BF).reshape(-1, 3 * D)
    def attend_part(chains, after, span):
        inputs = slot((gbr, packed, lse, mask, table, joint), chains, after)
        return call(
            attend_back_kernel, scal, inputs,
            [rows_spec(D), rows_spec(3 * D), rows_spec(128), per_sample(1, GRID), fixed(HEADS, GRID, GRID), fixed(1, D, D, at=(3, 0, 0))],
            [((span[1] * GRID, WIDE), BF, own_rows(WIDE)),
             ((1, 3 * D), F32, fixed(1, 3 * D)), ((HEADS, GRID, GRID), F32, fixed(HEADS, GRID, GRID))],
            [pltpu.VMEM((GRID, D), BF)] + [pltpu.VMEM((GRID, D), F32)] * 3,
            span, "attend_back", cost(count * D * D + 5 * count * GRID * 256 * HEADS, 20 << 20),
        )

    joined_a, joined_sum_a, placed_a = attend_part(sums, (), half_a)
    joined_b, joined_sum_b, placed_b = attend_part(sums, (joined_a,), half_b)
    joined_sum = joined_sum_a + joined_sum_b

    done = joined_b
    if wires.cube:
        lefts, roles = [[h1], [attended]], wires.roles()
        theirs = jnp.stack([roles[0] ^ 2, roles[1] ^ 2, roles[2] ^ 1])
        rights = slot((joined_a, joined_b), slow=sums)
        give = outer_tiles(lefts, rights, scal, theirs, TILE, 1, ORDER, "joint_give")
        joint_sum = Chain(wires.reduce(give))
        rights = slot(rights, [joint_sum], (give[0],), slow=sums[:1])
        keep = outer_tiles(lefts, rights, scal, roles, TILE, 1, ORDER, "joint_keep")
        joint_sum.ready = tuple(keep)
        joint_sum.advance(joint_sum.ready)
        done = keep[0]

    joints = [joint_sum] if wires.cube else []
    placed_a, placed_b = slot((placed_a, placed_b), sums[1:], (done,), slow=joints)
    (strip_grad,) = call(
        strips_kernel, scal, (placed_a, placed_b), [per_sample(GRID, GRID)] * 2,
        [((HEADS, SIDE, 2 * GRID), F32, per_sample(SIDE, 2 * GRID))], [], (0, HEADS), "strips", cost(0, 9 << 20),
    )
    strip_grad = strip_grad[:, :, : SPAN * SIDE].reshape(HEADS, SIDE, SPAN, SIDE)
    table_grad = jnp.einsum(
        "hpkq,jpq->hkj", strip_grad, jnp.asarray(gaps), precision=lax.Precision.HIGHEST
    )[:, ::-1].reshape(-1)
    sizes = [2 * D, D, FF, D, HEADS * SPAN * SPAN]
    loose = jnp.concatenate(
        [joined_sum[0, :D], joined_sum[0, 2 * D :], gbr_sum[0], gu_sum[0], gm_sum[0], table_grad]
    )
    loose = jnp.pad(loose, (0, -loose.shape[0] % 1024)).reshape(-1, 128)
    loose = jnp.sum(lax.all_gather(loose, ("dp", "seq")), axis=0)
    done = strip_grad
    def front_part(own, chains, after, span, prior):
        (own,) = slot((own,), chains, after)
        return turned_product(
            [own], scal, in_order[:3], [joint], (xg, gmid, mods, index_col),
            [rows_spec(D), rows_spec(D), per_sample(6, D), rows_spec(1)],
            [((count, D), F32, rows_spec(D)), ((samples, 2, D), F32, per_sample(2, D))],
            front_back_finish, span, "front_back", prior,
        )

    def down_part_of(chains, after, span, prior, slow=()):
        own = slot(acts, chains, after, slow)
        return turned_product(
            own, scal, order, [downw], (middle, cg, mods, line(down_bias), index_col),
            [rows_spec(D), rows_spec(D), per_sample(6, D), fixed(1, D), rows_spec(1)],
            [((count, D), BF, rows_spec(D)), ((samples, 1, D), F32, per_sample(1, D))],
            down_finish, span, "down", prior,
        )

    output, down_grads = down_part_of([], (done,), half_a, None, joints)
    output, down_grads = down_part_of(joints, (down_grads,), half_b, [output, down_grads])
    tgrad, front_grads = front_part(joined_a, joints + sums, (output,), half_a, None)
    tgrad, front_grads = front_part(joined_b, joints + sums, (front_grads,), half_b, [tgrad, front_grads])

    end_grads = jnp.concatenate([front_grads, down_grads], axis=1).astype(BF).reshape(samples, 3 * D)
    end_chain = Chain(gather_steps(end_grads, everyone))
    if wires.cube:
        for _ in range(2):
            (mid_all,) = slot((mid_all,), [joint_sum, end_chain])
        up_grad, down_grad, joint_grad = up_sum.finish(), down_sum.finish(), joint_sum.finish()
    else:
        up_grad = Chain(wires.spread(up_part)).finish()
        down_grad = Chain(wires.spread(down_part)).finish()
        joint_grad = wires.scatter(plain_outer([h1, attended], jnp.concatenate([joined_a, joined_b]), scal, "joint_outer"))
        joint_grad = Chain(wires.spread(joint_grad)).finish()
    loose = loose.reshape(-1)
    end_all = end_chain.finish()
    mod_all = jnp.concatenate([end_all[:, : 2 * D], mid_all, end_all[:, 2 * D :]], axis=1)
    silu_all = jax.nn.silu(cond_chain.finish().astype(F32)).astype(BF)
    modulate_grad = dot_lt(silu_all, mod_all)
    modulate_total = jnp.sum(mod_all.astype(F32), axis=0)

    edges = np.cumsum([0] + sizes)
    heads_total, merge_total, up_total, down_total, table_total = [
        loose[a:b] for a, b in zip(edges[:-1], edges[1:])
    ]
    return (
        output,
        tgrad,
        joint_grad[:, : 3 * D].astype(F32),
        joint_grad[:, 3 * D :].astype(F32),
        up_grad.astype(F32),
        down_grad.astype(F32),
        modulate_grad,
        heads_total,
        merge_total,
        up_total,
        down_total,
        modulate_total,
        table_total.reshape(HEADS, SPAN * SPAN),
    )


def solution(mesh):
    in_specs = (
        P(("dp", "seq"), None),
        P("dp", None),
        P(("dp", "seq")),
        P(("dp", "seq"), None),
        P("seq", None),
        P(),
        P("seq", None),
        P(),
        P("seq", None),
        P(),
        P("seq", None),
        P(),
        P("seq", None),
        P(),
        P(),
        P(("dp", "seq"), None),
    )
    out_specs = (
        P(("dp", "seq"), None),
        P(("dp", "seq"), None),
        P("seq", None),
        P("seq", None),
        P("seq", None),
        P("seq", None),
        P("seq", None),
        P(),
        P(),
        P(),
        P(),
        P(),
        P(),
    )
    return jax.shard_map(
        functools.partial(local, mesh), mesh=mesh, in_specs=in_specs, out_specs=out_specs, check_vma=False
    )
```

time: 2070 us -> 715 us (0.35)
  waiting for transfers between devices: 1150 us -> 110 us
  local copies, waits for them, and re-layouts: 431 us -> 38.1 us
  Pallas kernels: 0 us -> 349 us
  matrix products: 327 us -> 10.5 us
  starting transfers between devices: 2.45 us -> 48.4 us
    reduce_scatter x1 -> x0, waiting for transfers between devices: 749 us -> none  [local(): lax.psum_scatter(jnp.concatenate(pieces, axis=1).astype(jnp.bfloat16), 's...]
    pallas_call x0 -> x21, Pallas kernels: none -> 349 us  [the longest x8 122 us: call(): pl.pallas_call(body, grid_spec=pltpu.PrefetchScalarGridSpec(num_scalar_pr...]
    dot_general x42 -> x4, matrix products: 327 us -> 10.5 us  [the longest x1 5.62 us: local(): jnp.einsum('hpkq,jpq->hkj', strip_grad, jnp.asarray(gaps), precision=lax....]
    all_gather x6 -> x3, waiting for transfers between devices: 293 us -> 0.01 us  [the longest x2 0.01 us: gather(): lax.all_gather(quarter, ('dp', 'seq'), axis=0, tiled=True)]
    gather x2 -> x0, local copies, waits for them, and re-layouts: 245 us -> none  [local(): jnp.take(relative_table, relative_index(jnp.arange(GRID)), axis=1)]
    ppermute x0 -> x54, waiting for transfers between devices: none -> 110 us  [flip(): lax.ppermute(value, axis, [(i, i ^ bit) for i in range(size)])]
    psum x1 -> x0, waiting for transfers between devices: 109 us -> none  [local(): lax.psum((heads_part, merge_part, up_part, down_part, modulate_part, tabl...]
    all_gather x0 -> x1, blocking collectives: none -> 74.4 us  [local(): lax.all_gather(mid_grads.reshape(1, samples * 3, D), ('dp', 'seq'), axis=...]
  transfers between devices with their start and end apart: 9 -> 57, of which waited for: 6 -> 17; matrix products, arithmetic and copies ran while one was open for 25% -> 13% of each run, Pallas kernels for 0% -> 48%
where the time goes in v1:
time: 715 us; the launch traced here: 702 us
  Pallas kernels  349 us (49%)
  waiting for transfers between devices  110 us (15%)
  blocking collectives  74.4 us (10%)
  other arithmetic  55.6 us (8%)
  starting transfers between devices  48.4 us (7%)
  local copies, waits for them, and re-layouts  38.1 us (5%)
  between operations  15.3 us (2%)
  matrix products  10.5 us (1%)
    pallas_call x8, Pallas kernels, call(): pl.pallas_call(body, grid_spec=pltpu.PrefetchScalarGridSpec(num_scalar_pr...  122 us
    ppermute x54, waiting for transfers between devices, flip(): lax.ppermute(value, axis, [(i, i ^ bit) for i in range(size)])  110 us
    pallas_call x5, Pallas kernels, turned_product(): pl.pallas_call(body, grid_spec=pltpu.PrefetchScalarGridSpec(num_scalar_pr...  98 us
    all_gather x1, blocking collectives, local(): lax.all_gather(mid_grads.reshape(1, samples * 3, D), ('dp', 'seq'), axis=...  74.4 us
    pallas_call x4, Pallas kernels, outer_tiles(): pl.pallas_call(functools.partial(outer_kernel, kinds, sources, width, rol...  70.9 us
    ppermute x54, starting transfers between devices, flip(): lax.ppermute(value, axis, [(i, i ^ bit) for i in range(size)])  48.2 us
    pallas_call x2, Pallas kernels, up_quarters(): pl.pallas_call(functools.partial(up_kernel, count // GRID, gaps), grid_sp...  33.5 us
    pallas_call x2, Pallas kernels, act_back(): pl.pallas_call(functools.partial(act_back_kernel, count // GRID), grid_sp...  25.3 us
  transfers between devices with their start and end apart: 57, of which 17 were waited for; matrix products, arithmetic and copies ran while one was open for 13% of the time, Pallas kernels for 48%

profile of v1, /device:TPU:0, one launch (start us, length us, event | category | flops | bytes accessed | tf_op | source)
XLA Modules:
  0.0 701.9 jit_solution(3793125419105751860)
XLA Ops:
  7.3 1.9 dynamic-slice_select_fusion
  12.4 4.1 collective-permute-start
  17.1 6.5 place.1
  23.6 1.8 constant_dynamic-slice_fusion
  27.1 1.8 convolution_bitcast_fusion
  28.9 4.4 copy.57
  33.3 4.4 reshape.214
  39.6 1.7 collective-permute-start.2
  41.3 10.2 %bias.1.refs_2_.refs_4_ = f32[16,256,256]{2,1,0:T(8,128)} custom-call(s32[6]{0:T(128)} %pad_add_fusion.scal_ref.scal, f32[16,16,512]{2,1,0:T(8,128)} %pad.8.refs_0_), custom_call_target="tpu_custom_call" | custom-call | bytes 5242880 | tf_op jit(solution)/shard_map/bias/pallas_call | solution.py:85
  54.7 21.4 %collective-permute-done.3 = bf16[2,144,1152]{2,1,0:T(8,128)(2,1)S(1)} collective-permute-done((bf16[2,144,1152]{2,1,0:T(8,128)(2,1)S(1)}, bf16[2,144,1152]{2,1,0:T(8,128)(2,1)S(1)}, u32[]{:S(2)}, u32[]{:S(2)}) %collective-permute-start.3) | collective-permute-done | bytes 663584 | tf_op jit(solution)/shard_map/ppermute | solution.py:566
  77.2 13.2 %collective-permute-done.5 = bf16[2,4,6912]{2,1,0:T(4,128)(2,1)S(1)} collective-permute-done((bf16[2,4,6912]{2,1,0:T(4,128)(2,1)S(1)}, bf16[2,4,6912]{2,1,0:T(4,128)(2,1)S(1)}, u32[]{:S(2)}, u32[]{:S(2)}) %collective-permute-start.5) | collective-permute-done | bytes 110624 | tf_op jit(solution)/shard_map/ppermute | solution.py:566
  91.3 1.5 collective-permute-start.7
  94.3 5.6 collective-permute-done.6
  100.7 25.5 %collective-permute-done.7.refs_1_ = bf16[4,144,1152]{2,1,0:T(8,128)(2,1)} collective-permute-done((bf16[4,144,1152]{2,1,0:T(8,128)(2,1)S(1)}, bf16[4,144,1152]{2,1,0:T(8,128)(2,1)}, u32[]{:S(2)}, u32[]{:S(2)}) %collective-permute-start.7) | collective-permute-done | bytes 1327136 | tf_op jit(solution)/shard_map/ppermute | solution.py:566
  128.8 17.6 %qkv.1 = (bf16[1024,1152]{1,0:T(8,128)(2,1)}, bf16[1024,3456]{1,0:T(8,128)(2,1)}) custom-call(s32[6]{0:T(128)} %pad_add_fusion.scal_ref.scal, bf16[1024,1152]{1,0:T(8,128)(2,1)} %get-tuple-element.223.refs_0_.refs_1_.refs_2_, f32[4,6,1152]{2,1,0:T(8,128)} %broadcast_add_fusion.refs_1_.refs_3_.refs_7_.refs_5_.refs_4_, f32[1,3456]{1,0:T(1,128)} %fusion.31.refs_2_, ...), custom_call_target="tpu_custom_call" | custom-call | flops 8153726976 | bytes 23068672 | tf_op jit(solution)/shard_map/qkv/pallas_call | solution.py:85
  146.4 15.6 %attend.1 = (bf16[1024,1152]{1,0:T(8,128)(2,1)}, f32[1024,128]{1,0:T(8,128)}) custom-call(s32[6]{0:T(128)} %pad_add_fusion.scal_ref.scal, bf16[1024,3456]{1,0:T(8,128)(2,1)} %get-tuple-element.302.refs_0_.refs_1_, f32[4,1,256]{2,1,0:T(1,128)} %get-tuple-element.304.refs_1_.refs_3_, f32[16,256,256]{2,1,0:T(8,128)} %bias.1.refs_2_.refs_4_), custom_call_target="tpu_custom_call" | custom-call | flops 4294967296 | bytes 15728640 | tf_op jit(solution)/shard_map/attend/pallas_call | solution.py:85
  162.0 6.6 collective-permute-done.9.refs_3_
  170.1 11.6 %merge.1 = (bf16[1024,1152]{1,0:T(8,128)(2,1)}, f32[1024,1152]{1,0:T(8,128)}, bf16[1024,1152]{1,0:T(8,128)(2,1)}, bf16[1024,1152]{1,0:T(8,128)(2,1)}, f32[1,1152]{1,0:T(1,128)}) custom-call(s32[6]{0:T(128)} %pad_add_fusion.scal_ref.scal, bf16[1024,1152]{1,0:T(8,128)(2,1)} %get-tuple-element.222.refs_0_.refs_2_.refs_3_, ...), custom_call_target="tpu_custom_call" | custom-call | flops 2717908992 | bytes 20971520 | tf_op jit(solution)/shard_map/merge/pallas_call | solution.py:85
  182.9 16.9 %up.2 = (bf16[2,1024,1152]{2,1,0:T(8,128)(2,1)}, bf16[2,1024,1152]{2,1,0:T(8,128)(2,1)}, bf16[2,1152,1152]{2,1,0:T(8,128)(2,1)}) custom-call(s32[6]{0:T(128)} %pad_add_fusion.scal_ref.scal, s32[2]{0:T(128)} %pad_add_fusion.3.quarters, bf16[1024,1152]{1,0:T(8,128)(2,1)} %get-tuple-element.239.h2.refs_0_, f32[1,4608]{1,0:T(1,128)} %reshape.237.bias, ...), custom_call_target="tpu_custom_call" | custom-call | flops 5435817984 | bytes 24772608 | tf_op jit(solution)/shard_map/up/pallas_call | solution.py:270
  201.3 16.7 %up.3 = (bf16[2,1024,1152]{2,1,0:T(8,128)(2,1)}, bf16[2,1024,1152]{2,1,0:T(8,128)(2,1)}, bf16[2,1152,1152]{2,1,0:T(8,128)(2,1)}) custom-call(s32[6]{0:T(128)} %pad_add_fusion.scal_ref.scal, s32[2]{0:T(128)} %pad_add_fusion.2.quarters, bf16[1024,1152]{1,0:T(8,128)(2,1)} %get-tuple-element.239.h2.refs_0_, f32[1,4608]{1,0:T(1,128)} %reshape.237.bias, ...), custom_call_target="tpu_custom_call" | custom-call | flops 5435817984 | bytes 24772608 | tf_op jit(solution)/shard_map/up/pallas_call | solution.py:270
  218.6 20.1 %down_outer.1 = (bf16[2,144,1152]{2,1,0:T(8,128)(2,1)}, bf16[2,144,1152]{2,1,0:T(8,128)(2,1)}, bf16[2,144,1152]{2,1,0:T(8,128)(2,1)}, bf16[2,144,1152]{2,1,0:T(8...) custom-call(s32[6]{0:T(128)} %pad_add_fusion.scal_ref.scal, ...), custom_call_target="tpu_custom_call" | custom-call | flops 10871635968 | bytes 14155776 | tf_op jit(solution)/shard_map/down_outer/pallas_call | solution.py:544
  238.8 12.7 %act_back.2 = (bf16[2,1024,1152]{2,1,0:T(8,128)(2,1)}, f32[1,4608]{1,0:T(1,128)}) custom-call(s32[6]{0:T(128)} %pad_add_fusion.scal_ref.scal, s32[2]{0:T(128)} %pad_add_fusion.3.quarters, bf16[1024,1152]{1,0:T(8,128)(2,1)} %get-tuple-element.259.refs_0_.gm, bf16[2,1024,1152]{2,1,0:T(8,128)(2,1)} %get-tuple-element.255.slope, bf16[4,1152,1152]{2,1,0:T(8,128)(2,1)} %bitcast.137), custom_call_target="tpu_custom_call" | custom-call | flops 5435817984 | bytes 14745600 | tf_op jit(solution)/shard_map/act_back/pallas_call | solution.py:301
  255.4 12.6 %act_back.3 = (bf16[2,1024,1152]{2,1,0:T(8,128)(2,1)}, f32[1,4608]{1,0:T(1,128)}) custom-call(s32[6]{0:T(128)} %pad_add_fusion.scal_ref.scal, s32[2]{0:T(128)} %pad_add_fusion.2.quarters, bf16[1024,1152]{1,0:T(8,128)(2,1)} %get-tuple-element.259.refs_0_.gm, bf16[2,1024,1152]{2,1,0:T(8,128)(2,1)} %get-tuple-element.260.slope, ...), custom_call_target="tpu_custom_call", output_to_operand_aliasing={{1}: (5, {})} | custom-call | flops 5435817984 | bytes 14745600 | tf_op jit(solution)/shard_map/act_back/pallas_call | solution.py:301
  270.6 20.3 %up_outer.1 = (bf16[2,144,1152]{2,1,0:T(8,128)(2,1)}, bf16[2,144,1152]{2,1,0:T(8,128)(2,1)}, bf16[2,144,1152]{2,1,0:T(8,128)(2,1)}, bf16[2,144,1152]{2,1,0:T(8,1...) custom-call(s32[6]{0:T(128)} %pad_add_fusion.scal_ref.scal, ...), custom_call_target="tpu_custom_call" | custom-call | flops 10871635968 | bytes 14155776 | tf_op jit(solution)/shard_map/up_outer/pallas_call | solution.py:544
  295.9 33.6 %mid_back.1 = (f32[1024,1152]{1,0:T(8,128)}, bf16[1024,1152]{1,0:T(8,128)(2,1)}, f32[1,1152]{1,0:T(1,128)}, f32[4,3,1152]{2,1,0:T(4,128)}) custom-call(s32[6]{0:T(128)} %pad_add_fusion.scal_ref.scal, s32[4]{0:T(128)} %pad_add_fusion.1.quarters_ref, bf16[2,1024,1152]{2,1,0:T(8,128)(2,1)} %get-tuple-element.273.refs_2_.refs_0_, ...), custom_call_target="tpu_custom_call" | custom-call | flops 10871635968 | bytes 31850496 | tf_op jit(solution)/shard_map/mid_back/pallas_call | solution.py:373
  329.5 1.5 reshape.228
  331.0 2.7 add_convert_fusion.7
  334.4 74.4 %all_gather.14 = bf16[32,12,1152]{2,1,0:T(8,128)(2,1)S(1)} all-gather(bf16[1,12,1152]{2,1,0:T(8,128)(2,1)S(1)} %copy-done.19), channel_id=1, replica_groups=mesh['dp'=4,'seq'=8] {'dp','seq'}, dimensions={0}, use_global_device_ids=true | all-gather | bytes 912384 | tf_op jit(solution)/shard_map/all_gather | solution.py:877
  410.4 24.1 %attend_back.2 = (bf16[512,4608]{1,0:T(8,128)(2,1)}, f32[1,3456]{1,0:T(1,128)}, f32[16,256,256]{2,1,0:T(8,128)}) custom-call(s32[6]{0:T(128)} %pad_add_fusion.scal_ref.scal, bf16[1024,1152]{1,0:T(8,128)(2,1)} %get-tuple-element.301.refs_0_, bf16[1024,3456]{1,0:T(8,128)(2,1)} %get-tuple-element.302.refs_0_.refs_1_, f32[1024,128]{1,0:T(8,128)} %get-tuple-element.303.refs_2_, ...), custom_call_target="tpu_custom_call" | custom-call | flops 6727663616 | bytes 20971520 | tf_op jit(solution)/shard_map/attend_back/pallas_call | solution.py:85
  441.6 24.2 %attend_back.3 = (bf16[512,4608]{1,0:T(8,128)(2,1)}, f32[1,3456]{1,0:T(1,128)}, f32[16,256,256]{2,1,0:T(8,128)}) custom-call(s32[6]{0:T(128)} %pad_add_fusion.scal_ref.scal, bf16[1024,1152]{1,0:T(8,128)(2,1)} %get-tuple-element.301.refs_0_, bf16[1024,3456]{1,0:T(8,128)(2,1)} %get-tuple-element.302.refs_0_.refs_1_, f32[1024,128]{1,0:T(8,128)} %get-tuple-element.303.refs_2_, ...), custom_call_target="tpu_custom_call" | custom-call | flops 6727663616 | bytes 20971520 | tf_op jit(solution)/shard_map/attend_back/pallas_call | solution.py:85
  473.2 1.5 add_convert_fusion.14
  474.8 2.7 add_convert_fusion.4
  477.5 1.9 collective-permute-start.32
  479.4 15.3 %joint_give.1 = (bf16[8,144,768]{2,1,0:T(8,128)(2,1)}, bf16[8,144,768]{2,1,0:T(8,128)(2,1)}, bf16[8,144,768]{2,1,0:T(8,128)(2,1)}) custom-call(s32[6]{0:T(128)} %pad_add_fusion.scal_ref.scal, s32[3]{0:T(128)} %get-tuple-element.416.blocks, bf16[1024,1152]{1,0:T(8,128)(2,1)} %get-tuple-element.245.refs_0_.refs_1_, ...), custom_call_target="tpu_custom_call" | custom-call | flops 5435817984 | bytes 9437184 | tf_op jit(solution)/shard_map/joint_give/pallas_call | solution.py:544
  497.3 15.1 %joint_keep.1 = (bf16[8,144,768]{2,1,0:T(8,128)(2,1)}, bf16[8,144,768]{2,1,0:T(8,128)(2,1)}, bf16[8,144,768]{2,1,0:T(8,128)(2,1)}) custom-call(s32[6]{0:T(128)} %pad_add_fusion.scal_ref.scal, s32[3]{0:T(128)} %get-tuple-element.415.blocks, bf16[1024,1152]{1,0:T(8,128)(2,1)} %get-tuple-element.245.refs_0_.refs_1_, ...), custom_call_target="tpu_custom_call" | custom-call | flops 5435817984 | bytes 9437184 | tf_op jit(solution)/shard_map/joint_keep/pallas_call | solution.py:544
  512.4 2.0 add_convert_fusion.13
  515.7 1.8 maximum_convert_fusion.1
  517.8 3.1 add_convert_fusion.1
  521.7 11.8 %strips.1 = f32[16,16,512]{2,1,0:T(8,128)} custom-call(s32[6]{0:T(128)} %pad_add_fusion.scal_ref.scal, f32[16,256,256]{2,1,0:T(8,128)} %get-tuple-element.332.refs_0_, f32[16,256,256]{2,1,0:T(8,128)} %get-tuple-element.333.refs_1_), custom_call_target="tpu_custom_call" | custom-call | bytes 9437184 | tf_op jit(solution)/shard_map/strips/pallas_call | solution.py:85
  533.5 4.1 reshape.224
  537.5 2.9 collective-permute-start.36
  540.5 5.6 convolution_bitcast_fusion.1
  546.4 2.3 add_convert_fusion
  548.7 6.2 collective-permute-done.36
  554.9 2.0 collective-permute-start.37
  558.9 17.0 %down.2 = (bf16[1024,1152]{1,0:T(8,128)(2,1)}, f32[4,1,1152]{2,1,0:T(1,128)}) custom-call(s32[6]{0:T(128)} %pad_add_fusion.scal_ref.scal, s32[4]{0:T(128)} %pad_add_fusion.1.quarters_ref, bf16[2,1024,1152]{2,1,0:T(8,128)(2,1)} %get-tuple-element.339.refs_2_.refs_0_, bf16[2,1024,1152]{2,1,0:T(8,128)(2,1)} %get-tuple-element.340.refs_1_, ...), custom_call_target="tpu_custom_call" | custom-call | flops 5435817984 | bytes 21233664 | tf_op jit(solution)/shard_map/down/pallas_call | solution.py:373
  575.9 2.7 add_convert_fusion.2
  578.7 1.5 add_convert_fusion.11
  582.6 17.1 %down.3 = (bf16[1024,1152]{1,0:T(8,128)(2,1)}, f32[4,1,1152]{2,1,0:T(1,128)}) custom-call(s32[6]{0:T(128)} %pad_add_fusion.scal_ref.scal, s32[4]{0:T(128)} %pad_add_fusion.1.quarters_ref, bf16[2,1024,1152]{2,1,0:T(8,128)(2,1)} %get-tuple-element.339.refs_2_.refs_0_, ...), custom_call_target="tpu_custom_call", output_to_operand_aliasing={{0}: (10, {}), {1}: (11, {})} | custom-call | flops 5435817984 | bytes 21233664 | tf_op jit(solution)/shard_map/down/pallas_call | solution.py:373
  601.9 2.3 collective-permute-done.39
  604.2 2.3 add_convert_fusion.10
  607.7 15.1 %front_back.2 = (f32[1024,1152]{1,0:T(8,128)}, f32[4,2,1152]{2,1,0:T(2,128)}) custom-call(s32[6]{0:T(128)} %pad_add_fusion.scal_ref.scal, s32[3]{0:T(128)} %bitcast.153, bf16[512,4608]{1,0:T(8,128)(2,1)} %get-tuple-element.349.refs_4_.refs_0_, bf16[4,1152,1152]{2,1,0:T(8,128)(2,1)} %bitcast.135, ...), custom_call_target="tpu_custom_call" | custom-call | flops 4076863488 | bytes 17399808 | tf_op jit(solution)/shard_map/front_back/pallas_call | solution.py:373
  622.7 1.9 collective-permute-done.42
  627.9 3.2 collective-permute-start.44
  632.1 15.3 %front_back.3 = (f32[1024,1152]{1,0:T(8,128)}, f32[4,2,1152]{2,1,0:T(2,128)}) custom-call(s32[6]{0:T(128)} %pad_add_fusion.scal_ref.scal, s32[3]{0:T(128)} %bitcast.154, bf16[512,4608]{1,0:T(8,128)(2,1)} %get-tuple-element.352.refs_5_.refs_0_, bf16[4,1152,1152]{2,1,0:T(8,128)(2,1)} %bitcast.136, ...), custom_call_target="tpu_custom_call", output_to_operand_aliasing={{0}: (8, {}), {1}: (9, {})} | custom-call | flops 4076863488 | bytes 17399808 | tf_op jit(solution)/shard_map/front_back/pallas_call | solution.py:373
  652.1 2.6 collective-permute-done.47
  654.8 5.6 collective-permute-done.46
  661.3 3.6 collective-permute-done.50
  664.9 1.5 collective-permute-start.51
  666.4 5.3 collective-permute-done.51
  671.9 1.8 maximum_convert_fusion
  678.6 7.8 %collective-permute-done.53 = bf16[64,3456]{1,0:T(8,128)(2,1)S(1)} collective-permute-done((bf16[64,3456]{1,0:T(8,128)(2,1)S(1)}, bf16[64,3456]{1,0:T(8,128)(2,1)S(1)}, u32[]{:S(2)}, u32[]{:S(2)}) %collective-permute-start.53) | collective-permute-done | bytes 442400 | tf_op jit(solution)/shard_map/ppermute | solution.py:566
  686.7 2.7 fusion.16
  690.3 2.1 reduce_sum.18
  (289 shorter events, 81.5 us)
Async XLA Ops:
  7.2 119.0 %all-gather.8.cloned.1.call-start = ((), (), s32[]{:S(2)}) async-start(), calls=%async_computation.1 | async-start | bytes 10948608 | tf_op jit(solution)/shard_map/all_gather | solution.py:651
  9.2 229.6 %all-gather.10.cloned.1.call-start = ((), (), s32[]{:S(2)}) async-start(), calls=%async_computation.2 | async-start | bytes 10948608 | tf_op jit(solution)/shard_map/all_gather | solution.py:651
  12.4 26.2 %collective-permute-start = (bf16[1,144,1152]{2,1,0:T(8,128)(2,1)S(1)}, bf16[1,144,1152]{2,1,0:T(8,128)(2,1)}, u32[]{:S(2)}, u32[]{:S(2)}) collective-permute-start(bf16[1,144,1152]{2,1,0:T(8,128)(2,1)S(1)} %dynamic-slice_bitcast_fusion), channel_id=1, source_target_pairs={{0,4},{1,5},{2,6},{3,7},{4,0},{5,1},{6,2},{7,3},{8,12},{9,13},{10,... | collective-permute-start | bytes 995336 | tf_op jit(solution)/shard_map/ppermute | solution.py:566
  16.5 22.1 %collective-permute-start.1 = (bf16[32,144]{1,0:T(8,128)(2,1)S(1)}, bf16[32,144]{1,0:T(8,128)(2,1)S(1)}, u32[]{:S(2)}, u32[]{:S(2)}) collective-permute-start(bf16[32,144]{1,0:T(8,128)(2,1)S(1)} %constant_dynamic-slice_fusion.1), channel_id=1, source_target_pairs={{0,8},{8,0},{16,24},{24,16},{1,9},{9,1},{17,25},{25,17},{2,10},{10... | collective-permute-start | bytes 27656 | tf_op jit(solution)/shard_map/ppermute | solution.py:566
  25.4 664.9 %all-gather.6.cloned.1.call-start = ((), (), s32[]{:S(2)}) async-start(), calls=%async_computation | async-start | bytes 3379200 | tf_op jit(solution)/shard_map/all_gather | solution.py:922
  39.6 14.8 %collective-permute-start.2 = (bf16[4,4,6912]{2,1,0:T(4,128)(2,1)S(1)}, bf16[4,4,6912]{2,1,0:T(4,128)(2,1)S(1)}, u32[]{:S(2)}, u32[]{:S(2)}) collective-permute-start(bf16[4,4,6912]{2,1,0:T(4,128)(2,1)S(1)} %fusion.6), channel_id=1, source_target_pairs={{0,1},{1,0},{2,3},{3,2},{4,5},{5,4},{6,7},{7,6},{8,9},{9,8},{10,11... | collective-permute-start | bytes 663560 | tf_op jit(solution)/shard_map/ppermute | solution.py:566
  51.5 24.6 %collective-permute-start.3 = (bf16[2,144,1152]{2,1,0:T(8,128)(2,1)S(1)}, bf16[2,144,1152]{2,1,0:T(8,128)(2,1)S(1)}, u32[]{:S(2)}, u32[]{:S(2)}) collective-permute-start(bf16[2,144,1152]{2,1,0:T(8,128)(2,1)S(1)} %pad_maximum_fusion.3), channel_id=1, source_target_pairs={{0,2},{1,3},{2,0},{3,1},{4,6},{5,7},{6,4},{7,5},{8,10},{9,11},{10,... | collective-permute-start | bytes 1990664 | tf_op jit(solution)/shard_map/ppermute | solution.py:566
  53.0 23.3 %collective-permute-start.4 = (bf16[64,144]{1,0:T(8,128)(2,1)S(1)}, bf16[64,144]{1,0:T(8,128)(2,1)S(1)}, u32[]{:S(2)}, u32[]{:S(2)}) collective-permute-start(bf16[64,144]{1,0:T(8,128)(2,1)S(1)} %pad_maximum_fusion.13), channel_id=1, source_target_pairs={{0,16},{8,24},{16,0},{24,8},{1,17},{9,25},{17,1},{25,9},{2,18},{10... | collective-permute-start | bytes 55304 | tf_op jit(solution)/shard_map/ppermute | solution.py:566
  54.7 36.6 %copy-start.29 = (bf16[6912]{0:T(1024)(128)(2,1)S(1)}, bf16[6912]{0:T(1024)(128)(2,1)}, u32[]{:S(2)}) copy-start(bf16[6912]{0:T(1024)(128)(2,1)} %param.32) | copy-start | bytes 41476
  54.7 73.5 %copy-start.35 = (bf16[1152]{0:T(1024)(128)(2,1)S(1)}, bf16[1152]{0:T(1024)(128)(2,1)}, u32[]{:S(2)}) copy-start(bf16[1152]{0:T(1024)(128)(2,1)} %param.26) | copy-start | bytes 6916
  76.2 70.2 %copy-start.5 = (bf16[4,144,1152]{2,1,0:T(8,128)(2,1)}, bf16[4,144,1152]{2,1,0:T(8,128)(2,1)S(1)}, u32[]{:S(2)}) copy-start(bf16[4,144,1152]{2,1,0:T(8,128)(2,1)S(1)} %pad_maximum_fusion.refs_0_) | copy-start | bytes 3981316
  76.3 14.1 %collective-permute-start.5 = (bf16[2,4,6912]{2,1,0:T(4,128)(2,1)S(1)}, bf16[2,4,6912]{2,1,0:T(4,128)(2,1)S(1)}, u32[]{:S(2)}, u32[]{:S(2)}) collective-permute-start(bf16[2,4,6912]{2,1,0:T(4,128)(2,1)S(1)} %fusion.15), channel_id=1, source_target_pairs={{0,2},{1,3},{2,0},{3,1},{4,6},{5,7},{6,4},{7,5},{8,10},{9,11},{10,... | collective-permute-start | bytes 331784 | tf_op jit(solution)/shard_map/ppermute | solution.py:566
  90.5 9.4 %collective-permute-start.6 = (bf16[1,4,6912]{2,1,0:T(4,128)(2,1)S(1)}, bf16[1,4,6912]{2,1,0:T(4,128)(2,1)S(1)}, u32[]{:S(2)}, u32[]{:S(2)}) collective-permute-start(bf16[1,4,6912]{2,1,0:T(4,128)(2,1)S(1)} %fusion.22), channel_id=1, source_target_pairs={{0,4},{1,5},{2,6},{3,7},{4,0},{5,1},{6,2},{7,3},{8,12},{9,13},{10,... | collective-permute-start | bytes 165896 | tf_op jit(solution)/shard_map/ppermute | solution.py:566
  91.3 35.0 %collective-permute-start.7 = (bf16[4,144,1152]{2,1,0:T(8,128)(2,1)S(1)}, bf16[4,144,1152]{2,1,0:T(8,128)(2,1)}, u32[]{:S(2)}, u32[]{:S(2)}) collective-permute-start(bf16[4,144,1152]{2,1,0:T(8,128)(2,1)S(1)} %pad_maximum_fusion.refs_0_), channel_id=1, source_target_pairs={{0,1},{1,0},{2,3},{3,2},{4,5},{5,4},{6,7},{7,6},{8,9},{9,8},{10,11... | collective-permute-start | bytes 3981320 | tf_op jit(solution)/shard_map/ppermute | solution.py:566
  92.8 33.4 %collective-permute-start.8 = (bf16[4,144,1152]{2,1,0:T(8,128)(2,1)S(1)}, bf16[4,144,1152]{2,1,0:T(8,128)(2,1)}, u32[]{:S(2)}, u32[]{:S(2)}) collective-permute-start(bf16[4,144,1152]{2,1,0:T(8,128)(2,1)S(1)} %pad_maximum_fusion.refs_0_), channel_id=1, source_target_pairs={{0,16},{8,24},{16,0},{24,8},{1,17},{9,25},{17,1},{25,9},{2,18},{10... | collective-permute-start | bytes 3981320 | tf_op jit(solution)/shard_map/ppermute | solution.py:566
  126.2 42.4 %collective-permute-start.9 = (bf16[4,144,1152]{2,1,0:T(8,128)(2,1)}, bf16[4,144,1152]{2,1,0:T(8,128)(2,1)S(1)}, u32[]{:S(2)}, u32[]{:S(2)}) collective-permute-start(bf16[4,144,1152]{2,1,0:T(8,128)(2,1)} %collective-permute-done.7.refs_1_), channel_id=1, source_target_pairs={{0,16},{8,24},{16,0},{24,8},{1,17},{9,25},{17,1},{25,9},{2,18},{10... | collective-permute-start | bytes 3981320 | tf_op jit(solution)/shard_map/ppermute | solution.py:566
  127.7 40.9 %collective-permute-start.11 = (bf16[4,144,1152]{2,1,0:T(8,128)(2,1)}, bf16[4,144,1152]{2,1,0:T(8,128)(2,1)}, u32[]{:S(2)}, u32[]{:S(2)}) collective-permute-start(bf16[4,144,1152]{2,1,0:T(8,128)(2,1)} %collective-permute-done.7.refs_1_), channel_id=1, source_target_pairs={{0,8},{8,0},{16,24},{24,16},{1,9},{9,1},{17,25},{25,17},{2,10},{10... | collective-permute-start | bytes 3981320 | tf_op jit(solution)/shard_map/ppermute | solution.py:566
  127.7 40.9 %collective-permute-start.10 = (bf16[4,144,1152]{2,1,0:T(8,128)(2,1)S(1)}, bf16[4,144,1152]{2,1,0:T(8,128)(2,1)}, u32[]{:S(2)}, u32[]{:S(2)}) collective-permute-start(bf16[4,144,1152]{2,1,0:T(8,128)(2,1)S(1)} %pad_maximum_fusion.refs_0_), channel_id=1, source_target_pairs={{0,8},{8,0},{16,24},{24,16},{1,9},{9,1},{17,25},{25,17},{2,10},{10... | collective-permute-start | bytes 3981320 | tf_op jit(solution)/shard_map/ppermute | solution.py:566
  128.2 40.4 %collective-permute-start.12 = (bf16[4,144,1152]{2,1,0:T(8,128)(2,1)}, bf16[4,144,1152]{2,1,0:T(8,128)(2,1)}, u32[]{:S(2)}, u32[]{:S(2)}) collective-permute-start(bf16[4,144,1152]{2,1,0:T(8,128)(2,1)} %collective-permute-done.8.refs_2_), channel_id=1, source_target_pairs={{0,8},{8,0},{16,24},{24,16},{1,9},{9,1},{17,25},{25,17},{2,10},{10... | collective-permute-start | bytes 3981320 | tf_op jit(solution)/shard_map/ppermute | solution.py:566
  168.7 13.1 %collective-permute-start.13 = (bf16[4,144,1152]{2,1,0:T(8,128)(2,1)S(1)}, bf16[4,144,1152]{2,1,0:T(8,128)(2,1)S(1)}, u32[]{:S(2)}, u32[]{:S(2)}) collective-permute-start(bf16[4,144,1152]{2,1,0:T(8,128)(2,1)S(1)} %collective-permute-done.9.refs_3_), channel_id=1, source_target_pairs={{0,8},{8,0},{16,24},{24,16},{1,9},{9,1},{17,25},{25,17},{2,10},{10... | collective-permute-start | bytes 3981320 | tf_op jit(solution)/shard_map/ppermute | solution.py:566
  199.7 18.9 %collective-permute-start.15 = (bf16[2,1024,1152]{2,1,0:T(8,128)(2,1)}, bf16[2,1024,1152]{2,1,0:T(8,128)(2,1)}, u32[]{:S(2)}, u32[]{:S(2)}) collective-permute-start(bf16[2,1024,1152]{2,1,0:T(8,128)(2,1)} %get-tuple-element.340.refs_1_), channel_id=1, source_target_pairs={{0,8},{8,0},{16,24},{24,16},{1,9},{9,1},{17,25},{25,17},{2,10},{10... | collective-permute-start | bytes 14155784 | tf_op jit(solution)/shard_map/ppermute | solution.py:566
  200.2 17.8 %collective-permute-start.14 = (bf16[1024,1152]{1,0:T(8,128)(2,1)}, bf16[1024,1152]{1,0:T(8,128)(2,1)}, u32[]{:S(2)}, u32[]{:S(2)}) collective-permute-start(bf16[1024,1152]{1,0:T(8,128)(2,1)} %get-tuple-element.259.refs_0_.gm), channel_id=1, source_target_pairs={{0,8},{8,0},{16,24},{24,16},{1,9},{9,1},{17,25},{25,17},{2,10},{10... | collective-permute-start | bytes 7077896 | tf_op jit(solution)/shard_map/ppermute | solution.py:566
  200.3 18.3 %collective-permute-start.16 = (bf16[1024,1152]{1,0:T(8,128)(2,1)}, bf16[1024,1152]{1,0:T(8,128)(2,1)}, u32[]{:S(2)}, u32[]{:S(2)}) collective-permute-start(bf16[1024,1152]{1,0:T(8,128)(2,1)} %get-tuple-element.239.h2.refs_0_), channel_id=1, source_target_pairs={{0,8},{8,0},{16,24},{24,16},{1,9},{9,1},{17,25},{25,17},{2,10},{10... | collective-permute-start | bytes 7077896 | tf_op jit(solution)/shard_map/ppermute | solution.py:566
  251.4 17.7 %collective-permute-start.18 = (bf16[2,1024,1152]{2,1,0:T(8,128)(2,1)}, bf16[2,1024,1152]{2,1,0:T(8,128)(2,1)}, u32[]{:S(2)}, u32[]{:S(2)}) collective-permute-start(bf16[2,1024,1152]{2,1,0:T(8,128)(2,1)} %get-tuple-element.274.refs_1_), channel_id=1, source_target_pairs={{0,8},{8,0},{16,24},{24,16},{1,9},{9,1},{17,25},{25,17},{2,10},{10... | collective-permute-start | bytes 14155784 | tf_op jit(solution)/shard_map/ppermute | solution.py:566
  251.8 17.2 %collective-permute-start.17 = (bf16[2,144,1152]{2,1,0:T(8,128)(2,1)}, bf16[2,144,1152]{2,1,0:T(8,128)(2,1)S(1)}, u32[]{:S(2)}, u32[]{:S(2)}) collective-permute-start(bf16[2,144,1152]{2,1,0:T(8,128)(2,1)} %get-tuple-element.265), channel_id=1, source_target_pairs={{0,16},{8,24},{16,0},{24,8},{1,17},{9,25},{17,1},{25,9},{2,18},{10... | collective-permute-start | bytes 1990664 | tf_op jit(solution)/shard_map/ppermute | solution.py:566
  269.2 21.7 %collective-permute-start.19 = (bf16[2,144,1152]{2,1,0:T(8,128)(2,1)S(1)}, bf16[2,144,1152]{2,1,0:T(8,128)(2,1)S(1)}, u32[]{:S(2)}, u32[]{:S(2)}) collective-permute-start(bf16[2,144,1152]{2,1,0:T(8,128)(2,1)S(1)} %copy-done.40), channel_id=1, source_target_pairs={{0,16},{8,24},{16,0},{24,8},{1,17},{9,25},{17,1},{25,9},{2,18},{10... | collective-permute-start | bytes 1990664 | tf_op jit(solution)/shard_map/ppermute | solution.py:566
  291.3 39.7 %collective-permute-start.21 = (bf16[4,144,1152]{2,1,0:T(8,128)(2,1)S(1)}, bf16[4,144,1152]{2,1,0:T(8,128)(2,1)S(1)}, u32[]{:S(2)}, u32[]{:S(2)}) collective-permute-start(bf16[4,144,1152]{2,1,0:T(8,128)(2,1)S(1)} %pad_maximum_fusion.1), channel_id=1, source_target_pairs={{0,1},{1,0},{2,3},{3,2},{4,5},{5,4},{6,7},{7,6},{8,9},{9,8},{10,11... | collective-permute-start | bytes 3981320 | tf_op jit(solution)/shard_map/ppermute | solution.py:566
  293.8 37.2 %collective-permute-start.20 = (bf16[2,144,1152]{2,1,0:T(8,128)(2,1)}, bf16[2,144,1152]{2,1,0:T(8,128)(2,1)}, u32[]{:S(2)}, u32[]{:S(2)}) collective-permute-start(bf16[2,144,1152]{2,1,0:T(8,128)(2,1)} %get-tuple-element.282), channel_id=1, source_target_pairs={{0,16},{8,24},{16,0},{24,8},{1,17},{9,25},{17,1},{25,9},{2,18},{10... | collective-permute-start | bytes 1990664 | tf_op jit(solution)/shard_map/ppermute | solution.py:566
  294.4 39.3 %collective-permute-start.22 = (bf16[2,144,1152]{2,1,0:T(8,128)(2,1)}, bf16[2,144,1152]{2,1,0:T(8,128)(2,1)}, u32[]{:S(2)}, u32[]{:S(2)}) collective-permute-start(bf16[2,144,1152]{2,1,0:T(8,128)(2,1)} %get-tuple-element.286), channel_id=1, source_target_pairs={{0,16},{8,24},{16,0},{24,8},{1,17},{9,25},{17,1},{25,9},{2,18},{10... | collective-permute-start | bytes 1990664 | tf_op jit(solution)/shard_map/ppermute | solution.py:566
  295.9 35.2 %copy-start.13 = (bf16[2,144,1152]{2,1,0:T(8,128)(2,1)S(1)}, bf16[2,144,1152]{2,1,0:T(8,128)(2,1)}, u32[]{:S(2)}) copy-start(bf16[2,144,1152]{2,1,0:T(8,128)(2,1)} %get-tuple-element.281) | copy-start | bytes 1990660
  333.7 75.7 %copy-start.34 = (f32[1,1152]{1,0:T(1,128)S(1)}, f32[1,1152]{1,0:T(1,128)}, u32[]{:S(2)}) copy-start(f32[1,1152]{1,0:T(1,128)} %get-tuple-element.370) | copy-start | bytes 13828
  333.7 100.8 %collective-permute-start.25 = (bf16[2,144,1152]{2,1,0:T(8,128)(2,1)}, bf16[2,144,1152]{2,1,0:T(8,128)(2,1)S(1)}, u32[]{:S(2)}, u32[]{:S(2)}) collective-permute-start(bf16[2,144,1152]{2,1,0:T(8,128)(2,1)} %get-tuple-element.299), channel_id=1, source_target_pairs={{0,16},{8,24},{16,0},{24,8},{1,17},{9,25},{17,1},{25,9},{2,18},{10... | collective-permute-start | bytes 1990664 | tf_op jit(solution)/shard_map/ppermute | solution.py:566
  409.4 28.6 %collective-permute-start.23 = (bf16[2,144,1152]{2,1,0:T(8,128)(2,1)}, bf16[2,144,1152]{2,1,0:T(8,128)(2,1)}, u32[]{:S(2)}, u32[]{:S(2)}) collective-permute-start(bf16[2,144,1152]{2,1,0:T(8,128)(2,1)} %add_convert_fusion.7), channel_id=1, source_target_pairs={{0,2},{1,3},{2,0},{3,1},{4,6},{5,7},{6,4},{7,5},{8,10},{9,11},{10,... | collective-permute-start | bytes 1990664 | tf_op jit(solution)/shard_map/ppermute | solution.py:566
  409.5 25.2 %collective-permute-start.24 = (bf16[2,144,1152]{2,1,0:T(8,128)(2,1)}, bf16[2,144,1152]{2,1,0:T(8,128)(2,1)}, u32[]{:S(2)}, u32[]{:S(2)}) collective-permute-start(bf16[2,144,1152]{2,1,0:T(8,128)(2,1)} %get-tuple-element.297), channel_id=1, source_target_pairs={{0,16},{8,24},{16,0},{24,8},{1,17},{9,25},{17,1},{25,9},{2,18},{10... | collective-permute-start | bytes 1990664 | tf_op jit(solution)/shard_map/ppermute | solution.py:566
  439.4 31.2 %copy-start.22 = (f32[4608]{0:T(1024)S(1)}, f32[4608]{0:T(1024)}, u32[]{:S(2)}) copy-start(f32[4608]{0:T(1024)} %reduce.3) | copy-start | bytes 55300
  439.4 33.8 %collective-permute-start.26 = (bf16[1,144,1152]{2,1,0:T(8,128)(2,1)S(1)}, bf16[1,144,1152]{2,1,0:T(8,128)(2,1)}, u32[]{:S(2)}, u32[]{:S(2)}) collective-permute-start(bf16[1,144,1152]{2,1,0:T(8,128)(2,1)S(1)} %add_convert_fusion.15), channel_id=1, source_target_pairs={{0,4},{1,5},{2,6},{3,7},{4,0},{5,1},{6,2},{7,3},{8,12},{9,13},{10,... | collective-permute-start | bytes 995336 | tf_op jit(solution)/shard_map/ppermute | solution.py:566
  439.5 35.2 %collective-permute-start.27 = (bf16[2,144,1152]{2,1,0:T(8,128)(2,1)}, bf16[2,144,1152]{2,1,0:T(8,128)(2,1)}, u32[]{:S(2)}, u32[]{:S(2)}) collective-permute-start(bf16[2,144,1152]{2,1,0:T(8,128)(2,1)} %get-tuple-element.310), channel_id=1, source_target_pairs={{0,16},{8,24},{16,0},{24,8},{1,17},{9,25},{17,1},{25,9},{2,18},{10... | collective-permute-start | bytes 1990664 | tf_op jit(solution)/shard_map/ppermute | solution.py:566
  440.8 34.0 %collective-permute-start.28 = (bf16[4,144,1152]{2,1,0:T(8,128)(2,1)}, bf16[4,144,1152]{2,1,0:T(8,128)(2,1)S(1)}, u32[]{:S(2)}, u32[]{:S(2)}) collective-permute-start(bf16[4,144,1152]{2,1,0:T(8,128)(2,1)} %pad_maximum_fusion.2), channel_id=1, source_target_pairs={{0,1},{1,0},{2,3},{3,2},{4,5},{5,4},{6,7},{7,6},{8,9},{9,8},{10,11... | collective-permute-start | bytes 3981320 | tf_op jit(solution)/shard_map/ppermute | solution.py:566
  440.8 36.7 %collective-permute-start.29 = (bf16[2,144,1152]{2,1,0:T(8,128)(2,1)}, bf16[2,144,1152]{2,1,0:T(8,128)(2,1)S(1)}, u32[]{:S(2)}, u32[]{:S(2)}) collective-permute-start(bf16[2,144,1152]{2,1,0:T(8,128)(2,1)} %get-tuple-element.312), channel_id=1, source_target_pairs={{0,16},{8,24},{16,0},{24,8},{1,17},{9,25},{17,1},{25,9},{2,18},{10... | collective-permute-start | bytes 1990664 | tf_op jit(solution)/shard_map/ppermute | solution.py:566
  474.7 37.6 %copy-start.6 = (bf16[4,144,1152]{2,1,0:T(8,128)(2,1)}, bf16[4,144,1152]{2,1,0:T(8,128)(2,1)S(1)}, u32[]{:S(2)}) copy-start(bf16[4,144,1152]{2,1,0:T(8,128)(2,1)S(1)} %collective-permute-done.28) | copy-start | bytes 3981316
  477.5 34.8 %collective-permute-start.32 = (bf16[2,144,1152]{2,1,0:T(8,128)(2,1)}, bf16[2,144,1152]{2,1,0:T(8,128)(2,1)}, u32[]{:S(2)}, u32[]{:S(2)}) collective-permute-start(bf16[2,144,1152]{2,1,0:T(8,128)(2,1)} %add_convert_fusion.4), channel_id=1, source_target_pairs={{0,2},{1,3},{2,0},{3,1},{4,6},{5,7},{6,4},{7,5},{8,10},{9,11},{10,... | collective-permute-start | bytes 1990664 | tf_op jit(solution)/shard_map/ppermute | solution.py:566
  479.4 15.3 %collective-permute-start.30 = (bf16[1,144,1152]{2,1,0:T(8,128)(2,1)S(1)}, bf16[1,144,1152]{2,1,0:T(8,128)(2,1)S(1)}, u32[]{:S(2)}, u32[]{:S(2)}) collective-permute-start(bf16[1,144,1152]{2,1,0:T(8,128)(2,1)S(1)} %add_convert_fusion.14), channel_id=1, source_target_pairs={{0,8},{8,0},{16,24},{24,16},{1,9},{9,1},{17,25},{25,17},{2,10},{10... | collective-permute-start | bytes 995336 | tf_op jit(solution)/shard_map/ppermute | solution.py:566
  494.9 22.6 %collective-permute-start.33 = (bf16[8,144,768]{2,1,0:T(8,128)(2,1)}, bf16[8,144,768]{2,1,0:T(8,128)(2,1)}, u32[]{:S(2)}, u32[]{:S(2)}) collective-permute-start(bf16[8,144,768]{2,1,0:T(8,128)(2,1)} %get-tuple-element.328), channel_id=1, source_target_pairs={{0,8},{8,0},{16,24},{24,16},{1,9},{9,1},{17,25},{25,17},{2,10},{10... | collective-permute-start | bytes 5308424 | tf_op jit(solution)/shard_map/ppermute | solution.py:566
  495.5 25.3 %collective-permute-start.31 = (bf16[8,144,768]{2,1,0:T(8,128)(2,1)}, bf16[8,144,768]{2,1,0:T(8,128)(2,1)}, u32[]{:S(2)}, u32[]{:S(2)}) collective-permute-start(bf16[8,144,768]{2,1,0:T(8,128)(2,1)} %get-tuple-element.322), channel_id=1, source_target_pairs={{0,8},{8,0},{16,24},{24,16},{1,9},{9,1},{17,25},{25,17},{2,10},{10... | collective-permute-start | bytes 5308424 | tf_op jit(solution)/shard_map/ppermute | solution.py:566
  495.6 25.3 %collective-permute-start.34 = (bf16[8,144,768]{2,1,0:T(8,128)(2,1)}, bf16[8,144,768]{2,1,0:T(8,128)(2,1)}, u32[]{:S(2)}, u32[]{:S(2)}) collective-permute-start(bf16[8,144,768]{2,1,0:T(8,128)(2,1)} %get-tuple-element.329), channel_id=1, source_target_pairs={{0,8},{8,0},{16,24},{24,16},{1,9},{9,1},{17,25},{25,17},{2,10},{10... | collective-permute-start | bytes 5308424 | tf_op jit(solution)/shard_map/ppermute | solution.py:566
  496.0 18.4 %collective-permute-start.49 = (bf16[2,144,1152]{2,1,0:T(8,128)(2,1)S(1)}, bf16[2,144,1152]{2,1,0:T(8,128)(2,1)}, u32[]{:S(2)}, u32[]{:S(2)}) collective-permute-start(bf16[2,144,1152]{2,1,0:T(8,128)(2,1)S(1)} %pad_maximum_fusion.4), channel_id=1, source_target_pairs={{0,16},{8,24},{16,0},{24,8},{1,17},{9,25},{17,1},{25,9},{2,18},{10... | collective-permute-start | bytes 1990664 | tf_op jit(solution)/shard_map/ppermute | solution.py:566
  520.9 55.1 %collective-permute-start.35 = (bf16[4,144,768]{2,1,0:T(8,128)(2,1)}, bf16[4,144,768]{2,1,0:T(8,128)(2,1)}, u32[]{:S(2)}, u32[]{:S(2)}) collective-permute-start(bf16[4,144,768]{2,1,0:T(8,128)(2,1)} %get-tuple-element.330), channel_id=1, source_target_pairs={{0,16},{8,24},{16,0},{24,8},{1,17},{9,25},{17,1},{25,9},{2,18},{10... | collective-permute-start | bytes 2654216 | tf_op jit(solution)/shard_map/ppermute | solution.py:566
  537.5 17.4 %collective-permute-start.36 = (bf16[1,144,1152]{2,1,0:T(8,128)(2,1)}, bf16[1,144,1152]{2,1,0:T(8,128)(2,1)}, u32[]{:S(2)}, u32[]{:S(2)}) collective-permute-start(bf16[1,144,1152]{2,1,0:T(8,128)(2,1)} %add_convert_fusion.13), channel_id=1, source_target_pairs={{0,4},{1,5},{2,6},{3,7},{4,0},{5,1},{6,2},{7,3},{8,12},{9,13},{10,... | collective-permute-start | bytes 995336 | tf_op jit(solution)/shard_map/ppermute | solution.py:566
  554.9 23.7 %collective-permute-start.37 = (bf16[4,144,768]{2,1,0:T(8,128)(2,1)}, bf16[4,144,768]{2,1,0:T(8,128)(2,1)}, u32[]{:S(2)}, u32[]{:S(2)}) collective-permute-start(bf16[4,144,768]{2,1,0:T(8,128)(2,1)} %add_convert_fusion), channel_id=1, source_target_pairs={{0,1},{1,0},{2,3},{3,2},{4,5},{5,4},{6,7},{7,6},{8,9},{9,8},{10,11... | collective-permute-start | bytes 2654216 | tf_op jit(solution)/shard_map/ppermute | solution.py:566
  557.6 44.2 %collective-permute-start.38 = (bf16[4,144,768]{2,1,0:T(8,128)(2,1)}, bf16[4,144,768]{2,1,0:T(8,128)(2,1)}, u32[]{:S(2)}, u32[]{:S(2)}) collective-permute-start(bf16[4,144,768]{2,1,0:T(8,128)(2,1)} %get-tuple-element.343), channel_id=1, source_target_pairs={{0,16},{8,24},{16,0},{24,8},{1,17},{9,25},{17,1},{25,9},{2,18},{10... | collective-permute-start | bytes 2654216 | tf_op jit(solution)/shard_map/ppermute | solution.py:566
  580.2 24.0 %collective-permute-start.39 = (bf16[4,144,768]{2,1,0:T(8,128)(2,1)}, bf16[4,144,768]{2,1,0:T(8,128)(2,1)}, u32[]{:S(2)}, u32[]{:S(2)}) collective-permute-start(bf16[4,144,768]{2,1,0:T(8,128)(2,1)} %add_convert_fusion.2), channel_id=1, source_target_pairs={{0,1},{1,0},{2,3},{3,2},{4,5},{5,4},{6,7},{7,6},{8,9},{9,8},{10,11... | collective-permute-start | bytes 2654216 | tf_op jit(solution)/shard_map/ppermute | solution.py:566
  582.5 17.9 %collective-permute-start.40 = (bf16[2,144,768]{2,1,0:T(8,128)(2,1)S(1)}, bf16[2,144,768]{2,1,0:T(8,128)(2,1)}, u32[]{:S(2)}, u32[]{:S(2)}) collective-permute-start(bf16[2,144,768]{2,1,0:T(8,128)(2,1)S(1)} %add_convert_fusion.11), channel_id=1, source_target_pairs={{0,2},{1,3},{2,0},{3,1},{4,6},{5,7},{6,4},{7,5},{8,10},{9,11},{10,... | collective-permute-start | bytes 1327112 | tf_op jit(solution)/shard_map/ppermute | solution.py:566
  606.5 20.0 %collective-permute-start.41 = (bf16[2,144,768]{2,1,0:T(8,128)(2,1)}, bf16[2,144,768]{2,1,0:T(8,128)(2,1)S(1)}, u32[]{:S(2)}, u32[]{:S(2)}) collective-permute-start(bf16[2,144,768]{2,1,0:T(8,128)(2,1)} %add_convert_fusion.10), channel_id=1, source_target_pairs={{0,2},{1,3},{2,0},{3,1},{4,6},{5,7},{6,4},{7,5},{8,10},{9,11},{10,... | collective-permute-start | bytes 1327112 | tf_op jit(solution)/shard_map/ppermute | solution.py:566
  606.5 18.1 %collective-permute-start.42 = (bf16[1,144,768]{2,1,0:T(8,128)(2,1)S(1)}, bf16[1,144,768]{2,1,0:T(8,128)(2,1)S(1)}, u32[]{:S(2)}, u32[]{:S(2)}) collective-permute-start(bf16[1,144,768]{2,1,0:T(8,128)(2,1)S(1)} %add_convert_fusion.20), channel_id=1, source_target_pairs={{0,4},{1,5},{2,6},{3,7},{4,0},{5,1},{6,2},{7,3},{8,12},{9,13},{10,... | collective-permute-start | bytes 663560 | tf_op jit(solution)/shard_map/ppermute | solution.py:566
  607.1 18.9 %collective-permute-start.43 = (bf16[1,144,1152]{2,1,0:T(8,128)(2,1)S(1)}, bf16[1,144,1152]{2,1,0:T(8,128)(2,1)S(1)}, u32[]{:S(2)}, u32[]{:S(2)}) collective-permute-start(bf16[1,144,1152]{2,1,0:T(8,128)(2,1)S(1)} %add_convert_fusion.12), channel_id=1, source_target_pairs={{0,8},{8,0},{16,24},{24,16},{1,9},{9,1},{17,25},{25,17},{2,10},{10... | collective-permute-start | bytes 995336 | tf_op jit(solution)/shard_map/ppermute | solution.py:566
  627.9 20.4 %collective-permute-start.44 = (bf16[1,144,768]{2,1,0:T(8,128)(2,1)S(1)}, bf16[1,144,768]{2,1,0:T(8,128)(2,1)S(1)}, u32[]{:S(2)}, u32[]{:S(2)}) collective-permute-start(bf16[1,144,768]{2,1,0:T(8,128)(2,1)S(1)} %add_convert_fusion.19), channel_id=1, source_target_pairs={{0,4},{1,5},{2,6},{3,7},{4,0},{5,1},{6,2},{7,3},{8,12},{9,13},{10,... | collective-permute-start | bytes 663560 | tf_op jit(solution)/shard_map/ppermute | solution.py:566
  631.1 18.7 %collective-permute-start.45 = (bf16[2,144,1152]{2,1,0:T(8,128)(2,1)S(1)}, bf16[2,144,1152]{2,1,0:T(8,128)(2,1)S(1)}, u32[]{:S(2)}, u32[]{:S(2)}) collective-permute-start(bf16[2,144,1152]{2,1,0:T(8,128)(2,1)S(1)} %pad_maximum_fusion.5), channel_id=1, source_target_pairs={{0,16},{8,24},{16,0},{24,8},{1,17},{9,25},{17,1},{25,9},{2,18},{10... | collective-permute-start | bytes 1990664 | tf_op jit(solution)/shard_map/ppermute | solution.py:566
  649.8 10.6 %collective-permute-start.46 = (bf16[2,144,768]{2,1,0:T(8,128)(2,1)S(1)}, bf16[2,144,768]{2,1,0:T(8,128)(2,1)S(1)}, u32[]{:S(2)}, u32[]{:S(2)}) collective-permute-start(bf16[2,144,768]{2,1,0:T(8,128)(2,1)S(1)} %pad_maximum_fusion.7), channel_id=1, source_target_pairs={{0,16},{8,24},{16,0},{24,8},{1,17},{9,25},{17,1},{25,9},{2,18},{10... | collective-permute-start | bytes 1327112 | tf_op jit(solution)/shard_map/ppermute | solution.py:566
  650.9 3.9 collective-permute-start.47
  660.6 4.2 collective-permute-start.50
  664.9 6.9 collective-permute-start.51
  671.8 2.4 collective-permute-start.52
  673.7 2.2 collective-permute-start.48
  674.3 12.2 %collective-permute-start.53 = (bf16[64,3456]{1,0:T(8,128)(2,1)S(1)}, bf16[64,3456]{1,0:T(8,128)(2,1)S(1)}, u32[]{:S(2)}, u32[]{:S(2)}) collective-permute-start(bf16[64,3456]{1,0:T(8,128)(2,1)S(1)} %pad_maximum_fusion.8), channel_id=1, source_target_pairs={{0,16},{8,24},{16,0},{24,8},{1,17},{9,25},{17,1},{25,9},{2,18},{10... | collective-permute-start | bytes 1327112 | tf_op jit(solution)/shard_map/ppermute | solution.py:566
  (34 other events, 337.6 us)
Sparse Core Ops, SparseCore 0:
  11.5 103.8 all-gather.7
  118.3 100.1 all-gather.9
  557.7 64.0 all-gather.5

commit v2 on v1

--- a/solution.py
+++ b/solution.py
@@ -65,6 +65,10 @@
     return lambda first: pl.BlockSpec((1,) + tail, lambda s, *_: (s + first,) + (0,) * len(tail))
 
 
+def four_heads(rows, columns=GRID):
+    return lambda first: pl.BlockSpec((4, rows, columns), lambda s, *_: (s, 0, 0))
+
+
 def fixed(*shape, at=None):
     where = (0,) * len(shape) if at is None else at
     return lambda first: pl.BlockSpec(shape, lambda s, *_: where)
@@ -147,11 +151,14 @@
 
 
 def strips_kernel(span, scal, first, second, out):
-    out[...] = jnp.zeros_like(out)
-    for row in range(SIDE):
-        start = (SIDE - 1 - row) * SIDE
-        rows = slice(row * SIDE, (row + 1) * SIDE)
-        out[0, :, start : start + GRID] = out[0, :, start : start + GRID] + (first[0, rows, :] + second[0, rows, :])
+    for head in range(4):
+        total = jnp.zeros((SIDE, 2 * GRID), F32)
+        for row in range(SIDE):
+            rows = slice(row * SIDE, (row + 1) * SIDE)
+            pair = first[head, rows, :] + second[head, rows, :]
+            wide = jnp.concatenate([pair, jnp.zeros((SIDE, GRID), F32)], axis=1)
+            total = total + pltpu.roll(wide, (SIDE - 1 - row) * SIDE, axis=1)
+        out[head] = total
 
 
 def window(h):
@@ -326,61 +333,43 @@
     first, samples = span
     count, tiles = samples * GRID, quarters.shape[0]
     kept = [] if prior is None else [(i, v) for i, v in enumerate(prior) if v is not None]
-    starts = np.minimum(np.cumsum([0] + [p.shape[0] if p.ndim == 3 else p.shape[1] // D for p in parts]), tiles)
     used = len(parts) + len(weights)
 
     def body(scal_ref, quarters_ref, *refs):
-        total = refs[-1]
         ins, ws = refs[: len(parts)], refs[len(parts) : used]
         late_refs = refs[used : used + len(late)]
-        out_refs = refs[used + len(late) + len(kept) : -1]
-        step = pl.program_id(0)
+        out_refs = refs[used + len(late) + len(kept) :]
+        total, tile = None, 0
         for n, ref in enumerate(ins):
-            w = ws[n % len(ws)]
-
-            @pl.when(jnp.logical_and(step >= starts[n], step < starts[n + 1]))
-            def _():
-                for s in range(samples):
-                    part = dot_rt(ref[s * GRID : (s + 1) * GRID, :], w[0])
-
-                    @pl.when(step == 0)
-                    def _():
-                        total[s] = part
-
-                    @pl.when(step > 0)
-                    def _():
-                        total[s] = total[s] + part
-
-        @pl.when(step >= tiles)
-        def _():
-            finish(span, scal_ref, step - tiles, total[step - tiles], late_refs, out_refs)
-
-    def shift(spec):
-        block = spec(first)
-        return pl.BlockSpec(block.block_shape, lambda k, *a: block.index_map(jnp.maximum(k - tiles, 0), *a))
-
-    def part_spec(n):
-        low, high = int(starts[n]), int(starts[n + 1]) - 1
-        offset = 0 if parts[n].shape[-2] == count else first // samples
-        return column_block(parts[n], count, D, lambda k, *_: jnp.clip(k, low, high) - low, offset)
-
-    def weight_spec(n):
-        if len(weights) == 1:
-            return pl.BlockSpec((1, D, D), lambda k, scal, q: (q[jnp.minimum(k, tiles - 1)], 0, 0))
-        low, high = int(starts[n]), int(starts[n + 1]) - 1
-        return pl.BlockSpec((1, D, D), lambda k, *_: (jnp.clip(k, low, high) - low, 0, 0))
+            blocks = ref.shape[0] if len(ref.shape) == 3 else ref.shape[1] // D
+            for k in range(min(blocks, tiles - tile)):
+                left = ref[k] if len(ref.shape) == 3 else ref[:, k * D : (k + 1) * D]
+                right = ws[n][k] if len(ws) > 1 else ws[0][quarters_ref[tile]]
+                part = dot_rt(left, right)
+                total = part if total is None else total + part
+                tile += 1
+        finish(span, scal_ref, pl.program_id(0), total, late_refs, out_refs)
+
+    def part_spec(part):
+        offset = 0 if part.shape[-2] == count else first
+        if part.ndim == 2:
+            return pl.BlockSpec((GRID, part.shape[1]), lambda s, *_: (s + offset, 0))
+        return pl.BlockSpec((part.shape[0], GRID, D), lambda s, *_: (0, s + offset, 0))
+
+    def weight_spec(weight):
+        blocks = min(weight.shape[0], tiles)
+        return pl.BlockSpec((blocks, D, D), lambda s, *_: (0, 0, 0), pipeline_mode=pl.Buffered(1))
 
     return pl.pallas_call(
         body,
         grid_spec=pltpu.PrefetchScalarGridSpec(
             num_scalar_prefetch=2,
-            grid=(tiles + samples,),
-            in_specs=[part_spec(n) for n in range(len(parts))]
-            + [weight_spec(n) for n in range(len(weights))]
-            + [shift(spec) for spec in late_specs]
-            + [anywhere(0)] * len(kept),
-            out_specs=[shift(spec) for _, _, spec in outs],
-            scratch_shapes=[pltpu.VMEM((samples, GRID, D), F32)],
+            grid=(samples,),
+            in_specs=[part_spec(part) for part in parts]
+            + [weight_spec(weight) for weight in weights]
+            + [spec(first) for spec in late_specs]
+            + [anywhere(first)] * len(kept),
+            out_specs=[spec(first) for _, _, spec in outs],
         ),
         out_shape=[jax.ShapeDtypeStruct(shape, kind) for shape, kind, _ in outs],
         input_output_aliases={2 + used + len(late) + n: i for n, (i, _) in enumerate(kept)},
@@ -874,8 +863,9 @@
         [((count, D), F32, rows_spec(D)), ((count, D), BF, rows_spec(D)), ((1, D), F32, fixed(1, D)), ((samples, 3, D), F32, per_sample(3, D))],
         mid_back_finish, everything, "mid_back",
     )
-    mid_all = lax.all_gather(mid_grads.reshape(1, samples * 3, D), ("dp", "seq"), axis=0, tiled=True)
-    mid_all = mid_all.astype(BF).reshape(-1, 3 * D)
+    mid_rows = jnp.pad(mid_grads.astype(BF), ((0, 0), (0, 1), (0, 0))).reshape(1, samples * 4, D)
+    mid_all = lax.all_gather(mid_rows, ("dp", "seq"), axis=0, tiled=True).reshape(-1, 4, D)[:, :3].reshape(-1, 3 * D)
+
     def attend_part(chains, after, span):
         inputs = slot((gbr, packed, lse, mask, table, joint), chains, after)
         return call(
@@ -907,8 +897,8 @@
     joints = [joint_sum] if wires.cube else []
     placed_a, placed_b = slot((placed_a, placed_b), sums[1:], (done,), slow=joints)
     (strip_grad,) = call(
-        strips_kernel, scal, (placed_a, placed_b), [per_sample(GRID, GRID)] * 2,
-        [((HEADS, SIDE, 2 * GRID), F32, per_sample(SIDE, 2 * GRID))], [], (0, HEADS), "strips", cost(0, 9 << 20),
+        strips_kernel, scal, (placed_a, placed_b), [four_heads(GRID)] * 2,
+        [((HEADS, SIDE, 2 * GRID), F32, four_heads(SIDE, 2 * GRID))], [], (0, HEADS // 4), "strips", cost(0, 9 << 20),
     )
     strip_grad = strip_grad[:, :, : SPAN * SIDE].reshape(HEADS, SIDE, SPAN, SIDE)
     table_grad = jnp.einsum(

time: 715 us -> 633 us (0.89)
  blocking collectives: 74.4 us -> 0 us
  Pallas kernels: 349 us -> 330 us
    all_gather x1 -> x0, blocking collectives: 74.4 us -> none  [local(): lax.all_gather(mid_grads.reshape(1, samples * 3, D), ('dp', 'seq'), axis=...]
    pallas_call x5, Pallas kernels: 98 us -> 84.9 us  [turned_product(): pl.pallas_call(body, grid_spec=pltpu.PrefetchScalarGridSpec(num_scalar_pr...]
  transfers between devices with their start and end apart: 57 -> 58, of which waited for: 17 -> 18; matrix products, arithmetic and copies ran while one was open for 13% -> 16% of each run, Pallas kernels for 48% -> 51%
where the time goes in v2:
time: 633 us; the launch traced here: 620 us
  Pallas kernels  330 us (52%)
  waiting for transfers between devices  113 us (18%)
  other arithmetic  60.1 us (9%)
  starting transfers between devices  52.7 us (8%)
  local copies, waits for them, and re-layouts  39.3 us (6%)
  between operations  15.4 us (2%)
  matrix products  10.5 us (2%)
    pallas_call x8, Pallas kernels, call(): pl.pallas_call(body, grid_spec=pltpu.PrefetchScalarGridSpec(num_scalar_pr...  115 us
    ppermute x54, waiting for transfers between devices, flip(): lax.ppermute(value, axis, [(i, i ^ bit) for i in range(size)])  112 us
    pallas_call x5, Pallas kernels, turned_product(): pl.pallas_call(body, grid_spec=pltpu.PrefetchScalarGridSpec(num_scalar_pr...  84.9 us
    pallas_call x4, Pallas kernels, outer_tiles(): pl.pallas_call(functools.partial(outer_kernel, kinds, sources, width, rol...  70.8 us
    ppermute x54, starting transfers between devices, flip(): lax.ppermute(value, axis, [(i, i ^ bit) for i in range(size)])  52.5 us
    pallas_call x2, Pallas kernels, up_quarters(): pl.pallas_call(functools.partial(up_kernel, count // GRID, gaps), grid_sp...  33.5 us
    pallas_call x2, Pallas kernels, act_back(): pl.pallas_call(functools.partial(act_back_kernel, count // GRID), grid_sp...  25.2 us
  transfers between devices with their start and end apart: 58, of which 18 were waited for; matrix products, arithmetic and copies ran while one was open for 16% of the time, Pallas kernels for 51%

profile of v2, /device:TPU:0, one launch (start us, length us, event | category | flops | bytes accessed | tf_op | source)
XLA Modules:
  0.0 620.5 jit_solution(18172363211979572793)
XLA Ops:
  7.3 1.9 dynamic-slice_select_fusion
  12.4 4.1 collective-permute-start
  17.1 6.5 %place.1 = (bf16[1024,1152]{1,0:T(8,128)(2,1)}, bf16[1024,1152]{1,0:T(8,128)(2,1)}, f32[4,1,256]{2,1,0:T(1,128)}) custom-call(s32[6]{0:T(128)} %pad_add_fusion.scal_ref.scal, bf16[1024,1152]{1,0:T(8,128)(2,1)} %refs_0_, bf16[1024,1152]{1,0:T(8,128)(2,1)} %refs_1_, s32[4,1,256]{2,1,0:T(1,128)} %reshape.215.refs_2_), custom_call_target="tpu_custom_call" | custom-call | flops 1207959552 | bytes 9437184 | tf_op jit(solution)/shard_map/place/pallas_call | solution.py:89
  23.6 1.8 constant_dynamic-slice_fusion
  27.1 1.8 convolution_bitcast_fusion
  28.9 4.4 copy.76
  33.2 4.4 reshape.217
  39.6 1.7 collective-permute-start.2
  41.3 10.2 %bias.1.refs_2_.refs_4_ = f32[16,256,256]{2,1,0:T(8,128)} custom-call(s32[6]{0:T(128)} %pad_add_fusion.scal_ref.scal, f32[16,16,512]{2,1,0:T(8,128)} %pad.12.refs_0_), custom_call_target="tpu_custom_call" | custom-call | bytes 5242880 | tf_op jit(solution)/shard_map/bias/pallas_call | solution.py:89
  54.7 21.4 %collective-permute-done.3 = bf16[2,144,1152]{2,1,0:T(8,128)(2,1)S(1)} collective-permute-done((bf16[2,144,1152]{2,1,0:T(8,128)(2,1)S(1)}, bf16[2,144,1152]{2,1,0:T(8,128)(2,1)S(1)}, u32[]{:S(2)}, u32[]{:S(2)}) %collective-permute-start.3) | collective-permute-done | bytes 663584 | tf_op jit(solution)/shard_map/ppermute | solution.py:555
  77.2 13.2 %collective-permute-done.5 = bf16[2,4,6912]{2,1,0:T(4,128)(2,1)S(1)} collective-permute-done((bf16[2,4,6912]{2,1,0:T(4,128)(2,1)S(1)}, bf16[2,4,6912]{2,1,0:T(4,128)(2,1)S(1)}, u32[]{:S(2)}, u32[]{:S(2)}) %collective-permute-start.5) | collective-permute-done | bytes 110624 | tf_op jit(solution)/shard_map/ppermute | solution.py:555
  94.3 5.8 collective-permute-done.6
  100.9 25.3 %collective-permute-done.7.refs_1_ = bf16[4,144,1152]{2,1,0:T(8,128)(2,1)} collective-permute-done((bf16[4,144,1152]{2,1,0:T(8,128)(2,1)S(1)}, bf16[4,144,1152]{2,1,0:T(8,128)(2,1)}, u32[]{:S(2)}, u32[]{:S(2)}) %collective-permute-start.7) | collective-permute-done | bytes 1327136 | tf_op jit(solution)/shard_map/ppermute | solution.py:555
  128.8 17.6 %qkv.1 = (bf16[1024,1152]{1,0:T(8,128)(2,1)}, bf16[1024,3456]{1,0:T(8,128)(2,1)}) custom-call(s32[6]{0:T(128)} %pad_add_fusion.scal_ref.scal, bf16[1024,1152]{1,0:T(8,128)(2,1)} %get-tuple-element.223.refs_0_.refs_1_.refs_2_, f32[4,6,1152]{2,1,0:T(8,128)} %broadcast_add_fusion.refs_1_.refs_3_.refs_7_.refs_5_.refs_4_, f32[1,3456]{1,0:T(1,128)} %fusion.31.refs_2_, ...), custom_call_target="tpu_custom_call" | custom-call | flops 8153726976 | bytes 23068672 | tf_op jit(solution)/shard_map/qkv/pallas_call | solution.py:89
  146.4 15.6 %attend.1 = (bf16[1024,1152]{1,0:T(8,128)(2,1)}, f32[1024,128]{1,0:T(8,128)}) custom-call(s32[6]{0:T(128)} %pad_add_fusion.scal_ref.scal, bf16[1024,3456]{1,0:T(8,128)(2,1)} %get-tuple-element.302.refs_0_.refs_1_, f32[4,1,256]{2,1,0:T(1,128)} %get-tuple-element.304.refs_1_.refs_3_, f32[16,256,256]{2,1,0:T(8,128)} %bias.1.refs_2_.refs_4_), custom_call_target="tpu_custom_call" | custom-call | flops 4294967296 | bytes 15728640 | tf_op jit(solution)/shard_map/attend/pallas_call | solution.py:89
  161.9 6.6 %collective-permute-done.9.refs_3_ = bf16[4,144,1152]{2,1,0:T(8,128)(2,1)S(1)} collective-permute-done((bf16[4,144,1152]{2,1,0:T(8,128)(2,1)}, bf16[4,144,1152]{2,1,0:T(8,128)(2,1)S(1)}, u32[]{:S(2)}, u32[]{:S(2)}) %collective-permute-start.9) | collective-permute-done | bytes 1327136 | tf_op jit(solution)/shard_map/ppermute | solution.py:555
  170.0 11.3 %merge.1 = (bf16[1024,1152]{1,0:T(8,128)(2,1)}, f32[1024,1152]{1,0:T(8,128)}, bf16[1024,1152]{1,0:T(8,128)(2,1)}, bf16[1024,1152]{1,0:T(8,128)(2,1)}, f32[1,1152]{1,0:T(1,128)}) custom-call(s32[6]{0:T(128)} %pad_add_fusion.scal_ref.scal, bf16[1024,1152]{1,0:T(8,128)(2,1)} %get-tuple-element.222.refs_0_.refs_2_.refs_3_, ...), custom_call_target="tpu_custom_call" | custom-call | flops 2717908992 | bytes 20971520 | tf_op jit(solution)/shard_map/merge/pallas_call | solution.py:89
  182.4 16.8 %up.2 = (bf16[2,1024,1152]{2,1,0:T(8,128)(2,1)}, bf16[2,1024,1152]{2,1,0:T(8,128)(2,1)}, bf16[2,1152,1152]{2,1,0:T(8,128)(2,1)}) custom-call(s32[6]{0:T(128)} %pad_add_fusion.scal_ref.scal, s32[2]{0:T(128)} %pad_add_fusion.3.quarters, bf16[1024,1152]{1,0:T(8,128)(2,1)} %get-tuple-element.239.h2.refs_0_, f32[1,4608]{1,0:T(1,128)} %reshape.241.bias, ...), custom_call_target="tpu_custom_call" | custom-call | flops 5435817984 | bytes 24772608 | tf_op jit(solution)/shard_map/up/pallas_call | solution.py:277
  200.8 16.7 %up.3 = (bf16[2,1024,1152]{2,1,0:T(8,128)(2,1)}, bf16[2,1024,1152]{2,1,0:T(8,128)(2,1)}, bf16[2,1152,1152]{2,1,0:T(8,128)(2,1)}) custom-call(s32[6]{0:T(128)} %pad_add_fusion.scal_ref.scal, s32[2]{0:T(128)} %pad_add_fusion.2.quarters, bf16[1024,1152]{1,0:T(8,128)(2,1)} %get-tuple-element.239.h2.refs_0_, f32[1,4608]{1,0:T(1,128)} %reshape.241.bias, ...), custom_call_target="tpu_custom_call" | custom-call | flops 5435817984 | bytes 24772608 | tf_op jit(solution)/shard_map/up/pallas_call | solution.py:277
  217.5 20.1 %down_outer.1 = (bf16[2,144,1152]{2,1,0:T(8,128)(2,1)}, bf16[2,144,1152]{2,1,0:T(8,128)(2,1)}, bf16[2,144,1152]{2,1,0:T(8,128)(2,1)}, bf16[2,144,1152]{2,1,0:T(8...) custom-call(s32[6]{0:T(128)} %pad_add_fusion.scal_ref.scal, ...), custom_call_target="tpu_custom_call" | custom-call | flops 10871635968 | bytes 14155776 | tf_op jit(solution)/shard_map/down_outer/pallas_call | solution.py:533
  237.7 12.7 %act_back.2 = (bf16[2,1024,1152]{2,1,0:T(8,128)(2,1)}, f32[1,4608]{1,0:T(1,128)}) custom-call(s32[6]{0:T(128)} %pad_add_fusion.scal_ref.scal, s32[2]{0:T(128)} %pad_add_fusion.3.quarters, bf16[1024,1152]{1,0:T(8,128)(2,1)} %get-tuple-element.259.refs_0_.gm, bf16[2,1024,1152]{2,1,0:T(8,128)(2,1)} %get-tuple-element.255.slope, bf16[4,1152,1152]{2,1,0:T(8,128)(2,1)} %bitcast.140), custom_call_target="tpu_custom_call" | custom-call | flops 5435817984 | bytes 14745600 | tf_op jit(solution)/shard_map/act_back/pallas_call | solution.py:308
  250.4 1.6 collective-permute-start.17
  252.0 12.5 %act_back.3 = (bf16[2,1024,1152]{2,1,0:T(8,128)(2,1)}, f32[1,4608]{1,0:T(1,128)}) custom-call(s32[6]{0:T(128)} %pad_add_fusion.scal_ref.scal, s32[2]{0:T(128)} %pad_add_fusion.2.quarters, bf16[1024,1152]{1,0:T(8,128)(2,1)} %get-tuple-element.259.refs_0_.gm, bf16[2,1024,1152]{2,1,0:T(8,128)(2,1)} %get-tuple-element.260.slope, ...), custom_call_target="tpu_custom_call", output_to_operand_aliasing={{1}: (5, {})} | custom-call | flops 5435817984 | bytes 14745600 | tf_op jit(solution)/shard_map/act_back/pallas_call | solution.py:308
  264.5 3.2 collective-permute-done.17
  269.5 20.4 %up_outer.1 = (bf16[2,144,1152]{2,1,0:T(8,128)(2,1)}, bf16[2,144,1152]{2,1,0:T(8,128)(2,1)}, bf16[2,144,1152]{2,1,0:T(8,128)(2,1)}, bf16[2,144,1152]{2,1,0:T(8,1...) custom-call(s32[6]{0:T(128)} %pad_add_fusion.scal_ref.scal, ...), custom_call_target="tpu_custom_call" | custom-call | flops 10871635968 | bytes 14155776 | tf_op jit(solution)/shard_map/up_outer/pallas_call | solution.py:533
  295.8 25.8 %mid_back.1 = (f32[1024,1152]{1,0:T(8,128)}, bf16[1024,1152]{1,0:T(8,128)(2,1)}, f32[1,1152]{1,0:T(1,128)}, f32[4,3,1152]{2,1,0:T(4,128)}) custom-call(s32[6]{0:T(128)} %pad_add_fusion.scal_ref.scal, s32[4]{0:T(128)} %pad_add_fusion.1.quarters_ref, bf16[2,1024,1152]{2,1,0:T(8,128)(2,1)} %get-tuple-element.273.refs_2_.refs_0_, ...), custom_call_target="tpu_custom_call" | custom-call | flops 10871635968 | bytes 31850496 | tf_op jit(solution)/shard_map/mid_back/pallas_call | solution.py:363
  321.7 2.7 add_convert_fusion.7
  329.9 24.1 %attend_back.2 = (bf16[512,4608]{1,0:T(8,128)(2,1)}, f32[1,3456]{1,0:T(1,128)}, f32[16,256,256]{2,1,0:T(8,128)}) custom-call(s32[6]{0:T(128)} %pad_add_fusion.scal_ref.scal, bf16[1024,1152]{1,0:T(8,128)(2,1)} %get-tuple-element.301.refs_0_, bf16[1024,3456]{1,0:T(8,128)(2,1)} %get-tuple-element.302.refs_0_.refs_1_, f32[1024,128]{1,0:T(8,128)} %get-tuple-element.303.refs_2_, ...), custom_call_target="tpu_custom_call" | custom-call | flops 6727663616 | bytes 20971520 | tf_op jit(solution)/shard_map/attend_back/pallas_call | solution.py:89
  356.4 2.1 add_convert_fusion.15
  358.5 2.5 collective-permute-start.26
  361.0 1.7 collective-permute-start.27
  364.6 24.2 %attend_back.3 = (bf16[512,4608]{1,0:T(8,128)(2,1)}, f32[1,3456]{1,0:T(1,128)}, f32[16,256,256]{2,1,0:T(8,128)}) custom-call(s32[6]{0:T(128)} %pad_add_fusion.scal_ref.scal, bf16[1024,1152]{1,0:T(8,128)(2,1)} %get-tuple-element.301.refs_0_, bf16[1024,3456]{1,0:T(8,128)(2,1)} %get-tuple-element.302.refs_0_.refs_1_, f32[1024,128]{1,0:T(8,128)} %get-tuple-element.303.refs_2_, ...), custom_call_target="tpu_custom_call" | custom-call | flops 6727663616 | bytes 20971520 | tf_op jit(solution)/shard_map/attend_back/pallas_call | solution.py:89
  390.8 2.5 reshape.232
  393.3 2.0 copy.85
  396.8 2.4 add_convert_fusion.4
  399.8 15.3 %joint_give.1 = (bf16[8,144,768]{2,1,0:T(8,128)(2,1)}, bf16[8,144,768]{2,1,0:T(8,128)(2,1)}, bf16[8,144,768]{2,1,0:T(8,128)(2,1)}) custom-call(s32[6]{0:T(128)} %pad_add_fusion.scal_ref.scal, s32[3]{0:T(128)} %get-tuple-element.418.blocks, bf16[1024,1152]{1,0:T(8,128)(2,1)} %get-tuple-element.245.refs_0_.refs_1_, ...), custom_call_target="tpu_custom_call" | custom-call | flops 5435817984 | bytes 9437184 | tf_op jit(solution)/shard_map/joint_give/pallas_call | solution.py:533
  417.8 15.0 %joint_keep.1 = (bf16[8,144,768]{2,1,0:T(8,128)(2,1)}, bf16[8,144,768]{2,1,0:T(8,128)(2,1)}, bf16[8,144,768]{2,1,0:T(8,128)(2,1)}) custom-call(s32[6]{0:T(128)} %pad_add_fusion.scal_ref.scal, s32[3]{0:T(128)} %get-tuple-element.417.blocks, bf16[1024,1152]{1,0:T(8,128)(2,1)} %get-tuple-element.245.refs_0_.refs_1_, ...), custom_call_target="tpu_custom_call" | custom-call | flops 5435817984 | bytes 9437184 | tf_op jit(solution)/shard_map/joint_keep/pallas_call | solution.py:533
  435.7 1.8 maximum_convert_fusion.1
  437.7 3.1 add_convert_fusion.1
  441.5 5.9 strips.1
  447.4 4.1 reshape.227
  451.5 2.4 collective-permute-start.36
  453.9 5.6 convolution_bitcast_fusion.1
  459.8 2.3 add_convert_fusion
  462.1 6.6 %collective-permute-done.36 = bf16[1,144,1152]{2,1,0:T(8,128)(2,1)S(1)} collective-permute-done((bf16[1,144,1152]{2,1,0:T(8,128)(2,1)S(1)}, bf16[1,144,1152]{2,1,0:T(8,128)(2,1)S(1)}, u32[]{:S(2)}, u32[]{:S(2)}) %collective-permute-start.36) | collective-permute-done | bytes 331808 | tf_op jit(solution)/shard_map/ppermute | solution.py:555
  472.1 15.0 %down.2 = (bf16[1024,1152]{1,0:T(8,128)(2,1)}, f32[4,1,1152]{2,1,0:T(1,128)}) custom-call(s32[6]{0:T(128)} %pad_add_fusion.scal_ref.scal, s32[4]{0:T(128)} %pad_add_fusion.1.quarters_ref, bf16[2,1024,1152]{2,1,0:T(8,128)(2,1)} %get-tuple-element.339.refs_2_.refs_0_, bf16[2,1024,1152]{2,1,0:T(8,128)(2,1)} %get-tuple-element.340.refs_1_, ...), custom_call_target="tpu_custom_call" | custom-call | flops 5435817984 | bytes 21233664 | tf_op jit(solution)/shard_map/down/pallas_call | solution.py:363
  487.1 2.4 add_convert_fusion.2
  490.4 2.2 add_convert_fusion.11
  495.5 14.6 %down.3 = (bf16[1024,1152]{1,0:T(8,128)(2,1)}, f32[4,1,1152]{2,1,0:T(1,128)}) custom-call(s32[6]{0:T(128)} %pad_add_fusion.scal_ref.scal, s32[4]{0:T(128)} %pad_add_fusion.1.quarters_ref, bf16[2,1024,1152]{2,1,0:T(8,128)(2,1)} %get-tuple-element.339.refs_2_.refs_0_, ...), custom_call_target="tpu_custom_call", output_to_operand_aliasing={{0}: (10, {}), {1}: (11, {})} | custom-call | flops 5435817984 | bytes 21233664 | tf_op jit(solution)/shard_map/down/pallas_call | solution.py:363
  510.9 2.1 add_convert_fusion.20
  514.2 2.1 add_convert_fusion.10
  518.8 14.8 %front_back.2 = (f32[1024,1152]{1,0:T(8,128)}, f32[4,2,1152]{2,1,0:T(2,128)}) custom-call(s32[6]{0:T(128)} %pad_add_fusion.scal_ref.scal, s32[3]{0:T(128)} %bitcast.158, bf16[512,4608]{1,0:T(8,128)(2,1)} %get-tuple-element.349.refs_4_.refs_0_, bf16[4,1152,1152]{2,1,0:T(8,128)(2,1)} %bitcast.138, ...), custom_call_target="tpu_custom_call" | custom-call | flops 4076863488 | bytes 17399808 | tf_op jit(solution)/shard_map/front_back/pallas_call | solution.py:363
  533.6 2.6 collective-permute-done.42
  539.6 2.9 collective-permute-start.44
  542.5 1.7 collective-permute-start.45
  544.2 14.8 %front_back.3 = (f32[1024,1152]{1,0:T(8,128)}, f32[4,2,1152]{2,1,0:T(2,128)}) custom-call(s32[6]{0:T(128)} %pad_add_fusion.scal_ref.scal, s32[3]{0:T(128)} %bitcast.159, bf16[512,4608]{1,0:T(8,128)(2,1)} %get-tuple-element.352.refs_5_.refs_0_, bf16[4,1152,1152]{2,1,0:T(8,128)(2,1)} %bitcast.139, ...), custom_call_target="tpu_custom_call", output_to_operand_aliasing={{0}: (8, {}), {1}: (9, {})} | custom-call | flops 4076863488 | bytes 17399808 | tf_op jit(solution)/shard_map/front_back/pallas_call | solution.py:363
  561.7 1.7 collective-permute-start.47
  565.6 6.3 %collective-permute-done.46 = bf16[2,144,768]{2,1,0:T(8,128)(2,1)S(1)} collective-permute-done((bf16[2,144,768]{2,1,0:T(8,128)(2,1)S(1)}, bf16[2,144,768]{2,1,0:T(8,128)(2,1)S(1)}, u32[]{:S(2)}, u32[]{:S(2)}) %collective-permute-start.46) | collective-permute-done | bytes 442400 | tf_op jit(solution)/shard_map/ppermute | solution.py:555
  572.6 3.7 collective-permute-done.50
  576.9 6.3 %collective-permute-done.51 = bf16[16,3456]{1,0:T(8,128)(2,1)S(1)} collective-permute-done((bf16[16,3456]{1,0:T(8,128)(2,1)S(1)}, bf16[16,3456]{1,0:T(8,128)(2,1)S(1)}, u32[]{:S(2)}, u32[]{:S(2)}) %collective-permute-start.51) | collective-permute-done | bytes 110624 | tf_op jit(solution)/shard_map/ppermute | solution.py:555
  583.4 1.8 maximum_convert_fusion
  596.1 6.4 %collective-permute-done.53 = bf16[64,3456]{1,0:T(8,128)(2,1)S(1)} collective-permute-done((bf16[64,3456]{1,0:T(8,128)(2,1)}, bf16[64,3456]{1,0:T(8,128)(2,1)S(1)}, u32[]{:S(2)}, u32[]{:S(2)}) %collective-permute-start.53) | collective-permute-done | bytes 442400 | tf_op jit(solution)/shard_map/ppermute | solution.py:555
  606.2 2.7 fusion.16
  608.9 2.1 reduce_sum.18
  (308 shorter events, 89.3 us)
Async XLA Ops:
  7.2 119.0 %all-gather.11.cloned.1.call-start = ((), (), s32[]{:S(2)}) async-start(), calls=%async_computation.2 | async-start | bytes 10948608 | tf_op jit(solution)/shard_map/all_gather | solution.py:640
  9.2 228.5 %all-gather.13.cloned.1.call-start = ((), (), s32[]{:S(2)}) async-start(), calls=%async_computation.3 | async-start | bytes 10948608 | tf_op jit(solution)/shard_map/all_gather | solution.py:640
  12.4 26.2 %collective-permute-start = (bf16[1,144,1152]{2,1,0:T(8,128)(2,1)S(1)}, bf16[1,144,1152]{2,1,0:T(8,128)(2,1)}, u32[]{:S(2)}, u32[]{:S(2)}) collective-permute-start(bf16[1,144,1152]{2,1,0:T(8,128)(2,1)S(1)} %dynamic-slice_bitcast_fusion), channel_id=1, source_target_pairs={{0,4},{1,5},{2,6},{3,7},{4,0},{5,1},{6,2},{7,3},{8,12},{9,13},{10,... | collective-permute-start | bytes 995336 | tf_op jit(solution)/shard_map/ppermute | solution.py:555
  16.5 22.1 %collective-permute-start.1 = (bf16[32,144]{1,0:T(8,128)(2,1)S(1)}, bf16[32,144]{1,0:T(8,128)(2,1)S(1)}, u32[]{:S(2)}, u32[]{:S(2)}) collective-permute-start(bf16[32,144]{1,0:T(8,128)(2,1)S(1)} %constant_dynamic-slice_fusion.1), channel_id=1, source_target_pairs={{0,8},{8,0},{16,24},{24,16},{1,9},{9,1},{17,25},{25,17},{2,10},{10... | collective-permute-start | bytes 27656 | tf_op jit(solution)/shard_map/ppermute | solution.py:555
  25.4 365.4 %all-gather.7.cloned.1.call-start = ((), (), s32[]{:S(2)}) async-start(), calls=%async_computation | async-start | bytes 1216512 | tf_op jit(solution)/shard_map/all_gather | solution.py:867
  39.6 14.8 %collective-permute-start.2 = (bf16[4,4,6912]{2,1,0:T(4,128)(2,1)S(1)}, bf16[4,4,6912]{2,1,0:T(4,128)(2,1)S(1)}, u32[]{:S(2)}, u32[]{:S(2)}) collective-permute-start(bf16[4,4,6912]{2,1,0:T(4,128)(2,1)S(1)} %fusion.6), channel_id=1, source_target_pairs={{0,1},{1,0},{2,3},{3,2},{4,5},{5,4},{6,7},{7,6},{8,9},{9,8},{10,11... | collective-permute-start | bytes 663560 | tf_op jit(solution)/shard_map/ppermute | solution.py:555
  51.5 24.6 %collective-permute-start.3 = (bf16[2,144,1152]{2,1,0:T(8,128)(2,1)S(1)}, bf16[2,144,1152]{2,1,0:T(8,128)(2,1)S(1)}, u32[]{:S(2)}, u32[]{:S(2)}) collective-permute-start(bf16[2,144,1152]{2,1,0:T(8,128)(2,1)S(1)} %pad_maximum_fusion.4), channel_id=1, source_target_pairs={{0,2},{1,3},{2,0},{3,1},{4,6},{5,7},{6,4},{7,5},{8,10},{9,11},{10,... | collective-permute-start | bytes 1990664 | tf_op jit(solution)/shard_map/ppermute | solution.py:555
  53.0 23.3 %collective-permute-start.4 = (bf16[64,144]{1,0:T(8,128)(2,1)S(1)}, bf16[64,144]{1,0:T(8,128)(2,1)S(1)}, u32[]{:S(2)}, u32[]{:S(2)}) collective-permute-start(bf16[64,144]{1,0:T(8,128)(2,1)S(1)} %pad_maximum_fusion.13), channel_id=1, source_target_pairs={{0,16},{8,24},{16,0},{24,8},{1,17},{9,25},{17,1},{25,9},{2,18},{10... | collective-permute-start | bytes 55304 | tf_op jit(solution)/shard_map/ppermute | solution.py:555
  54.7 37.2 %copy-start.33 = (bf16[6912]{0:T(1024)(128)(2,1)S(1)}, bf16[6912]{0:T(1024)(128)(2,1)}, u32[]{:S(2)}) copy-start(bf16[6912]{0:T(1024)(128)(2,1)} %param.32) | copy-start | bytes 41476
  54.7 73.5 %copy-start.39 = (bf16[1152]{0:T(1024)(128)(2,1)S(1)}, bf16[1152]{0:T(1024)(128)(2,1)}, u32[]{:S(2)}) copy-start(bf16[1152]{0:T(1024)(128)(2,1)} %param.26) | copy-start | bytes 6916
  76.2 70.1 %copy-start.8 = (bf16[4,144,1152]{2,1,0:T(8,128)(2,1)}, bf16[4,144,1152]{2,1,0:T(8,128)(2,1)S(1)}, u32[]{:S(2)}) copy-start(bf16[4,144,1152]{2,1,0:T(8,128)(2,1)S(1)} %pad_maximum_fusion.refs_0_) | copy-start | bytes 3981316
  76.3 14.1 %collective-permute-start.5 = (bf16[2,4,6912]{2,1,0:T(4,128)(2,1)S(1)}, bf16[2,4,6912]{2,1,0:T(4,128)(2,1)S(1)}, u32[]{:S(2)}, u32[]{:S(2)}) collective-permute-start(bf16[2,4,6912]{2,1,0:T(4,128)(2,1)S(1)} %fusion.15), channel_id=1, source_target_pairs={{0,2},{1,3},{2,0},{3,1},{4,6},{5,7},{6,4},{7,5},{8,10},{9,11},{10,... | collective-permute-start | bytes 331784 | tf_op jit(solution)/shard_map/ppermute | solution.py:555
  90.5 9.6 %collective-permute-start.6 = (bf16[1,4,6912]{2,1,0:T(4,128)(2,1)S(1)}, bf16[1,4,6912]{2,1,0:T(4,128)(2,1)S(1)}, u32[]{:S(2)}, u32[]{:S(2)}) collective-permute-start(bf16[1,4,6912]{2,1,0:T(4,128)(2,1)S(1)} %fusion.22), channel_id=1, source_target_pairs={{0,4},{1,5},{2,6},{3,7},{4,0},{5,1},{6,2},{7,3},{8,12},{9,13},{10,... | collective-permute-start | bytes 165896 | tf_op jit(solution)/shard_map/ppermute | solution.py:555
  91.9 34.3 %collective-permute-start.7 = (bf16[4,144,1152]{2,1,0:T(8,128)(2,1)S(1)}, bf16[4,144,1152]{2,1,0:T(8,128)(2,1)}, u32[]{:S(2)}, u32[]{:S(2)}) collective-permute-start(bf16[4,144,1152]{2,1,0:T(8,128)(2,1)S(1)} %pad_maximum_fusion.refs_0_), channel_id=1, source_target_pairs={{0,1},{1,0},{2,3},{3,2},{4,5},{5,4},{6,7},{7,6},{8,9},{9,8},{10,11... | collective-permute-start | bytes 3981320 | tf_op jit(solution)/shard_map/ppermute | solution.py:555
  92.8 33.4 %collective-permute-start.8 = (bf16[4,144,1152]{2,1,0:T(8,128)(2,1)S(1)}, bf16[4,144,1152]{2,1,0:T(8,128)(2,1)}, u32[]{:S(2)}, u32[]{:S(2)}) collective-permute-start(bf16[4,144,1152]{2,1,0:T(8,128)(2,1)S(1)} %pad_maximum_fusion.refs_0_), channel_id=1, source_target_pairs={{0,16},{8,24},{16,0},{24,8},{1,17},{9,25},{17,1},{25,9},{2,18},{10... | collective-permute-start | bytes 3981320 | tf_op jit(solution)/shard_map/ppermute | solution.py:555
  126.2 42.3 %collective-permute-start.9 = (bf16[4,144,1152]{2,1,0:T(8,128)(2,1)}, bf16[4,144,1152]{2,1,0:T(8,128)(2,1)S(1)}, u32[]{:S(2)}, u32[]{:S(2)}) collective-permute-start(bf16[4,144,1152]{2,1,0:T(8,128)(2,1)} %collective-permute-done.7.refs_1_), channel_id=1, source_target_pairs={{0,16},{8,24},{16,0},{24,8},{1,17},{9,25},{17,1},{25,9},{2,18},{10... | collective-permute-start | bytes 3981320 | tf_op jit(solution)/shard_map/ppermute | solution.py:555
  127.7 40.9 %collective-permute-start.11 = (bf16[4,144,1152]{2,1,0:T(8,128)(2,1)}, bf16[4,144,1152]{2,1,0:T(8,128)(2,1)}, u32[]{:S(2)}, u32[]{:S(2)}) collective-permute-start(bf16[4,144,1152]{2,1,0:T(8,128)(2,1)} %collective-permute-done.7.refs_1_), channel_id=1, source_target_pairs={{0,8},{8,0},{16,24},{24,16},{1,9},{9,1},{17,25},{25,17},{2,10},{10... | collective-permute-start | bytes 3981320 | tf_op jit(solution)/shard_map/ppermute | solution.py:555
  127.7 40.9 %collective-permute-start.10 = (bf16[4,144,1152]{2,1,0:T(8,128)(2,1)S(1)}, bf16[4,144,1152]{2,1,0:T(8,128)(2,1)}, u32[]{:S(2)}, u32[]{:S(2)}) collective-permute-start(bf16[4,144,1152]{2,1,0:T(8,128)(2,1)S(1)} %pad_maximum_fusion.refs_0_), channel_id=1, source_target_pairs={{0,8},{8,0},{16,24},{24,16},{1,9},{9,1},{17,25},{25,17},{2,10},{10... | collective-permute-start | bytes 3981320 | tf_op jit(solution)/shard_map/ppermute | solution.py:555
  128.2 40.4 %collective-permute-start.12 = (bf16[4,144,1152]{2,1,0:T(8,128)(2,1)}, bf16[4,144,1152]{2,1,0:T(8,128)(2,1)}, u32[]{:S(2)}, u32[]{:S(2)}) collective-permute-start(bf16[4,144,1152]{2,1,0:T(8,128)(2,1)} %collective-permute-done.8.refs_2_), channel_id=1, source_target_pairs={{0,8},{8,0},{16,24},{24,16},{1,9},{9,1},{17,25},{25,17},{2,10},{10... | collective-permute-start | bytes 3981320 | tf_op jit(solution)/shard_map/ppermute | solution.py:555
  168.6 12.8 %collective-permute-start.13 = (bf16[4,144,1152]{2,1,0:T(8,128)(2,1)S(1)}, bf16[4,144,1152]{2,1,0:T(8,128)(2,1)S(1)}, u32[]{:S(2)}, u32[]{:S(2)}) collective-permute-start(bf16[4,144,1152]{2,1,0:T(8,128)(2,1)S(1)} %collective-permute-done.9.refs_3_), channel_id=1, source_target_pairs={{0,8},{8,0},{16,24},{24,16},{1,9},{9,1},{17,25},{25,17},{2,10},{10... | collective-permute-start | bytes 3981320 | tf_op jit(solution)/shard_map/ppermute | solution.py:555
  199.2 18.3 %collective-permute-start.15 = (bf16[2,1024,1152]{2,1,0:T(8,128)(2,1)}, bf16[2,1024,1152]{2,1,0:T(8,128)(2,1)}, u32[]{:S(2)}, u32[]{:S(2)}) collective-permute-start(bf16[2,1024,1152]{2,1,0:T(8,128)(2,1)} %get-tuple-element.340.refs_1_), channel_id=1, source_target_pairs={{0,8},{8,0},{16,24},{24,16},{1,9},{9,1},{17,25},{25,17},{2,10},{10... | collective-permute-start | bytes 14155784 | tf_op jit(solution)/shard_map/ppermute | solution.py:555
  199.7 17.8 %collective-permute-start.14 = (bf16[1024,1152]{1,0:T(8,128)(2,1)}, bf16[1024,1152]{1,0:T(8,128)(2,1)}, u32[]{:S(2)}, u32[]{:S(2)}) collective-permute-start(bf16[1024,1152]{1,0:T(8,128)(2,1)} %get-tuple-element.259.refs_0_.gm), channel_id=1, source_target_pairs={{0,8},{8,0},{16,24},{24,16},{1,9},{9,1},{17,25},{25,17},{2,10},{10... | collective-permute-start | bytes 7077896 | tf_op jit(solution)/shard_map/ppermute | solution.py:555
  199.8 17.7 %collective-permute-start.16 = (bf16[1024,1152]{1,0:T(8,128)(2,1)}, bf16[1024,1152]{1,0:T(8,128)(2,1)}, u32[]{:S(2)}, u32[]{:S(2)}) collective-permute-start(bf16[1024,1152]{1,0:T(8,128)(2,1)} %get-tuple-element.239.h2.refs_0_), channel_id=1, source_target_pairs={{0,8},{8,0},{16,24},{24,16},{1,9},{9,1},{17,25},{25,17},{2,10},{10... | collective-permute-start | bytes 7077896 | tf_op jit(solution)/shard_map/ppermute | solution.py:555
  250.4 17.5 %collective-permute-start.18 = (bf16[2,1024,1152]{2,1,0:T(8,128)(2,1)}, bf16[2,1024,1152]{2,1,0:T(8,128)(2,1)}, u32[]{:S(2)}, u32[]{:S(2)}) collective-permute-start(bf16[2,1024,1152]{2,1,0:T(8,128)(2,1)} %get-tuple-element.274.refs_1_), channel_id=1, source_target_pairs={{0,8},{8,0},{16,24},{24,16},{1,9},{9,1},{17,25},{25,17},{2,10},{10... | collective-permute-start | bytes 14155784 | tf_op jit(solution)/shard_map/ppermute | solution.py:555
  250.4 17.3 %collective-permute-start.17 = (bf16[2,144,1152]{2,1,0:T(8,128)(2,1)S(1)}, bf16[2,144,1152]{2,1,0:T(8,128)(2,1)S(1)}, u32[]{:S(2)}, u32[]{:S(2)}) collective-permute-start(bf16[2,144,1152]{2,1,0:T(8,128)(2,1)S(1)} %copy-done.45), channel_id=1, source_target_pairs={{0,16},{8,24},{16,0},{24,8},{1,17},{9,25},{17,1},{25,9},{2,18},{10... | collective-permute-start | bytes 1990664 | tf_op jit(solution)/shard_map/ppermute | solution.py:555
  267.9 22.0 %collective-permute-start.19 = (bf16[2,144,1152]{2,1,0:T(8,128)(2,1)S(1)}, bf16[2,144,1152]{2,1,0:T(8,128)(2,1)S(1)}, u32[]{:S(2)}, u32[]{:S(2)}) collective-permute-start(bf16[2,144,1152]{2,1,0:T(8,128)(2,1)S(1)} %copy-done.44), channel_id=1, source_target_pairs={{0,16},{8,24},{16,0},{24,8},{1,17},{9,25},{17,1},{25,9},{2,18},{10... | collective-permute-start | bytes 1990664 | tf_op jit(solution)/shard_map/ppermute | solution.py:555
  290.2 31.4 %collective-permute-start.21 = (bf16[4,144,1152]{2,1,0:T(8,128)(2,1)S(1)}, bf16[4,144,1152]{2,1,0:T(8,128)(2,1)S(1)}, u32[]{:S(2)}, u32[]{:S(2)}) collective-permute-start(bf16[4,144,1152]{2,1,0:T(8,128)(2,1)S(1)} %pad_maximum_fusion.1), channel_id=1, source_target_pairs={{0,1},{1,0},{2,3},{3,2},{4,5},{5,4},{6,7},{7,6},{8,9},{9,8},{10,11... | collective-permute-start | bytes 3981320 | tf_op jit(solution)/shard_map/ppermute | solution.py:555
  293.8 27.9 %collective-permute-start.20 = (bf16[2,144,1152]{2,1,0:T(8,128)(2,1)}, bf16[2,144,1152]{2,1,0:T(8,128)(2,1)}, u32[]{:S(2)}, u32[]{:S(2)}) collective-permute-start(bf16[2,144,1152]{2,1,0:T(8,128)(2,1)} %get-tuple-element.282), channel_id=1, source_target_pairs={{0,16},{8,24},{16,0},{24,8},{1,17},{9,25},{17,1},{25,9},{2,18},{10... | collective-permute-start | bytes 1990664 | tf_op jit(solution)/shard_map/ppermute | solution.py:555
  295.4 29.0 %collective-permute-start.22 = (bf16[2,144,1152]{2,1,0:T(8,128)(2,1)}, bf16[2,144,1152]{2,1,0:T(8,128)(2,1)}, u32[]{:S(2)}, u32[]{:S(2)}) collective-permute-start(bf16[2,144,1152]{2,1,0:T(8,128)(2,1)} %get-tuple-element.286), channel_id=1, source_target_pairs={{0,16},{8,24},{16,0},{24,8},{1,17},{9,25},{17,1},{25,9},{2,18},{10... | collective-permute-start | bytes 1990664 | tf_op jit(solution)/shard_map/ppermute | solution.py:555
  321.7 32.4 %copy-start.9 = (bf16[4,144,1152]{2,1,0:T(8,128)(2,1)}, bf16[4,144,1152]{2,1,0:T(8,128)(2,1)S(1)}, u32[]{:S(2)}) copy-start(bf16[4,144,1152]{2,1,0:T(8,128)(2,1)S(1)} %collective-permute-done.21) | copy-start | bytes 3981316
  324.4 29.7 %collective-permute-start.25 = (bf16[2,144,1152]{2,1,0:T(8,128)(2,1)}, bf16[2,144,1152]{2,1,0:T(8,128)(2,1)S(1)}, u32[]{:S(2)}, u32[]{:S(2)}) collective-permute-start(bf16[2,144,1152]{2,1,0:T(8,128)(2,1)} %get-tuple-element.299), channel_id=1, source_target_pairs={{0,16},{8,24},{16,0},{24,8},{1,17},{9,25},{17,1},{25,9},{2,18},{10... | collective-permute-start | bytes 1990664 | tf_op jit(solution)/shard_map/ppermute | solution.py:555
  327.4 281.5 %all-gather.9.cloned.1.call-start = ((), (), s32[]{:S(2)}) async-start(), calls=%async_computation.1 | async-start | bytes 3379200 | tf_op jit(solution)/shard_map/all_gather | solution.py:912
  327.5 26.6 %copy-start.15 = (bf16[2,144,1152]{2,1,0:T(8,128)(2,1)S(1)}, bf16[2,144,1152]{2,1,0:T(8,128)(2,1)}, u32[]{:S(2)}) copy-start(bf16[2,144,1152]{2,1,0:T(8,128)(2,1)} %get-tuple-element.298) | copy-start | bytes 1990660
  327.5 28.0 %collective-permute-start.23 = (bf16[2,144,1152]{2,1,0:T(8,128)(2,1)}, bf16[2,144,1152]{2,1,0:T(8,128)(2,1)}, u32[]{:S(2)}, u32[]{:S(2)}) collective-permute-start(bf16[2,144,1152]{2,1,0:T(8,128)(2,1)} %add_convert_fusion.7), channel_id=1, source_target_pairs={{0,2},{1,3},{2,0},{3,1},{4,6},{5,7},{6,4},{7,5},{8,10},{9,11},{10,... | collective-permute-start | bytes 1990664 | tf_op jit(solution)/shard_map/ppermute | solution.py:555
  328.8 25.7 %collective-permute-start.24 = (bf16[2,144,1152]{2,1,0:T(8,128)(2,1)}, bf16[2,144,1152]{2,1,0:T(8,128)(2,1)S(1)}, u32[]{:S(2)}, u32[]{:S(2)}) collective-permute-start(bf16[2,144,1152]{2,1,0:T(8,128)(2,1)} %get-tuple-element.297), channel_id=1, source_target_pairs={{0,16},{8,24},{16,0},{24,8},{1,17},{9,25},{17,1},{25,9},{2,18},{10... | collective-permute-start | bytes 1990664 | tf_op jit(solution)/shard_map/ppermute | solution.py:555
  358.5 30.4 %copy-start.34 = (f32[1,3456]{1,0:T(1,128)S(1)}, f32[1,3456]{1,0:T(1,128)}, u32[]{:S(2)}) copy-start(f32[1,3456]{1,0:T(1,128)} %get-tuple-element.368) | copy-start | bytes 41476
  358.5 36.8 %collective-permute-start.26 = (bf16[1,144,1152]{2,1,0:T(8,128)(2,1)}, bf16[1,144,1152]{2,1,0:T(8,128)(2,1)}, u32[]{:S(2)}, u32[]{:S(2)}) collective-permute-start(bf16[1,144,1152]{2,1,0:T(8,128)(2,1)} %add_convert_fusion.15), channel_id=1, source_target_pairs={{0,4},{1,5},{2,6},{3,7},{4,0},{5,1},{6,2},{7,3},{8,12},{9,13},{10,... | collective-permute-start | bytes 995336 | tf_op jit(solution)/shard_map/ppermute | solution.py:555
  361.0 35.8 %collective-permute-start.27 = (bf16[2,144,1152]{2,1,0:T(8,128)(2,1)}, bf16[2,144,1152]{2,1,0:T(8,128)(2,1)}, u32[]{:S(2)}, u32[]{:S(2)}) collective-permute-start(bf16[2,144,1152]{2,1,0:T(8,128)(2,1)} %get-tuple-element.310), channel_id=1, source_target_pairs={{0,16},{8,24},{16,0},{24,8},{1,17},{9,25},{17,1},{25,9},{2,18},{10... | collective-permute-start | bytes 1990664 | tf_op jit(solution)/shard_map/ppermute | solution.py:555
  362.7 34.1 %collective-permute-start.28 = (bf16[4,144,1152]{2,1,0:T(8,128)(2,1)S(1)}, bf16[4,144,1152]{2,1,0:T(8,128)(2,1)}, u32[]{:S(2)}, u32[]{:S(2)}) collective-permute-start(bf16[4,144,1152]{2,1,0:T(8,128)(2,1)S(1)} %pad_maximum_fusion.2), channel_id=1, source_target_pairs={{0,1},{1,0},{2,3},{3,2},{4,5},{5,4},{6,7},{7,6},{8,9},{9,8},{10,11... | collective-permute-start | bytes 3981320 | tf_op jit(solution)/shard_map/ppermute | solution.py:555
  363.6 35.7 %collective-permute-start.29 = (bf16[2,144,1152]{2,1,0:T(8,128)(2,1)}, bf16[2,144,1152]{2,1,0:T(8,128)(2,1)}, u32[]{:S(2)}, u32[]{:S(2)}) collective-permute-start(bf16[2,144,1152]{2,1,0:T(8,128)(2,1)} %get-tuple-element.312), channel_id=1, source_target_pairs={{0,16},{8,24},{16,0},{24,8},{1,17},{9,25},{17,1},{25,9},{2,18},{10... | collective-permute-start | bytes 1990664 | tf_op jit(solution)/shard_map/ppermute | solution.py:555
  399.2 33.5 %collective-permute-start.32 = (bf16[2,144,1152]{2,1,0:T(8,128)(2,1)}, bf16[2,144,1152]{2,1,0:T(8,128)(2,1)S(1)}, u32[]{:S(2)}, u32[]{:S(2)}) collective-permute-start(bf16[2,144,1152]{2,1,0:T(8,128)(2,1)} %add_convert_fusion.4), channel_id=1, source_target_pairs={{0,2},{1,3},{2,0},{3,1},{4,6},{5,7},{6,4},{7,5},{8,10},{9,11},{10,... | collective-permute-start | bytes 1990664 | tf_op jit(solution)/shard_map/ppermute | solution.py:555
  399.8 15.3 %collective-permute-start.30 = (bf16[1,144,1152]{2,1,0:T(8,128)(2,1)S(1)}, bf16[1,144,1152]{2,1,0:T(8,128)(2,1)S(1)}, u32[]{:S(2)}, u32[]{:S(2)}) collective-permute-start(bf16[1,144,1152]{2,1,0:T(8,128)(2,1)S(1)} %add_convert_fusion.14), channel_id=1, source_target_pairs={{0,8},{8,0},{16,24},{24,16},{1,9},{9,1},{17,25},{25,17},{2,10},{10... | collective-permute-start | bytes 995336 | tf_op jit(solution)/shard_map/ppermute | solution.py:555
  415.3 22.2 %collective-permute-start.33 = (bf16[8,144,768]{2,1,0:T(8,128)(2,1)}, bf16[8,144,768]{2,1,0:T(8,128)(2,1)}, u32[]{:S(2)}, u32[]{:S(2)}) collective-permute-start(bf16[8,144,768]{2,1,0:T(8,128)(2,1)} %get-tuple-element.328), channel_id=1, source_target_pairs={{0,8},{8,0},{16,24},{24,16},{1,9},{9,1},{17,25},{25,17},{2,10},{10... | collective-permute-start | bytes 5308424 | tf_op jit(solution)/shard_map/ppermute | solution.py:555
  415.9 24.9 %collective-permute-start.31 = (bf16[8,144,768]{2,1,0:T(8,128)(2,1)}, bf16[8,144,768]{2,1,0:T(8,128)(2,1)S(1)}, u32[]{:S(2)}, u32[]{:S(2)}) collective-permute-start(bf16[8,144,768]{2,1,0:T(8,128)(2,1)} %get-tuple-element.322), channel_id=1, source_target_pairs={{0,8},{8,0},{16,24},{24,16},{1,9},{9,1},{17,25},{25,17},{2,10},{10... | collective-permute-start | bytes 5308424 | tf_op jit(solution)/shard_map/ppermute | solution.py:555
  415.9 24.9 %collective-permute-start.34 = (bf16[8,144,768]{2,1,0:T(8,128)(2,1)}, bf16[8,144,768]{2,1,0:T(8,128)(2,1)}, u32[]{:S(2)}, u32[]{:S(2)}) collective-permute-start(bf16[8,144,768]{2,1,0:T(8,128)(2,1)} %get-tuple-element.329), channel_id=1, source_target_pairs={{0,8},{8,0},{16,24},{24,16},{1,9},{9,1},{17,25},{25,17},{2,10},{10... | collective-permute-start | bytes 5308424 | tf_op jit(solution)/shard_map/ppermute | solution.py:555
  416.4 18.0 %collective-permute-start.49 = (bf16[2,144,1152]{2,1,0:T(8,128)(2,1)S(1)}, bf16[2,144,1152]{2,1,0:T(8,128)(2,1)}, u32[]{:S(2)}, u32[]{:S(2)}) collective-permute-start(bf16[2,144,1152]{2,1,0:T(8,128)(2,1)S(1)} %pad_maximum_fusion.5), channel_id=1, source_target_pairs={{0,16},{8,24},{16,0},{24,8},{1,17},{9,25},{17,1},{25,9},{2,18},{10... | collective-permute-start | bytes 1990664 | tf_op jit(solution)/shard_map/ppermute | solution.py:555
  440.8 46.2 %collective-permute-start.35 = (bf16[4,144,768]{2,1,0:T(8,128)(2,1)}, bf16[4,144,768]{2,1,0:T(8,128)(2,1)}, u32[]{:S(2)}, u32[]{:S(2)}) collective-permute-start(bf16[4,144,768]{2,1,0:T(8,128)(2,1)} %get-tuple-element.330), channel_id=1, source_target_pairs={{0,16},{8,24},{16,0},{24,8},{1,17},{9,25},{17,1},{25,9},{2,18},{10... | collective-permute-start | bytes 2654216 | tf_op jit(solution)/shard_map/ppermute | solution.py:555
  451.5 17.3 %collective-permute-start.36 = (bf16[1,144,1152]{2,1,0:T(8,128)(2,1)S(1)}, bf16[1,144,1152]{2,1,0:T(8,128)(2,1)S(1)}, u32[]{:S(2)}, u32[]{:S(2)}) collective-permute-start(bf16[1,144,1152]{2,1,0:T(8,128)(2,1)S(1)} %add_convert_fusion.13), channel_id=1, source_target_pairs={{0,4},{1,5},{2,6},{3,7},{4,0},{5,1},{6,2},{7,3},{8,12},{9,13},{10,... | collective-permute-start | bytes 995336 | tf_op jit(solution)/shard_map/ppermute | solution.py:555
  468.8 21.6 %collective-permute-start.37 = (bf16[4,144,768]{2,1,0:T(8,128)(2,1)}, bf16[4,144,768]{2,1,0:T(8,128)(2,1)}, u32[]{:S(2)}, u32[]{:S(2)}) collective-permute-start(bf16[4,144,768]{2,1,0:T(8,128)(2,1)} %add_convert_fusion), channel_id=1, source_target_pairs={{0,1},{1,0},{2,3},{3,2},{4,5},{5,4},{6,7},{7,6},{8,9},{9,8},{10,11... | collective-permute-start | bytes 2654216 | tf_op jit(solution)/shard_map/ppermute | solution.py:555
  470.9 42.0 %collective-permute-start.38 = (bf16[4,144,768]{2,1,0:T(8,128)(2,1)}, bf16[4,144,768]{2,1,0:T(8,128)(2,1)}, u32[]{:S(2)}, u32[]{:S(2)}) collective-permute-start(bf16[4,144,768]{2,1,0:T(8,128)(2,1)} %get-tuple-element.343), channel_id=1, source_target_pairs={{0,16},{8,24},{16,0},{24,8},{1,17},{9,25},{17,1},{25,9},{2,18},{10... | collective-permute-start | bytes 2654216 | tf_op jit(solution)/shard_map/ppermute | solution.py:555
  492.6 21.6 %collective-permute-start.39 = (bf16[4,144,768]{2,1,0:T(8,128)(2,1)}, bf16[4,144,768]{2,1,0:T(8,128)(2,1)}, u32[]{:S(2)}, u32[]{:S(2)}) collective-permute-start(bf16[4,144,768]{2,1,0:T(8,128)(2,1)} %add_convert_fusion.2), channel_id=1, source_target_pairs={{0,1},{1,0},{2,3},{3,2},{4,5},{5,4},{6,7},{7,6},{8,9},{9,8},{10,11... | collective-permute-start | bytes 2654216 | tf_op jit(solution)/shard_map/ppermute | solution.py:555
  495.4 15.4 %collective-permute-start.40 = (bf16[2,144,768]{2,1,0:T(8,128)(2,1)}, bf16[2,144,768]{2,1,0:T(8,128)(2,1)}, u32[]{:S(2)}, u32[]{:S(2)}) collective-permute-start(bf16[2,144,768]{2,1,0:T(8,128)(2,1)} %add_convert_fusion.11), channel_id=1, source_target_pairs={{0,2},{1,3},{2,0},{3,1},{4,6},{5,7},{6,4},{7,5},{8,10},{9,11},{10,... | collective-permute-start | bytes 1327112 | tf_op jit(solution)/shard_map/ppermute | solution.py:555
  516.3 22.0 %collective-permute-start.41 = (bf16[2,144,768]{2,1,0:T(8,128)(2,1)}, bf16[2,144,768]{2,1,0:T(8,128)(2,1)S(1)}, u32[]{:S(2)}, u32[]{:S(2)}) collective-permute-start(bf16[2,144,768]{2,1,0:T(8,128)(2,1)} %add_convert_fusion.10), channel_id=1, source_target_pairs={{0,2},{1,3},{2,0},{3,1},{4,6},{5,7},{6,4},{7,5},{8,10},{9,11},{10,... | collective-permute-start | bytes 1327112 | tf_op jit(solution)/shard_map/ppermute | solution.py:555
  517.1 19.2 %collective-permute-start.42 = (bf16[1,144,768]{2,1,0:T(8,128)(2,1)}, bf16[1,144,768]{2,1,0:T(8,128)(2,1)S(1)}, u32[]{:S(2)}, u32[]{:S(2)}) collective-permute-start(bf16[1,144,768]{2,1,0:T(8,128)(2,1)} %add_convert_fusion.20), channel_id=1, source_target_pairs={{0,4},{1,5},{2,6},{3,7},{4,0},{5,1},{6,2},{7,3},{8,12},{9,13},{10,... | collective-permute-start | bytes 663560 | tf_op jit(solution)/shard_map/ppermute | solution.py:555
  518.3 19.3 %collective-permute-start.43 = (bf16[1,144,1152]{2,1,0:T(8,128)(2,1)S(1)}, bf16[1,144,1152]{2,1,0:T(8,128)(2,1)S(1)}, u32[]{:S(2)}, u32[]{:S(2)}) collective-permute-start(bf16[1,144,1152]{2,1,0:T(8,128)(2,1)S(1)} %add_convert_fusion.12), channel_id=1, source_target_pairs={{0,8},{8,0},{16,24},{24,16},{1,9},{9,1},{17,25},{25,17},{2,10},{10... | collective-permute-start | bytes 995336 | tf_op jit(solution)/shard_map/ppermute | solution.py:555
  539.6 20.3 %collective-permute-start.44 = (bf16[1,144,768]{2,1,0:T(8,128)(2,1)S(1)}, bf16[1,144,768]{2,1,0:T(8,128)(2,1)S(1)}, u32[]{:S(2)}, u32[]{:S(2)}) collective-permute-start(bf16[1,144,768]{2,1,0:T(8,128)(2,1)S(1)} %add_convert_fusion.19), channel_id=1, source_target_pairs={{0,4},{1,5},{2,6},{3,7},{4,0},{5,1},{6,2},{7,3},{8,12},{9,13},{10,... | collective-permute-start | bytes 663560 | tf_op jit(solution)/shard_map/ppermute | solution.py:555
  542.5 18.8 %collective-permute-start.45 = (bf16[2,144,1152]{2,1,0:T(8,128)(2,1)S(1)}, bf16[2,144,1152]{2,1,0:T(8,128)(2,1)}, u32[]{:S(2)}, u32[]{:S(2)}) collective-permute-start(bf16[2,144,1152]{2,1,0:T(8,128)(2,1)S(1)} %pad_maximum_fusion.6), channel_id=1, source_target_pairs={{0,16},{8,24},{16,0},{24,8},{1,17},{9,25},{17,1},{25,9},{2,18},{10... | collective-permute-start | bytes 1990664 | tf_op jit(solution)/shard_map/ppermute | solution.py:555
  561.3 10.7 %collective-permute-start.46 = (bf16[2,144,768]{2,1,0:T(8,128)(2,1)S(1)}, bf16[2,144,768]{2,1,0:T(8,128)(2,1)S(1)}, u32[]{:S(2)}, u32[]{:S(2)}) collective-permute-start(bf16[2,144,768]{2,1,0:T(8,128)(2,1)S(1)} %pad_maximum_fusion.8), channel_id=1, source_target_pairs={{0,16},{8,24},{16,0},{24,8},{1,17},{9,25},{17,1},{25,9},{2,18},{10... | collective-permute-start | bytes 1327112 | tf_op jit(solution)/shard_map/ppermute | solution.py:555
  561.7 3.9 collective-permute-start.47
  572.1 4.2 collective-permute-start.50
  576.4 6.9 %collective-permute-start.51 = (bf16[16,3456]{1,0:T(8,128)(2,1)S(1)}, bf16[16,3456]{1,0:T(8,128)(2,1)S(1)}, u32[]{:S(2)}, u32[]{:S(2)}) collective-permute-start(bf16[16,3456]{1,0:T(8,128)(2,1)S(1)} %pad_maximum_fusion.11), channel_id=1, source_target_pairs={{0,4},{1,5},{2,6},{3,7},{4,0},{5,1},{6,2},{7,3},{8,12},{9,13},{10,... | collective-permute-start | bytes 331784 | tf_op jit(solution)/shard_map/ppermute | solution.py:555
  583.3 2.8 collective-permute-start.52
  585.2 5.3 collective-permute-start.48
  590.2 12.3 %collective-permute-start.53 = (bf16[64,3456]{1,0:T(8,128)(2,1)}, bf16[64,3456]{1,0:T(8,128)(2,1)S(1)}, u32[]{:S(2)}, u32[]{:S(2)}) collective-permute-start(bf16[64,3456]{1,0:T(8,128)(2,1)} %copy.90), channel_id=1, source_target_pairs={{0,16},{8,24},{16,0},{24,8},{1,17},{9,25},{17,1},{25,9},{2,18},{10... | collective-permute-start | bytes 1327112 | tf_op jit(solution)/shard_map/ppermute | solution.py:555
  (40 other events, 316.1 us)
Sparse Core Ops, SparseCore 0:
  11.5 105.0 all-gather.10
  119.5 98.5 all-gather.12
  327.5 63.2 all-gather.6
  471.0 62.9 all-gather.8

commit v3 on v2

--- a/solution.py
+++ b/solution.py
@@ -895,7 +895,7 @@
         done = keep[0]
 
     joints = [joint_sum] if wires.cube else []
-    placed_a, placed_b = slot((placed_a, placed_b), sums[1:], (done,), slow=joints)
+    placed_a, placed_b = slot((placed_a, placed_b), (), (done,), slow=joints + sums[1:])
     (strip_grad,) = call(
         strips_kernel, scal, (placed_a, placed_b), [four_heads(GRID)] * 2,
         [((HEADS, SIDE, 2 * GRID), F32, four_heads(SIDE, 2 * GRID))], [], (0, HEADS // 4), "strips", cost(0, 9 << 20),
@@ -937,8 +937,8 @@
     end_grads = jnp.concatenate([front_grads, down_grads], axis=1).astype(BF).reshape(samples, 3 * D)
     end_chain = Chain(gather_steps(end_grads, everyone))
     if wires.cube:
-        for _ in range(2):
-            (mid_all,) = slot((mid_all,), [joint_sum, end_chain])
+        (mid_all,) = slot((mid_all,), [joint_sum, end_chain])
+        (mid_all,) = slot((mid_all,), [joint_sum, end_chain], (loose,))
         up_grad, down_grad, joint_grad = up_sum.finish(), down_sum.finish(), joint_sum.finish()
     else:
         up_grad = Chain(wires.spread(up_part)).finish()

time: 633 us -> 623 us (0.984)
  waiting for transfers between devices: 113 us -> 104 us
    ppermute x54, waiting for transfers between devices: 112 us -> 103 us  [flip(): lax.ppermute(value, axis, [(i, i ^ bit) for i in range(size)])]
  transfers between devices with their start and end apart: 58 -> 58, of which waited for: 18 -> 17; matrix products, arithmetic and copies ran while one was open for 16% -> 16% of each run, Pallas kernels for 51% -> 52%
where the time goes in v3:
time: 623 us; the launch traced here: 611 us
  Pallas kernels  330 us (53%)
  waiting for transfers between devices  104 us (17%)
  other arithmetic  60.6 us (10%)
  starting transfers between devices  51.5 us (8%)
  local copies, waits for them, and re-layouts  39.1 us (6%)
  between operations  15.4 us (2%)
  matrix products  10.4 us (2%)
    pallas_call x8, Pallas kernels, call(): pl.pallas_call(body, grid_spec=pltpu.PrefetchScalarGridSpec(num_scalar_pr...  116 us
    ppermute x54, waiting for transfers between devices, flip(): lax.ppermute(value, axis, [(i, i ^ bit) for i in range(size)])  103 us
    pallas_call x5, Pallas kernels, turned_product(): pl.pallas_call(body, grid_spec=pltpu.PrefetchScalarGridSpec(num_scalar_pr...  84.7 us
    pallas_call x4, Pallas kernels, outer_tiles(): pl.pallas_call(functools.partial(outer_kernel, kinds, sources, width, rol...  70.9 us
    ppermute x54, starting transfers between devices, flip(): lax.ppermute(value, axis, [(i, i ^ bit) for i in range(size)])  51.3 us
    pallas_call x2, Pallas kernels, up_quarters(): pl.pallas_call(functools.partial(up_kernel, count // GRID, gaps), grid_sp...  33.6 us
    pallas_call x2, Pallas kernels, act_back(): pl.pallas_call(functools.partial(act_back_kernel, count // GRID), grid_sp...  25.2 us
  transfers between devices with their start and end apart: 58, of which 17 were waited for; matrix products, arithmetic and copies ran while one was open for 16% of the time, Pallas kernels for 52%

profile of v3, /device:TPU:0, one launch (start us, length us, event | category | flops | bytes accessed | tf_op | source)
XLA Modules:
  0.0 611.2 jit_solution(11259583540603450569)
XLA Ops:
  7.3 1.9 dynamic-slice_select_fusion
  12.4 4.1 collective-permute-start
  17.1 6.5 %place.1 = (bf16[1024,1152]{1,0:T(8,128)(2,1)}, bf16[1024,1152]{1,0:T(8,128)(2,1)}, f32[4,1,256]{2,1,0:T(1,128)}) custom-call(s32[6]{0:T(128)} %pad_add_fusion.scal_ref.scal, bf16[1024,1152]{1,0:T(8,128)(2,1)} %refs_0_, bf16[1024,1152]{1,0:T(8,128)(2,1)} %refs_1_, s32[4,1,256]{2,1,0:T(1,128)} %reshape.215.refs_2_), custom_call_target="tpu_custom_call" | custom-call | flops 1207959552 | bytes 9437184 | tf_op jit(solution)/shard_map/place/pallas_call | solution.py:89
  23.6 1.7 constant_dynamic-slice_fusion
  27.1 1.8 convolution_bitcast_fusion
  28.9 4.4 copy.76
  33.2 4.4 reshape.217
  39.6 1.7 collective-permute-start.2
  41.3 10.2 %bias.1.refs_2_.refs_4_ = f32[16,256,256]{2,1,0:T(8,128)} custom-call(s32[6]{0:T(128)} %pad_add_fusion.scal_ref.scal, f32[16,16,512]{2,1,0:T(8,128)} %pad.12.refs_0_), custom_call_target="tpu_custom_call" | custom-call | bytes 5242880 | tf_op jit(solution)/shard_map/bias/pallas_call | solution.py:89
  54.7 21.4 %collective-permute-done.3 = bf16[2,144,1152]{2,1,0:T(8,128)(2,1)S(1)} collective-permute-done((bf16[2,144,1152]{2,1,0:T(8,128)(2,1)S(1)}, bf16[2,144,1152]{2,1,0:T(8,128)(2,1)S(1)}, u32[]{:S(2)}, u32[]{:S(2)}) %collective-permute-start.3) | collective-permute-done | bytes 663584 | tf_op jit(solution)/shard_map/ppermute | solution.py:555
  77.2 13.2 %collective-permute-done.5 = bf16[2,4,6912]{2,1,0:T(4,128)(2,1)S(1)} collective-permute-done((bf16[2,4,6912]{2,1,0:T(4,128)(2,1)S(1)}, bf16[2,4,6912]{2,1,0:T(4,128)(2,1)S(1)}, u32[]{:S(2)}, u32[]{:S(2)}) %collective-permute-start.5) | collective-permute-done | bytes 110624 | tf_op jit(solution)/shard_map/ppermute | solution.py:555
  94.3 5.7 collective-permute-done.6
  100.7 25.5 %collective-permute-done.7.refs_1_ = bf16[4,144,1152]{2,1,0:T(8,128)(2,1)} collective-permute-done((bf16[4,144,1152]{2,1,0:T(8,128)(2,1)S(1)}, bf16[4,144,1152]{2,1,0:T(8,128)(2,1)}, u32[]{:S(2)}, u32[]{:S(2)}) %collective-permute-start.7) | collective-permute-done | bytes 1327136 | tf_op jit(solution)/shard_map/ppermute | solution.py:555
  128.8 17.6 %qkv.1 = (bf16[1024,1152]{1,0:T(8,128)(2,1)}, bf16[1024,3456]{1,0:T(8,128)(2,1)}) custom-call(s32[6]{0:T(128)} %pad_add_fusion.scal_ref.scal, bf16[1024,1152]{1,0:T(8,128)(2,1)} %get-tuple-element.223.refs_0_.refs_1_.refs_2_, f32[4,6,1152]{2,1,0:T(8,128)} %broadcast_add_fusion.refs_1_.refs_3_.refs_7_.refs_5_.refs_4_, f32[1,3456]{1,0:T(1,128)} %fusion.31.refs_2_, ...), custom_call_target="tpu_custom_call" | custom-call | flops 8153726976 | bytes 23068672 | tf_op jit(solution)/shard_map/qkv/pallas_call | solution.py:89
  146.4 15.6 %attend.1 = (bf16[1024,1152]{1,0:T(8,128)(2,1)}, f32[1024,128]{1,0:T(8,128)}) custom-call(s32[6]{0:T(128)} %pad_add_fusion.scal_ref.scal, bf16[1024,3456]{1,0:T(8,128)(2,1)} %get-tuple-element.302.refs_0_.refs_1_, f32[4,1,256]{2,1,0:T(1,128)} %get-tuple-element.304.refs_1_.refs_3_, f32[16,256,256]{2,1,0:T(8,128)} %bias.1.refs_2_.refs_4_), custom_call_target="tpu_custom_call" | custom-call | flops 4294967296 | bytes 15728640 | tf_op jit(solution)/shard_map/attend/pallas_call | solution.py:89
  162.0 6.7 %collective-permute-done.9.refs_3_ = bf16[4,144,1152]{2,1,0:T(8,128)(2,1)S(1)} collective-permute-done((bf16[4,144,1152]{2,1,0:T(8,128)(2,1)}, bf16[4,144,1152]{2,1,0:T(8,128)(2,1)S(1)}, u32[]{:S(2)}, u32[]{:S(2)}) %collective-permute-start.9) | collective-permute-done | bytes 1327136 | tf_op jit(solution)/shard_map/ppermute | solution.py:555
  170.2 11.7 %merge.1 = (bf16[1024,1152]{1,0:T(8,128)(2,1)}, f32[1024,1152]{1,0:T(8,128)}, bf16[1024,1152]{1,0:T(8,128)(2,1)}, bf16[1024,1152]{1,0:T(8,128)(2,1)}, f32[1,1152]{1,0:T(1,128)}) custom-call(s32[6]{0:T(128)} %pad_add_fusion.scal_ref.scal, bf16[1024,1152]{1,0:T(8,128)(2,1)} %get-tuple-element.222.refs_0_.refs_2_.refs_3_, ...), custom_call_target="tpu_custom_call" | custom-call | flops 2717908992 | bytes 20971520 | tf_op jit(solution)/shard_map/merge/pallas_call | solution.py:89
  183.0 16.8 %up.2 = (bf16[2,1024,1152]{2,1,0:T(8,128)(2,1)}, bf16[2,1024,1152]{2,1,0:T(8,128)(2,1)}, bf16[2,1152,1152]{2,1,0:T(8,128)(2,1)}) custom-call(s32[6]{0:T(128)} %pad_add_fusion.scal_ref.scal, s32[2]{0:T(128)} %pad_add_fusion.3.quarters, bf16[1024,1152]{1,0:T(8,128)(2,1)} %get-tuple-element.239.h2.refs_0_, f32[1,4608]{1,0:T(1,128)} %reshape.241.bias, ...), custom_call_target="tpu_custom_call" | custom-call | flops 5435817984 | bytes 24772608 | tf_op jit(solution)/shard_map/up/pallas_call | solution.py:277
  201.3 16.7 %up.3 = (bf16[2,1024,1152]{2,1,0:T(8,128)(2,1)}, bf16[2,1024,1152]{2,1,0:T(8,128)(2,1)}, bf16[2,1152,1152]{2,1,0:T(8,128)(2,1)}) custom-call(s32[6]{0:T(128)} %pad_add_fusion.scal_ref.scal, s32[2]{0:T(128)} %pad_add_fusion.2.quarters, bf16[1024,1152]{1,0:T(8,128)(2,1)} %get-tuple-element.239.h2.refs_0_, f32[1,4608]{1,0:T(1,128)} %reshape.241.bias, ...), custom_call_target="tpu_custom_call" | custom-call | flops 5435817984 | bytes 24772608 | tf_op jit(solution)/shard_map/up/pallas_call | solution.py:277
  218.7 20.2 %down_outer.1 = (bf16[2,144,1152]{2,1,0:T(8,128)(2,1)}, bf16[2,144,1152]{2,1,0:T(8,128)(2,1)}, bf16[2,144,1152]{2,1,0:T(8,128)(2,1)}, bf16[2,144,1152]{2,1,0:T(8...) custom-call(s32[6]{0:T(128)} %pad_add_fusion.scal_ref.scal, ...), custom_call_target="tpu_custom_call" | custom-call | flops 10871635968 | bytes 14155776 | tf_op jit(solution)/shard_map/down_outer/pallas_call | solution.py:533
  238.8 12.7 %act_back.2 = (bf16[2,1024,1152]{2,1,0:T(8,128)(2,1)}, f32[1,4608]{1,0:T(1,128)}) custom-call(s32[6]{0:T(128)} %pad_add_fusion.scal_ref.scal, s32[2]{0:T(128)} %pad_add_fusion.3.quarters, bf16[1024,1152]{1,0:T(8,128)(2,1)} %get-tuple-element.259.refs_0_.gm, bf16[2,1024,1152]{2,1,0:T(8,128)(2,1)} %get-tuple-element.255.slope, bf16[4,1152,1152]{2,1,0:T(8,128)(2,1)} %bitcast.140), custom_call_target="tpu_custom_call" | custom-call | flops 5435817984 | bytes 14745600 | tf_op jit(solution)/shard_map/act_back/pallas_call | solution.py:308
  253.2 12.5 %act_back.3 = (bf16[2,1024,1152]{2,1,0:T(8,128)(2,1)}, f32[1,4608]{1,0:T(1,128)}) custom-call(s32[6]{0:T(128)} %pad_add_fusion.scal_ref.scal, s32[2]{0:T(128)} %pad_add_fusion.2.quarters, bf16[1024,1152]{1,0:T(8,128)(2,1)} %get-tuple-element.259.refs_0_.gm, bf16[2,1024,1152]{2,1,0:T(8,128)(2,1)} %get-tuple-element.260.slope, ...), custom_call_target="tpu_custom_call", output_to_operand_aliasing={{1}: (5, {})} | custom-call | flops 5435817984 | bytes 14745600 | tf_op jit(solution)/shard_map/act_back/pallas_call | solution.py:308
  265.7 3.0 collective-permute-done.17
  270.4 20.3 %up_outer.1 = (bf16[2,144,1152]{2,1,0:T(8,128)(2,1)}, bf16[2,144,1152]{2,1,0:T(8,128)(2,1)}, bf16[2,144,1152]{2,1,0:T(8,128)(2,1)}, bf16[2,144,1152]{2,1,0:T(8,1...) custom-call(s32[6]{0:T(128)} %pad_add_fusion.scal_ref.scal, ...), custom_call_target="tpu_custom_call" | custom-call | flops 10871635968 | bytes 14155776 | tf_op jit(solution)/shard_map/up_outer/pallas_call | solution.py:533
  296.7 25.8 %mid_back.1 = (f32[1024,1152]{1,0:T(8,128)}, bf16[1024,1152]{1,0:T(8,128)(2,1)}, f32[1,1152]{1,0:T(1,128)}, f32[4,3,1152]{2,1,0:T(4,128)}) custom-call(s32[6]{0:T(128)} %pad_add_fusion.scal_ref.scal, s32[4]{0:T(128)} %pad_add_fusion.1.quarters_ref, bf16[2,1024,1152]{2,1,0:T(8,128)(2,1)} %get-tuple-element.273.refs_2_.refs_0_, ...), custom_call_target="tpu_custom_call" | custom-call | flops 10871635968 | bytes 31850496 | tf_op jit(solution)/shard_map/mid_back/pallas_call | solution.py:363
  322.6 2.7 add_convert_fusion.7
  327.4 2.0 collective-permute-start.23
  330.3 24.1 %attend_back.2 = (bf16[512,4608]{1,0:T(8,128)(2,1)}, f32[1,3456]{1,0:T(1,128)}, f32[16,256,256]{2,1,0:T(8,128)}) custom-call(s32[6]{0:T(128)} %pad_add_fusion.scal_ref.scal, bf16[1024,1152]{1,0:T(8,128)(2,1)} %get-tuple-element.301.refs_0_, bf16[1024,3456]{1,0:T(8,128)(2,1)} %get-tuple-element.302.refs_0_.refs_1_, f32[1024,128]{1,0:T(8,128)} %get-tuple-element.303.refs_2_, ...), custom_call_target="tpu_custom_call" | custom-call | flops 6727663616 | bytes 20971520 | tf_op jit(solution)/shard_map/attend_back/pallas_call | solution.py:89
  356.8 2.1 add_convert_fusion.15
  358.9 2.6 collective-permute-start.26
  363.3 1.8 collective-permute-start.29
  365.1 24.2 %attend_back.3 = (bf16[512,4608]{1,0:T(8,128)(2,1)}, f32[1,3456]{1,0:T(1,128)}, f32[16,256,256]{2,1,0:T(8,128)}) custom-call(s32[6]{0:T(128)} %pad_add_fusion.scal_ref.scal, bf16[1024,1152]{1,0:T(8,128)(2,1)} %get-tuple-element.301.refs_0_, bf16[1024,3456]{1,0:T(8,128)(2,1)} %get-tuple-element.302.refs_0_.refs_1_, f32[1024,128]{1,0:T(8,128)} %get-tuple-element.303.refs_2_, ...), custom_call_target="tpu_custom_call" | custom-call | flops 6727663616 | bytes 20971520 | tf_op jit(solution)/shard_map/attend_back/pallas_call | solution.py:89
  391.5 2.5 reshape.232
  394.0 2.0 copy.85
  397.5 2.4 add_convert_fusion.4
  400.7 15.4 %joint_give.1 = (bf16[8,144,768]{2,1,0:T(8,128)(2,1)}, bf16[8,144,768]{2,1,0:T(8,128)(2,1)}, bf16[8,144,768]{2,1,0:T(8,128)(2,1)}) custom-call(s32[6]{0:T(128)} %pad_add_fusion.scal_ref.scal, s32[3]{0:T(128)} %get-tuple-element.418.blocks, bf16[1024,1152]{1,0:T(8,128)(2,1)} %get-tuple-element.245.refs_0_.refs_1_, ...), custom_call_target="tpu_custom_call" | custom-call | flops 5435817984 | bytes 9437184 | tf_op jit(solution)/shard_map/joint_give/pallas_call | solution.py:533
  418.3 15.0 %joint_keep.1 = (bf16[8,144,768]{2,1,0:T(8,128)(2,1)}, bf16[8,144,768]{2,1,0:T(8,128)(2,1)}, bf16[8,144,768]{2,1,0:T(8,128)(2,1)}) custom-call(s32[6]{0:T(128)} %pad_add_fusion.scal_ref.scal, s32[3]{0:T(128)} %get-tuple-element.417.blocks, bf16[1024,1152]{1,0:T(8,128)(2,1)} %get-tuple-element.245.refs_0_.refs_1_, ...), custom_call_target="tpu_custom_call" | custom-call | flops 5435817984 | bytes 9437184 | tf_op jit(solution)/shard_map/joint_keep/pallas_call | solution.py:533
  436.2 1.8 maximum_convert_fusion.1
  438.3 3.1 add_convert_fusion.1
  442.2 5.9 strips.1
  448.1 4.2 reshape.227
  452.3 2.3 add_convert_fusion
  456.7 2.3 collective-permute-start.40
  459.1 5.6 convolution_bitcast_fusion.1
  465.7 14.7 %down.2 = (bf16[1024,1152]{1,0:T(8,128)(2,1)}, f32[4,1,1152]{2,1,0:T(1,128)}) custom-call(s32[6]{0:T(128)} %pad_add_fusion.scal_ref.scal, s32[4]{0:T(128)} %pad_add_fusion.1.quarters_ref, bf16[2,1024,1152]{2,1,0:T(8,128)(2,1)} %get-tuple-element.338.refs_2_.refs_0_, bf16[2,1024,1152]{2,1,0:T(8,128)(2,1)} %get-tuple-element.339.refs_1_, ...), custom_call_target="tpu_custom_call" | custom-call | flops 5435817984 | bytes 21233664 | tf_op jit(solution)/shard_map/down/pallas_call | solution.py:363
  480.4 2.3 add_convert_fusion.11
  482.8 2.5 add_convert_fusion.2
  488.1 14.6 %down.3 = (bf16[1024,1152]{1,0:T(8,128)(2,1)}, f32[4,1,1152]{2,1,0:T(1,128)}) custom-call(s32[6]{0:T(128)} %pad_add_fusion.scal_ref.scal, s32[4]{0:T(128)} %pad_add_fusion.1.quarters_ref, bf16[2,1024,1152]{2,1,0:T(8,128)(2,1)} %get-tuple-element.338.refs_2_.refs_0_, ...), custom_call_target="tpu_custom_call", output_to_operand_aliasing={{0}: (10, {}), {1}: (11, {})} | custom-call | flops 5435817984 | bytes 21233664 | tf_op jit(solution)/shard_map/down/pallas_call | solution.py:363
  503.4 2.1 add_convert_fusion.20
  505.5 2.0 collective-permute-done.38
  507.5 2.1 add_convert_fusion.10
  509.6 2.1 collective-permute-start.42
  512.2 14.8 %front_back.2 = (f32[1024,1152]{1,0:T(8,128)}, f32[4,2,1152]{2,1,0:T(2,128)}) custom-call(s32[6]{0:T(128)} %pad_add_fusion.scal_ref.scal, s32[3]{0:T(128)} %bitcast.158, bf16[512,4608]{1,0:T(8,128)(2,1)} %get-tuple-element.349.refs_4_.refs_0_, bf16[4,1152,1152]{2,1,0:T(8,128)(2,1)} %bitcast.138, ...), custom_call_target="tpu_custom_call" | custom-call | flops 4076863488 | bytes 17399808 | tf_op jit(solution)/shard_map/front_back/pallas_call | solution.py:363
  526.9 3.5 collective-permute-done.42
  533.8 2.9 collective-permute-start.44
  536.7 1.7 collective-permute-start.45
  538.4 14.9 %front_back.3 = (f32[1024,1152]{1,0:T(8,128)}, f32[4,2,1152]{2,1,0:T(2,128)}) custom-call(s32[6]{0:T(128)} %pad_add_fusion.scal_ref.scal, s32[3]{0:T(128)} %bitcast.159, bf16[512,4608]{1,0:T(8,128)(2,1)} %get-tuple-element.352.refs_5_.refs_0_, bf16[4,1152,1152]{2,1,0:T(8,128)(2,1)} %bitcast.139, ...), custom_call_target="tpu_custom_call", output_to_operand_aliasing={{0}: (8, {}), {1}: (9, {})} | custom-call | flops 4076863488 | bytes 17399808 | tf_op jit(solution)/shard_map/front_back/pallas_call | solution.py:363
  559.0 1.8 maximum_convert_fusion
  560.9 5.4 collective-permute-done.46
  566.5 2.1 reduce_sum.18
  569.7 3.1 collective-permute-done.50
  575.1 4.6 collective-permute-done.51
  591.4 6.4 %collective-permute-done.53 = bf16[64,3456]{1,0:T(8,128)(2,1)S(1)} collective-permute-done((bf16[64,3456]{1,0:T(8,128)(2,1)}, bf16[64,3456]{1,0:T(8,128)(2,1)S(1)}, u32[]{:S(2)}, u32[]{:S(2)}) %collective-permute-start.53) | collective-permute-done | bytes 442400 | tf_op jit(solution)/shard_map/ppermute | solution.py:555
  601.5 2.7 fusion.16
  (304 shorter events, 85.7 us)
Async XLA Ops:
  7.2 119.0 %all-gather.11.cloned.1.call-start = ((), (), s32[]{:S(2)}) async-start(), calls=%async_computation.2 | async-start | bytes 10948608 | tf_op jit(solution)/shard_map/all_gather | solution.py:640
  9.2 229.6 %all-gather.13.cloned.1.call-start = ((), (), s32[]{:S(2)}) async-start(), calls=%async_computation.3 | async-start | bytes 10948608 | tf_op jit(solution)/shard_map/all_gather | solution.py:640
  12.4 26.2 %collective-permute-start = (bf16[1,144,1152]{2,1,0:T(8,128)(2,1)S(1)}, bf16[1,144,1152]{2,1,0:T(8,128)(2,1)}, u32[]{:S(2)}, u32[]{:S(2)}) collective-permute-start(bf16[1,144,1152]{2,1,0:T(8,128)(2,1)S(1)} %dynamic-slice_bitcast_fusion), channel_id=1, source_target_pairs={{0,4},{1,5},{2,6},{3,7},{4,0},{5,1},{6,2},{7,3},{8,12},{9,13},{10,... | collective-permute-start | bytes 995336 | tf_op jit(solution)/shard_map/ppermute | solution.py:555
  16.5 22.0 %collective-permute-start.1 = (bf16[32,144]{1,0:T(8,128)(2,1)S(1)}, bf16[32,144]{1,0:T(8,128)(2,1)S(1)}, u32[]{:S(2)}, u32[]{:S(2)}) collective-permute-start(bf16[32,144]{1,0:T(8,128)(2,1)S(1)} %constant_dynamic-slice_fusion.1), channel_id=1, source_target_pairs={{0,8},{8,0},{16,24},{24,16},{1,9},{9,1},{17,25},{25,17},{2,10},{10... | collective-permute-start | bytes 27656 | tf_op jit(solution)/shard_map/ppermute | solution.py:555
  25.3 366.1 %all-gather.7.cloned.1.call-start = ((), (), s32[]{:S(2)}) async-start(), calls=%async_computation | async-start | bytes 1216512 | tf_op jit(solution)/shard_map/all_gather | solution.py:867
  39.6 14.8 %collective-permute-start.2 = (bf16[4,4,6912]{2,1,0:T(4,128)(2,1)S(1)}, bf16[4,4,6912]{2,1,0:T(4,128)(2,1)S(1)}, u32[]{:S(2)}, u32[]{:S(2)}) collective-permute-start(bf16[4,4,6912]{2,1,0:T(4,128)(2,1)S(1)} %fusion.6), channel_id=1, source_target_pairs={{0,1},{1,0},{2,3},{3,2},{4,5},{5,4},{6,7},{7,6},{8,9},{9,8},{10,11... | collective-permute-start | bytes 663560 | tf_op jit(solution)/shard_map/ppermute | solution.py:555
  51.5 24.6 %collective-permute-start.3 = (bf16[2,144,1152]{2,1,0:T(8,128)(2,1)S(1)}, bf16[2,144,1152]{2,1,0:T(8,128)(2,1)S(1)}, u32[]{:S(2)}, u32[]{:S(2)}) collective-permute-start(bf16[2,144,1152]{2,1,0:T(8,128)(2,1)S(1)} %pad_maximum_fusion.4), channel_id=1, source_target_pairs={{0,2},{1,3},{2,0},{3,1},{4,6},{5,7},{6,4},{7,5},{8,10},{9,11},{10,... | collective-permute-start | bytes 1990664 | tf_op jit(solution)/shard_map/ppermute | solution.py:555
  52.9 23.3 %collective-permute-start.4 = (bf16[64,144]{1,0:T(8,128)(2,1)S(1)}, bf16[64,144]{1,0:T(8,128)(2,1)S(1)}, u32[]{:S(2)}, u32[]{:S(2)}) collective-permute-start(bf16[64,144]{1,0:T(8,128)(2,1)S(1)} %pad_maximum_fusion.13), channel_id=1, source_target_pairs={{0,16},{8,24},{16,0},{24,8},{1,17},{9,25},{17,1},{25,9},{2,18},{10... | collective-permute-start | bytes 55304 | tf_op jit(solution)/shard_map/ppermute | solution.py:555
  54.7 36.6 %copy-start.31 = (bf16[6912]{0:T(1024)(128)(2,1)S(1)}, bf16[6912]{0:T(1024)(128)(2,1)}, u32[]{:S(2)}) copy-start(bf16[6912]{0:T(1024)(128)(2,1)} %param.32) | copy-start | bytes 41476
  54.7 73.6 %copy-start.37 = (bf16[1152]{0:T(1024)(128)(2,1)S(1)}, bf16[1152]{0:T(1024)(128)(2,1)}, u32[]{:S(2)}) copy-start(bf16[1152]{0:T(1024)(128)(2,1)} %param.26) | copy-start | bytes 6916
  76.2 70.2 %copy-start.8 = (bf16[4,144,1152]{2,1,0:T(8,128)(2,1)}, bf16[4,144,1152]{2,1,0:T(8,128)(2,1)S(1)}, u32[]{:S(2)}) copy-start(bf16[4,144,1152]{2,1,0:T(8,128)(2,1)S(1)} %pad_maximum_fusion.refs_0_) | copy-start | bytes 3981316
  76.3 14.1 %collective-permute-start.5 = (bf16[2,4,6912]{2,1,0:T(4,128)(2,1)S(1)}, bf16[2,4,6912]{2,1,0:T(4,128)(2,1)S(1)}, u32[]{:S(2)}, u32[]{:S(2)}) collective-permute-start(bf16[2,4,6912]{2,1,0:T(4,128)(2,1)S(1)} %fusion.15), channel_id=1, source_target_pairs={{0,2},{1,3},{2,0},{3,1},{4,6},{5,7},{6,4},{7,5},{8,10},{9,11},{10,... | collective-permute-start | bytes 331784 | tf_op jit(solution)/shard_map/ppermute | solution.py:555
  90.5 9.4 %collective-permute-start.6 = (bf16[1,4,6912]{2,1,0:T(4,128)(2,1)S(1)}, bf16[1,4,6912]{2,1,0:T(4,128)(2,1)S(1)}, u32[]{:S(2)}, u32[]{:S(2)}) collective-permute-start(bf16[1,4,6912]{2,1,0:T(4,128)(2,1)S(1)} %fusion.22), channel_id=1, source_target_pairs={{0,4},{1,5},{2,6},{3,7},{4,0},{5,1},{6,2},{7,3},{8,12},{9,13},{10,... | collective-permute-start | bytes 165896 | tf_op jit(solution)/shard_map/ppermute | solution.py:555
  91.3 35.0 %collective-permute-start.7 = (bf16[4,144,1152]{2,1,0:T(8,128)(2,1)S(1)}, bf16[4,144,1152]{2,1,0:T(8,128)(2,1)}, u32[]{:S(2)}, u32[]{:S(2)}) collective-permute-start(bf16[4,144,1152]{2,1,0:T(8,128)(2,1)S(1)} %pad_maximum_fusion.refs_0_), channel_id=1, source_target_pairs={{0,1},{1,0},{2,3},{3,2},{4,5},{5,4},{6,7},{7,6},{8,9},{9,8},{10,11... | collective-permute-start | bytes 3981320 | tf_op jit(solution)/shard_map/ppermute | solution.py:555
  92.8 33.4 %collective-permute-start.8 = (bf16[4,144,1152]{2,1,0:T(8,128)(2,1)S(1)}, bf16[4,144,1152]{2,1,0:T(8,128)(2,1)}, u32[]{:S(2)}, u32[]{:S(2)}) collective-permute-start(bf16[4,144,1152]{2,1,0:T(8,128)(2,1)S(1)} %pad_maximum_fusion.refs_0_), channel_id=1, source_target_pairs={{0,16},{8,24},{16,0},{24,8},{1,17},{9,25},{17,1},{25,9},{2,18},{10... | collective-permute-start | bytes 3981320 | tf_op jit(solution)/shard_map/ppermute | solution.py:555
  126.2 42.4 %collective-permute-start.9 = (bf16[4,144,1152]{2,1,0:T(8,128)(2,1)}, bf16[4,144,1152]{2,1,0:T(8,128)(2,1)S(1)}, u32[]{:S(2)}, u32[]{:S(2)}) collective-permute-start(bf16[4,144,1152]{2,1,0:T(8,128)(2,1)} %collective-permute-done.7.refs_1_), channel_id=1, source_target_pairs={{0,16},{8,24},{16,0},{24,8},{1,17},{9,25},{17,1},{25,9},{2,18},{10... | collective-permute-start | bytes 3981320 | tf_op jit(solution)/shard_map/ppermute | solution.py:555
  127.7 40.9 %collective-permute-start.11 = (bf16[4,144,1152]{2,1,0:T(8,128)(2,1)}, bf16[4,144,1152]{2,1,0:T(8,128)(2,1)}, u32[]{:S(2)}, u32[]{:S(2)}) collective-permute-start(bf16[4,144,1152]{2,1,0:T(8,128)(2,1)} %collective-permute-done.7.refs_1_), channel_id=1, source_target_pairs={{0,8},{8,0},{16,24},{24,16},{1,9},{9,1},{17,25},{25,17},{2,10},{10... | collective-permute-start | bytes 3981320 | tf_op jit(solution)/shard_map/ppermute | solution.py:555
  127.7 40.9 %collective-permute-start.10 = (bf16[4,144,1152]{2,1,0:T(8,128)(2,1)S(1)}, bf16[4,144,1152]{2,1,0:T(8,128)(2,1)}, u32[]{:S(2)}, u32[]{:S(2)}) collective-permute-start(bf16[4,144,1152]{2,1,0:T(8,128)(2,1)S(1)} %pad_maximum_fusion.refs_0_), channel_id=1, source_target_pairs={{0,8},{8,0},{16,24},{24,16},{1,9},{9,1},{17,25},{25,17},{2,10},{10... | collective-permute-start | bytes 3981320 | tf_op jit(solution)/shard_map/ppermute | solution.py:555
  128.2 40.4 %collective-permute-start.12 = (bf16[4,144,1152]{2,1,0:T(8,128)(2,1)}, bf16[4,144,1152]{2,1,0:T(8,128)(2,1)}, u32[]{:S(2)}, u32[]{:S(2)}) collective-permute-start(bf16[4,144,1152]{2,1,0:T(8,128)(2,1)} %collective-permute-done.8.refs_2_), channel_id=1, source_target_pairs={{0,8},{8,0},{16,24},{24,16},{1,9},{9,1},{17,25},{25,17},{2,10},{10... | collective-permute-start | bytes 3981320 | tf_op jit(solution)/shard_map/ppermute | solution.py:555
  168.7 13.2 %collective-permute-start.13 = (bf16[4,144,1152]{2,1,0:T(8,128)(2,1)S(1)}, bf16[4,144,1152]{2,1,0:T(8,128)(2,1)S(1)}, u32[]{:S(2)}, u32[]{:S(2)}) collective-permute-start(bf16[4,144,1152]{2,1,0:T(8,128)(2,1)S(1)} %collective-permute-done.9.refs_3_), channel_id=1, source_target_pairs={{0,8},{8,0},{16,24},{24,16},{1,9},{9,1},{17,25},{25,17},{2,10},{10... | collective-permute-start | bytes 3981320 | tf_op jit(solution)/shard_map/ppermute | solution.py:555
  199.8 18.8 %collective-permute-start.15 = (bf16[2,1024,1152]{2,1,0:T(8,128)(2,1)}, bf16[2,1024,1152]{2,1,0:T(8,128)(2,1)}, u32[]{:S(2)}, u32[]{:S(2)}) collective-permute-start(bf16[2,1024,1152]{2,1,0:T(8,128)(2,1)} %get-tuple-element.339.refs_1_), channel_id=1, source_target_pairs={{0,8},{8,0},{16,24},{24,16},{1,9},{9,1},{17,25},{25,17},{2,10},{10... | collective-permute-start | bytes 14155784 | tf_op jit(solution)/shard_map/ppermute | solution.py:555
  200.2 17.8 %collective-permute-start.14 = (bf16[1024,1152]{1,0:T(8,128)(2,1)}, bf16[1024,1152]{1,0:T(8,128)(2,1)}, u32[]{:S(2)}, u32[]{:S(2)}) collective-permute-start(bf16[1024,1152]{1,0:T(8,128)(2,1)} %get-tuple-element.259.refs_0_.gm), channel_id=1, source_target_pairs={{0,8},{8,0},{16,24},{24,16},{1,9},{9,1},{17,25},{25,17},{2,10},{10... | collective-permute-start | bytes 7077896 | tf_op jit(solution)/shard_map/ppermute | solution.py:555
  200.4 18.3 %collective-permute-start.16 = (bf16[1024,1152]{1,0:T(8,128)(2,1)}, bf16[1024,1152]{1,0:T(8,128)(2,1)}, u32[]{:S(2)}, u32[]{:S(2)}) collective-permute-start(bf16[1024,1152]{1,0:T(8,128)(2,1)} %get-tuple-element.239.h2.refs_0_), channel_id=1, source_target_pairs={{0,8},{8,0},{16,24},{24,16},{1,9},{9,1},{17,25},{25,17},{2,10},{10... | collective-permute-start | bytes 7077896 | tf_op jit(solution)/shard_map/ppermute | solution.py:555
  251.5 17.5 %collective-permute-start.18 = (bf16[2,1024,1152]{2,1,0:T(8,128)(2,1)}, bf16[2,1024,1152]{2,1,0:T(8,128)(2,1)}, u32[]{:S(2)}, u32[]{:S(2)}) collective-permute-start(bf16[2,1024,1152]{2,1,0:T(8,128)(2,1)} %get-tuple-element.274.refs_1_), channel_id=1, source_target_pairs={{0,8},{8,0},{16,24},{24,16},{1,9},{9,1},{17,25},{25,17},{2,10},{10... | collective-permute-start | bytes 14155784 | tf_op jit(solution)/shard_map/ppermute | solution.py:555
  251.8 17.0 %collective-permute-start.17 = (bf16[2,144,1152]{2,1,0:T(8,128)(2,1)S(1)}, bf16[2,144,1152]{2,1,0:T(8,128)(2,1)S(1)}, u32[]{:S(2)}, u32[]{:S(2)}) collective-permute-start(bf16[2,144,1152]{2,1,0:T(8,128)(2,1)S(1)} %copy-done.43), channel_id=1, source_target_pairs={{0,16},{8,24},{16,0},{24,8},{1,17},{9,25},{17,1},{25,9},{2,18},{10... | collective-permute-start | bytes 1990664 | tf_op jit(solution)/shard_map/ppermute | solution.py:555
  269.0 21.8 %collective-permute-start.19 = (bf16[2,144,1152]{2,1,0:T(8,128)(2,1)S(1)}, bf16[2,144,1152]{2,1,0:T(8,128)(2,1)S(1)}, u32[]{:S(2)}, u32[]{:S(2)}) collective-permute-start(bf16[2,144,1152]{2,1,0:T(8,128)(2,1)S(1)} %copy-done.42), channel_id=1, source_target_pairs={{0,16},{8,24},{16,0},{24,8},{1,17},{9,25},{17,1},{25,9},{2,18},{10... | collective-permute-start | bytes 1990664 | tf_op jit(solution)/shard_map/ppermute | solution.py:555
  291.1 31.4 %collective-permute-start.21 = (bf16[4,144,1152]{2,1,0:T(8,128)(2,1)S(1)}, bf16[4,144,1152]{2,1,0:T(8,128)(2,1)S(1)}, u32[]{:S(2)}, u32[]{:S(2)}) collective-permute-start(bf16[4,144,1152]{2,1,0:T(8,128)(2,1)S(1)} %pad_maximum_fusion.1), channel_id=1, source_target_pairs={{0,1},{1,0},{2,3},{3,2},{4,5},{5,4},{6,7},{7,6},{8,9},{9,8},{10,11... | collective-permute-start | bytes 3981320 | tf_op jit(solution)/shard_map/ppermute | solution.py:555
  294.6 27.9 %collective-permute-start.20 = (bf16[2,144,1152]{2,1,0:T(8,128)(2,1)}, bf16[2,144,1152]{2,1,0:T(8,128)(2,1)}, u32[]{:S(2)}, u32[]{:S(2)}) collective-permute-start(bf16[2,144,1152]{2,1,0:T(8,128)(2,1)} %get-tuple-element.282), channel_id=1, source_target_pairs={{0,16},{8,24},{16,0},{24,8},{1,17},{9,25},{17,1},{25,9},{2,18},{10... | collective-permute-start | bytes 1990664 | tf_op jit(solution)/shard_map/ppermute | solution.py:555
  295.3 29.9 %collective-permute-start.22 = (bf16[2,144,1152]{2,1,0:T(8,128)(2,1)}, bf16[2,144,1152]{2,1,0:T(8,128)(2,1)}, u32[]{:S(2)}, u32[]{:S(2)}) collective-permute-start(bf16[2,144,1152]{2,1,0:T(8,128)(2,1)} %get-tuple-element.286), channel_id=1, source_target_pairs={{0,16},{8,24},{16,0},{24,8},{1,17},{9,25},{17,1},{25,9},{2,18},{10... | collective-permute-start | bytes 1990664 | tf_op jit(solution)/shard_map/ppermute | solution.py:555
  322.5 31.9 %copy-start.9 = (bf16[4,144,1152]{2,1,0:T(8,128)(2,1)}, bf16[4,144,1152]{2,1,0:T(8,128)(2,1)S(1)}, u32[]{:S(2)}) copy-start(bf16[4,144,1152]{2,1,0:T(8,128)(2,1)S(1)} %collective-permute-done.21) | copy-start | bytes 3981316
  325.2 29.2 %collective-permute-start.25 = (bf16[2,144,1152]{2,1,0:T(8,128)(2,1)}, bf16[2,144,1152]{2,1,0:T(8,128)(2,1)S(1)}, u32[]{:S(2)}, u32[]{:S(2)}) collective-permute-start(bf16[2,144,1152]{2,1,0:T(8,128)(2,1)} %get-tuple-element.299), channel_id=1, source_target_pairs={{0,16},{8,24},{16,0},{24,8},{1,17},{9,25},{17,1},{25,9},{2,18},{10... | collective-permute-start | bytes 1990664 | tf_op jit(solution)/shard_map/ppermute | solution.py:555
  327.3 239.1 %all-gather.9.cloned.1.call-start = ((), (), s32[]{:S(2)}) async-start(), calls=%async_computation.1 | async-start | bytes 3379200 | tf_op jit(solution)/shard_map/all_gather | solution.py:912
  327.4 27.1 %copy-start.15 = (bf16[2,144,1152]{2,1,0:T(8,128)(2,1)S(1)}, bf16[2,144,1152]{2,1,0:T(8,128)(2,1)}, u32[]{:S(2)}) copy-start(bf16[2,144,1152]{2,1,0:T(8,128)(2,1)} %get-tuple-element.298) | copy-start | bytes 1990660
  327.4 28.4 %collective-permute-start.23 = (bf16[2,144,1152]{2,1,0:T(8,128)(2,1)}, bf16[2,144,1152]{2,1,0:T(8,128)(2,1)}, u32[]{:S(2)}, u32[]{:S(2)}) collective-permute-start(bf16[2,144,1152]{2,1,0:T(8,128)(2,1)} %add_convert_fusion.7), channel_id=1, source_target_pairs={{0,2},{1,3},{2,0},{3,1},{4,6},{5,7},{6,4},{7,5},{8,10},{9,11},{10,... | collective-permute-start | bytes 1990664 | tf_op jit(solution)/shard_map/ppermute | solution.py:555
  329.4 25.8 %collective-permute-start.24 = (bf16[2,144,1152]{2,1,0:T(8,128)(2,1)}, bf16[2,144,1152]{2,1,0:T(8,128)(2,1)S(1)}, u32[]{:S(2)}, u32[]{:S(2)}) collective-permute-start(bf16[2,144,1152]{2,1,0:T(8,128)(2,1)} %get-tuple-element.297), channel_id=1, source_target_pairs={{0,16},{8,24},{16,0},{24,8},{1,17},{9,25},{17,1},{25,9},{2,18},{10... | collective-permute-start | bytes 1990664 | tf_op jit(solution)/shard_map/ppermute | solution.py:555
  358.9 30.5 %copy-start.32 = (f32[1,3456]{1,0:T(1,128)S(1)}, f32[1,3456]{1,0:T(1,128)}, u32[]{:S(2)}) copy-start(f32[1,3456]{1,0:T(1,128)} %get-tuple-element.364) | copy-start | bytes 41476
  358.9 37.1 %collective-permute-start.26 = (bf16[1,144,1152]{2,1,0:T(8,128)(2,1)}, bf16[1,144,1152]{2,1,0:T(8,128)(2,1)}, u32[]{:S(2)}, u32[]{:S(2)}) collective-permute-start(bf16[1,144,1152]{2,1,0:T(8,128)(2,1)} %add_convert_fusion.15), channel_id=1, source_target_pairs={{0,4},{1,5},{2,6},{3,7},{4,0},{5,1},{6,2},{7,3},{8,12},{9,13},{10,... | collective-permute-start | bytes 995336 | tf_op jit(solution)/shard_map/ppermute | solution.py:555
  361.5 36.0 %collective-permute-start.27 = (bf16[2,144,1152]{2,1,0:T(8,128)(2,1)}, bf16[2,144,1152]{2,1,0:T(8,128)(2,1)}, u32[]{:S(2)}, u32[]{:S(2)}) collective-permute-start(bf16[2,144,1152]{2,1,0:T(8,128)(2,1)} %get-tuple-element.310), channel_id=1, source_target_pairs={{0,16},{8,24},{16,0},{24,8},{1,17},{9,25},{17,1},{25,9},{2,18},{10... | collective-permute-start | bytes 1990664 | tf_op jit(solution)/shard_map/ppermute | solution.py:555
  362.5 35.0 %collective-permute-start.28 = (bf16[4,144,1152]{2,1,0:T(8,128)(2,1)S(1)}, bf16[4,144,1152]{2,1,0:T(8,128)(2,1)}, u32[]{:S(2)}, u32[]{:S(2)}) collective-permute-start(bf16[4,144,1152]{2,1,0:T(8,128)(2,1)S(1)} %pad_maximum_fusion.2), channel_id=1, source_target_pairs={{0,1},{1,0},{2,3},{3,2},{4,5},{5,4},{6,7},{7,6},{8,9},{9,8},{10,11... | collective-permute-start | bytes 3981320 | tf_op jit(solution)/shard_map/ppermute | solution.py:555
  363.3 36.6 %collective-permute-start.29 = (bf16[2,144,1152]{2,1,0:T(8,128)(2,1)}, bf16[2,144,1152]{2,1,0:T(8,128)(2,1)}, u32[]{:S(2)}, u32[]{:S(2)}) collective-permute-start(bf16[2,144,1152]{2,1,0:T(8,128)(2,1)} %get-tuple-element.312), channel_id=1, source_target_pairs={{0,16},{8,24},{16,0},{24,8},{1,17},{9,25},{17,1},{25,9},{2,18},{10... | collective-permute-start | bytes 1990664 | tf_op jit(solution)/shard_map/ppermute | solution.py:555
  399.9 16.2 %collective-permute-start.30 = (bf16[1,144,1152]{2,1,0:T(8,128)(2,1)S(1)}, bf16[1,144,1152]{2,1,0:T(8,128)(2,1)S(1)}, u32[]{:S(2)}, u32[]{:S(2)}) collective-permute-start(bf16[1,144,1152]{2,1,0:T(8,128)(2,1)S(1)} %add_convert_fusion.14), channel_id=1, source_target_pairs={{0,8},{8,0},{16,24},{24,16},{1,9},{9,1},{17,25},{25,17},{2,10},{10... | collective-permute-start | bytes 995336 | tf_op jit(solution)/shard_map/ppermute | solution.py:555
  400.2 33.1 %collective-permute-start.33 = (bf16[2,144,1152]{2,1,0:T(8,128)(2,1)}, bf16[2,144,1152]{2,1,0:T(8,128)(2,1)S(1)}, u32[]{:S(2)}, u32[]{:S(2)}) collective-permute-start(bf16[2,144,1152]{2,1,0:T(8,128)(2,1)} %add_convert_fusion.4), channel_id=1, source_target_pairs={{0,2},{1,3},{2,0},{3,1},{4,6},{5,7},{6,4},{7,5},{8,10},{9,11},{10,... | collective-permute-start | bytes 1990664 | tf_op jit(solution)/shard_map/ppermute | solution.py:555
  416.2 21.8 %collective-permute-start.32 = (bf16[8,144,768]{2,1,0:T(8,128)(2,1)}, bf16[8,144,768]{2,1,0:T(8,128)(2,1)}, u32[]{:S(2)}, u32[]{:S(2)}) collective-permute-start(bf16[8,144,768]{2,1,0:T(8,128)(2,1)} %get-tuple-element.326), channel_id=1, source_target_pairs={{0,8},{8,0},{16,24},{24,16},{1,9},{9,1},{17,25},{25,17},{2,10},{10... | collective-permute-start | bytes 5308424 | tf_op jit(solution)/shard_map/ppermute | solution.py:555
  416.3 25.0 %collective-permute-start.31 = (bf16[8,144,768]{2,1,0:T(8,128)(2,1)}, bf16[8,144,768]{2,1,0:T(8,128)(2,1)S(1)}, u32[]{:S(2)}, u32[]{:S(2)}) collective-permute-start(bf16[8,144,768]{2,1,0:T(8,128)(2,1)} %get-tuple-element.322), channel_id=1, source_target_pairs={{0,8},{8,0},{16,24},{24,16},{1,9},{9,1},{17,25},{25,17},{2,10},{10... | collective-permute-start | bytes 5308424 | tf_op jit(solution)/shard_map/ppermute | solution.py:555
  416.8 24.5 %collective-permute-start.34 = (bf16[8,144,768]{2,1,0:T(8,128)(2,1)}, bf16[8,144,768]{2,1,0:T(8,128)(2,1)}, u32[]{:S(2)}, u32[]{:S(2)}) collective-permute-start(bf16[8,144,768]{2,1,0:T(8,128)(2,1)} %get-tuple-element.329), channel_id=1, source_target_pairs={{0,8},{8,0},{16,24},{24,16},{1,9},{9,1},{17,25},{25,17},{2,10},{10... | collective-permute-start | bytes 5308424 | tf_op jit(solution)/shard_map/ppermute | solution.py:555
  416.9 18.0 %collective-permute-start.49 = (bf16[2,144,1152]{2,1,0:T(8,128)(2,1)S(1)}, bf16[2,144,1152]{2,1,0:T(8,128)(2,1)}, u32[]{:S(2)}, u32[]{:S(2)}) collective-permute-start(bf16[2,144,1152]{2,1,0:T(8,128)(2,1)S(1)} %pad_maximum_fusion.5), channel_id=1, source_target_pairs={{0,16},{8,24},{16,0},{24,8},{1,17},{9,25},{17,1},{25,9},{2,18},{10... | collective-permute-start | bytes 1990664 | tf_op jit(solution)/shard_map/ppermute | solution.py:555
  441.3 41.4 %collective-permute-start.35 = (bf16[4,144,768]{2,1,0:T(8,128)(2,1)}, bf16[4,144,768]{2,1,0:T(8,128)(2,1)}, u32[]{:S(2)}, u32[]{:S(2)}) collective-permute-start(bf16[4,144,768]{2,1,0:T(8,128)(2,1)} %get-tuple-element.330), channel_id=1, source_target_pairs={{0,16},{8,24},{16,0},{24,8},{1,17},{9,25},{17,1},{25,9},{2,18},{10... | collective-permute-start | bytes 2654216 | tf_op jit(solution)/shard_map/ppermute | solution.py:555
  454.6 25.8 %collective-permute-start.36 = (bf16[4,144,768]{2,1,0:T(8,128)(2,1)}, bf16[4,144,768]{2,1,0:T(8,128)(2,1)}, u32[]{:S(2)}, u32[]{:S(2)}) collective-permute-start(bf16[4,144,768]{2,1,0:T(8,128)(2,1)} %add_convert_fusion), channel_id=1, source_target_pairs={{0,1},{1,0},{2,3},{3,2},{4,5},{5,4},{6,7},{7,6},{8,9},{9,8},{10,11... | collective-permute-start | bytes 2654216 | tf_op jit(solution)/shard_map/ppermute | solution.py:555
  455.9 49.6 %collective-permute-start.37 = (bf16[4,144,768]{2,1,0:T(8,128)(2,1)}, bf16[4,144,768]{2,1,0:T(8,128)(2,1)}, u32[]{:S(2)}, u32[]{:S(2)}) collective-permute-start(bf16[4,144,768]{2,1,0:T(8,128)(2,1)} %get-tuple-element.342), channel_id=1, source_target_pairs={{0,16},{8,24},{16,0},{24,8},{1,17},{9,25},{17,1},{25,9},{2,18},{10... | collective-permute-start | bytes 2654216 | tf_op jit(solution)/shard_map/ppermute | solution.py:555
  456.7 29.7 %collective-permute-start.40 = (bf16[1,144,1152]{2,1,0:T(8,128)(2,1)S(1)}, bf16[1,144,1152]{2,1,0:T(8,128)(2,1)}, u32[]{:S(2)}, u32[]{:S(2)}) collective-permute-start(bf16[1,144,1152]{2,1,0:T(8,128)(2,1)S(1)} %add_convert_fusion.13), channel_id=1, source_target_pairs={{0,4},{1,5},{2,6},{3,7},{4,0},{5,1},{6,2},{7,3},{8,12},{9,13},{10,... | collective-permute-start | bytes 995336 | tf_op jit(solution)/shard_map/ppermute | solution.py:555
  485.3 22.2 %collective-permute-start.38 = (bf16[4,144,768]{2,1,0:T(8,128)(2,1)}, bf16[4,144,768]{2,1,0:T(8,128)(2,1)}, u32[]{:S(2)}, u32[]{:S(2)}) collective-permute-start(bf16[4,144,768]{2,1,0:T(8,128)(2,1)} %add_convert_fusion.2), channel_id=1, source_target_pairs={{0,1},{1,0},{2,3},{3,2},{4,5},{5,4},{6,7},{7,6},{8,9},{9,8},{10,11... | collective-permute-start | bytes 2654216 | tf_op jit(solution)/shard_map/ppermute | solution.py:555
  487.9 15.6 %collective-permute-start.39 = (bf16[2,144,768]{2,1,0:T(8,128)(2,1)}, bf16[2,144,768]{2,1,0:T(8,128)(2,1)}, u32[]{:S(2)}, u32[]{:S(2)}) collective-permute-start(bf16[2,144,768]{2,1,0:T(8,128)(2,1)} %add_convert_fusion.11), channel_id=1, source_target_pairs={{0,2},{1,3},{2,0},{3,1},{4,6},{5,7},{6,4},{7,5},{8,10},{9,11},{10,... | collective-permute-start | bytes 1327112 | tf_op jit(solution)/shard_map/ppermute | solution.py:555
  509.6 22.9 %collective-permute-start.41 = (bf16[2,144,768]{2,1,0:T(8,128)(2,1)}, bf16[2,144,768]{2,1,0:T(8,128)(2,1)S(1)}, u32[]{:S(2)}, u32[]{:S(2)}) collective-permute-start(bf16[2,144,768]{2,1,0:T(8,128)(2,1)} %add_convert_fusion.10), channel_id=1, source_target_pairs={{0,2},{1,3},{2,0},{3,1},{4,6},{5,7},{6,4},{7,5},{8,10},{9,11},{10,... | collective-permute-start | bytes 1327112 | tf_op jit(solution)/shard_map/ppermute | solution.py:555
  509.6 20.8 %collective-permute-start.42 = (bf16[1,144,768]{2,1,0:T(8,128)(2,1)}, bf16[1,144,768]{2,1,0:T(8,128)(2,1)S(1)}, u32[]{:S(2)}, u32[]{:S(2)}) collective-permute-start(bf16[1,144,768]{2,1,0:T(8,128)(2,1)} %add_convert_fusion.20), channel_id=1, source_target_pairs={{0,4},{1,5},{2,6},{3,7},{4,0},{5,1},{6,2},{7,3},{8,12},{9,13},{10,... | collective-permute-start | bytes 663560 | tf_op jit(solution)/shard_map/ppermute | solution.py:555
  511.7 20.2 %collective-permute-start.43 = (bf16[1,144,1152]{2,1,0:T(8,128)(2,1)S(1)}, bf16[1,144,1152]{2,1,0:T(8,128)(2,1)S(1)}, u32[]{:S(2)}, u32[]{:S(2)}) collective-permute-start(bf16[1,144,1152]{2,1,0:T(8,128)(2,1)S(1)} %add_convert_fusion.12), channel_id=1, source_target_pairs={{0,8},{8,0},{16,24},{24,16},{1,9},{9,1},{17,25},{25,17},{2,10},{10... | collective-permute-start | bytes 995336 | tf_op jit(solution)/shard_map/ppermute | solution.py:555
  533.8 20.3 %collective-permute-start.44 = (bf16[1,144,768]{2,1,0:T(8,128)(2,1)S(1)}, bf16[1,144,768]{2,1,0:T(8,128)(2,1)S(1)}, u32[]{:S(2)}, u32[]{:S(2)}) collective-permute-start(bf16[1,144,768]{2,1,0:T(8,128)(2,1)S(1)} %add_convert_fusion.19), channel_id=1, source_target_pairs={{0,4},{1,5},{2,6},{3,7},{4,0},{5,1},{6,2},{7,3},{8,12},{9,13},{10,... | collective-permute-start | bytes 663560 | tf_op jit(solution)/shard_map/ppermute | solution.py:555
  536.7 18.9 %collective-permute-start.45 = (bf16[2,144,1152]{2,1,0:T(8,128)(2,1)S(1)}, bf16[2,144,1152]{2,1,0:T(8,128)(2,1)}, u32[]{:S(2)}, u32[]{:S(2)}) collective-permute-start(bf16[2,144,1152]{2,1,0:T(8,128)(2,1)S(1)} %pad_maximum_fusion.6), channel_id=1, source_target_pairs={{0,16},{8,24},{16,0},{24,8},{1,17},{9,25},{17,1},{25,9},{2,18},{10... | collective-permute-start | bytes 1990664 | tf_op jit(solution)/shard_map/ppermute | solution.py:555
  555.5 10.7 %collective-permute-start.46 = (bf16[2,144,768]{2,1,0:T(8,128)(2,1)S(1)}, bf16[2,144,768]{2,1,0:T(8,128)(2,1)S(1)}, u32[]{:S(2)}, u32[]{:S(2)}) collective-permute-start(bf16[2,144,768]{2,1,0:T(8,128)(2,1)S(1)} %pad_maximum_fusion.8), channel_id=1, source_target_pairs={{0,16},{8,24},{16,0},{24,8},{1,17},{9,25},{17,1},{25,9},{2,18},{10... | collective-permute-start | bytes 1327112 | tf_op jit(solution)/shard_map/ppermute | solution.py:555
  556.0 4.8 collective-permute-start.47
  568.6 4.2 collective-permute-start.50
  572.8 6.9 %collective-permute-start.51 = (bf16[16,3456]{1,0:T(8,128)(2,1)S(1)}, bf16[16,3456]{1,0:T(8,128)(2,1)S(1)}, u32[]{:S(2)}, u32[]{:S(2)}) collective-permute-start(bf16[16,3456]{1,0:T(8,128)(2,1)S(1)} %pad_maximum_fusion.11), channel_id=1, source_target_pairs={{0,4},{1,5},{2,6},{3,7},{4,0},{5,1},{6,2},{7,3},{8,12},{9,13},{10,... | collective-permute-start | bytes 331784 | tf_op jit(solution)/shard_map/ppermute | solution.py:555
  574.4 11.4 %collective-permute-start.48 = (bf16[3,144,768]{2,1,0:T(8,128)(2,1)S(1)}, bf16[3,144,768]{2,1,0:T(8,128)(2,1)}, u32[]{:S(2)}, u32[]{:S(2)}) collective-permute-start(bf16[3,144,768]{2,1,0:T(8,128)(2,1)S(1)} %pad_maximum_fusion.7), channel_id=1, source_target_pairs={{0,8},{8,0},{16,24},{24,16},{1,9},{9,1},{17,25},{25,17},{2,10},{10... | collective-permute-start | bytes 1990664 | tf_op jit(solution)/shard_map/ppermute | solution.py:555
  579.8 1.5 collective-permute-start.52
  585.4 12.4 %collective-permute-start.53 = (bf16[64,3456]{1,0:T(8,128)(2,1)}, bf16[64,3456]{1,0:T(8,128)(2,1)S(1)}, u32[]{:S(2)}, u32[]{:S(2)}) collective-permute-start(bf16[64,3456]{1,0:T(8,128)(2,1)} %copy.91), channel_id=1, source_target_pairs={{0,16},{8,24},{16,0},{24,8},{1,17},{9,25},{17,1},{25,9},{2,18},{10... | collective-permute-start | bytes 1327112 | tf_op jit(solution)/shard_map/ppermute | solution.py:555
  (38 other events, 285.9 us)
Sparse Core Ops, SparseCore 0:
  11.5 103.8 all-gather.10
  118.3 100.1 all-gather.12
  327.5 63.9 all-gather.6
  465.8 62.7 all-gather.8
